TPU v7x, 512 devices: a whole 4x4x16 slice. The times are simulated.
512 devices in a mesh: facet: 16 (over z), sub: 8 (over x, core), vis: 4 (over y).
Axes of the slice: x: 4, y: 4, z: 16, core: 2. Of those that a mesh axis runs over, the one named last changes fastest.
Arguments:
- sky: float32 [8192, 512], P(('facet', 'vis')), may hold values from -6 to 6
- row_offsets: int32 [8], P('sub'), may hold values from 0 to 7936
- block_counts: int32 [512], P(('facet', 'sub', 'vis')), may hold values from 1 to 16, as said below
- block_ids: int32 [8192], P(('facet', 'sub', 'vis')), may hold values from 0 to 127
- kernel_rows: float32 [8192, 8, 128], P(('facet', 'sub', 'vis')), may hold values from -2 to 2
- kernel_cols: float32 [8192, 128, 128], P(('facet', 'sub', 'vis')), may hold values from -0.5 to 0.5
- observed: float32 [8192, 2, 128], P(('facet', 'sub', 'vis')), may hold values from -6 to 6
- weights: int32 [8192, 128], P(('facet', 'sub', 'vis')), may hold values from 1 to 4
Outputs:
- residual_image: float32 [8192, 512], P(('facet', 'vis'))
- residual_vis: float32 [8192, 2, 128], P(('facet', 'sub', 'vis'))
Inputs may be any that keep to these rules, and one draw needn't show every extreme that they name: `block_counts`: every device has at most 16 live slots, the first ones; some device has exactly 16.
All inputs are finite; a program needn't handle non-finite values.
Results may differ from a plain program's by a relative error of at most 0.0003.
Values sent between devices are 32-bit elements; how exact they have to be, the bound alone decides.
No kernel may reach another device: no remote copies, remote signals or barrier semaphores. Data moves between devices by JAX's collectives and lax.ppermute only.
A program may use at most 64 MiB of HBM per device.

v0:
```python
import jax
import jax.numpy as jnp
from jax import lax
from jax.sharding import PartitionSpec as P

K = 512
CR = 256
BR = 8
BC = 128


def cut_along(x, dim, devices):
    dims = x.shape
    parts = x.reshape(*dims[:dim], devices, dims[dim] // devices, *dims[dim + 1 :])
    return jnp.moveaxis(parts, dim, 0)


def summed_on_arrival(x, axis, dim):
    devices = lax.axis_size(axis)
    parts = lax.all_to_all(cut_along(x, dim, devices), axis, 0, 0, tiled=True)
    return jnp.sum(parts, axis=0)


def gathered_by_axis(x, axes, dim):
    if not axes:
        return x
    nearer = lax.all_gather(x, axes[-1], axis=dim, tiled=True)
    return gathered_by_axis(nearer, axes[:-1], dim)


def copy_for_each(x, axis):
    devices = lax.axis_size(axis)
    return lax.all_to_all(jnp.broadcast_to(x[None], (devices, *x.shape)), axis, 0, 0, tiled=True)


def over_copies(x, axis):
    return copy_for_each(x, axis).sum(axis=0)


def highest_dot(left, right):
    return jnp.dot(left, right, precision=lax.Precision.HIGHEST, preferred_element_type=jnp.float32)


def column_tables():
    index_k = jnp.arange(K, dtype=jnp.int32)
    product = index_k[:, None] * index_k[None, :] % K
    angle = product.astype(jnp.float32) * (2.0 * jnp.pi / K)
    scale = K ** (-0.5)
    return (jnp.cos(angle) * scale, jnp.sin(angle) * scale)


def row_tables(starts, pixels, total):
    product = starts[:, None] * pixels[None, :] % total
    angle = product.astype(jnp.float32) * (2.0 * jnp.pi / total)
    scale = total ** (-0.5)
    return (jnp.cos(angle) * scale, jnp.sin(angle) * scale)


def column_forward(real_part, imag_part, cos_cols, sin_cols):
    grid_real = highest_dot(real_part, cos_cols) + highest_dot(imag_part, sin_cols)
    grid_imag = highest_dot(imag_part, cos_cols) - highest_dot(real_part, sin_cols)
    return jnp.stack([grid_real, grid_imag], axis=1)


def column_adjoint(subgrid, cos_cols, sin_cols):
    grid_real = subgrid[:, 0]
    grid_imag = subgrid[:, 1]
    back_real = highest_dot(grid_real, cos_cols) - highest_dot(grid_imag, sin_cols)
    back_imag = highest_dot(grid_imag, cos_cols) + highest_dot(grid_real, sin_cols)
    return jnp.stack([back_real, back_imag], axis=1)


def degrid_grid(subgrid, live_count, block_index, kernel_rows, kernel_cols, observed, weights):
    band_rows = CR // BR
    band_cols = K // BC
    nblocks = band_rows * band_cols
    block_table = (
        subgrid.reshape(band_rows, BR, 2, band_cols, BC)
        .transpose(0, 3, 1, 2, 4)
        .reshape(nblocks, BR, 2, BC)
    )
    onehot = (block_index[:, None] == jnp.arange(nblocks, dtype=jnp.int32)[None, :]).astype(
        jnp.float32
    )
    hp = lax.Precision.HIGHEST
    chosen = jnp.einsum("bn,nrzc->brzc", onehot, block_table, precision=hp)
    along = jnp.einsum("brzc,bct->brzt", chosen, kernel_cols, precision=hp)
    model = jnp.sum(along * kernel_rows[:, :, None, :], axis=1)
    live = (jnp.arange(observed.shape[0], dtype=jnp.int32) < live_count)[:, None, None]
    residual = jnp.where(
        live, weights[:, None, :].astype(jnp.float32) * (observed - model), jnp.zeros_like(model)
    )
    spread = kernel_rows[:, :, None, :] * residual[:, None, :, :]
    back = jnp.einsum("brzt,bct->brzc", spread, kernel_cols, precision=hp)
    table_back = jnp.einsum("bn,brzc->nrzc", onehot, back, precision=hp)
    partial_value = (
        table_back.reshape(band_rows, band_cols, BR, 2, BC)
        .transpose(0, 2, 3, 1, 4)
        .reshape(CR, 2, K)
    )
    return (residual, partial_value)


def shards(sky, row_offsets, block_counts, block_ids, kernel_rows, kernel_cols, observed, weights):
    facets = lax.axis_size("facet")
    vises = lax.axis_size("vis")
    total = facets * K
    local_rows = sky.shape[0]
    first_pixel = (lax.axis_index("facet") * vises + lax.axis_index("vis")) * local_rows
    pixels = first_pixel + jnp.arange(local_rows, dtype=jnp.int32)
    cos_cols, sin_cols = column_tables()
    offset = row_offsets[0]

    def grid_rows(row_total):
        return offset + jnp.arange(row_total, dtype=jnp.int32)

    share_rows = CR // (facets * vises)
    cos_rows, sin_rows = row_tables(
        grid_rows(share_rows * lax.axis_size(("facet", "vis"))), pixels, total
    )
    real_part = highest_dot(cos_rows, sky)
    imag_part = -highest_dot(sin_rows, sky)
    mine = summed_on_arrival(jnp.stack([real_part, imag_part], axis=1), ("facet", "vis"), 0)
    row_part = column_forward(mine[:, 0], mine[:, 1], cos_cols, sin_cols)
    subgrid = gathered_by_axis(row_part, ("facet", "vis"), 0)
    residual, partial_value = degrid_grid(
        subgrid, block_counts[0], block_ids, kernel_rows, kernel_cols, observed, weights
    )
    shared = summed_on_arrival(partial_value, ("facet", "vis"), 0)
    adjoint = column_adjoint(shared, cos_cols, sin_cols)
    portion = gathered_by_axis(adjoint, ("facet", "vis"), 0)
    cos_rows, sin_rows = row_tables(grid_rows(portion.shape[0]), pixels, total)
    image = highest_dot(cos_rows.T, portion[:, 0]) - highest_dot(sin_rows.T, portion[:, 1])
    image = over_copies(image, "sub")
    return (image, residual)


def solution(mesh):
    return jax.shard_map(
        shards,
        mesh=mesh,
        in_specs=(
            P(("facet", "vis"), None),
            P("sub"),
            P(("facet", "sub", "vis")),
            P(("facet", "sub", "vis")),
            P(("facet", "sub", "vis"), None, None),
            P(("facet", "sub", "vis"), None, None),
            P(("facet", "sub", "vis"), None, None),
            P(("facet", "sub", "vis"), None),
        ),
        out_specs=(P(("facet", "vis"), None), P(("facet", "sub", "vis"), None, None)),
        check_vma=False,
    )
```

profile of v0, /device:TPU:1, one launch (start us, length us, event | category | flops | bytes accessed | tf_op | source)
XLA Modules:
  0.0 380.9 jit_solution(1868882590822935514)
XLA Ops:
  7.2 0.0 copy-start
  7.2 0.0 all-gather.3.cloned.1.call-start
  8.0 2.1 convolution_negate_fusion
  10.1 2.1 fusion.46
  12.1 0.1 stack.28
  12.3 0.1 stack.27
  12.4 0.2 pad_maximum_fusion
  12.7 70.6 %all_to_all.15 = f32[64,4,2,512]{3,1,2,0:T(4,128)S(1)} all-to-all(f32[64,4,2,512]{3,1,2,0:T(4,128)S(1)} %pad_maximum_fusion), channel_id=1, replica_groups=mesh['facet'=16,'sub'=8,'vis'=4] {'facet','vis'}, dimensions={0} | all-to-all | bytes 2097152 | tf_op jit(solution)/shard_map/all_to_all | solution.py:20
  83.2 0.2 reduce_sum.36
  83.4 4.5 %fusion.16 = f32[4,512]{1,0:T(4,128)S(1)} fusion(f32[4,2,512]{2,0,1:T(4,128)S(1)} %reduce_sum.36), kind=kOutput, calls=%fused_computation.30 | convolution fusion | flops 16515072 | bytes 16384 | tf_op jit(solution)/shard_map/dot_general | solution.py:41
  87.9 4.5 %fusion.17 = f32[4,512]{1,0:T(4,128)S(1)} fusion(f32[4,2,512]{2,0,1:T(4,128)S(1)} %reduce_sum.36), kind=kOutput, calls=%fused_computation.31 | convolution fusion | flops 16515072 | bytes 16384 | tf_op jit(solution)/shard_map/dot_general | solution.py:41
  92.5 4.6 %fusion.3 = f32[4,1,512]{2,0,1:T(4,128)S(1)} fusion(f32[4,512]{1,0:T(4,128)S(1)} %fusion.16, f32[4,2,512]{2,0,1:T(4,128)S(1)} %reduce_sum.36), kind=kOutput, calls=%fused_computation.12 | convolution fusion | flops 16517120 | bytes 24576 | tf_op jit(solution)/shard_map/dot_general | solution.py:41
  97.0 0.0 copy-start.4
  97.0 4.6 %fusion.4 = f32[4,1,512]{2,0,1:T(4,128)S(1)} fusion(f32[4,512]{1,0:T(4,128)S(1)} %fusion.17, f32[4,2,512]{2,0,1:T(4,128)S(1)} %reduce_sum.36), kind=kOutput, calls=%fused_computation.14 | convolution fusion | flops 16517120 | bytes 24576 | tf_op jit(solution)/shard_map/dot_general | solution.py:41
  101.6 0.1 pad_maximum_fusion.1
  101.7 12.5 %all_gather.12 = f32[16,2,512]{2,1,0:T(2,128)} all-gather(f32[4,2,512]{2,1,0:T(2,128)S(1)} %copy.32), channel_id=1, replica_groups=mesh['facet'=16,'sub'=8,'vis'=4] {'vis'}, dimensions={0}, use_global_device_ids=true | all-gather | bytes 81920 | tf_op jit(solution)/shard_map/all_gather | solution.py:27
  114.1 0.0 all-gather.3.cloned.1.call-update
  114.2 0.3 all-gather.5.cloned.1.call-start
  115.1 0.0 copy-done.4
  115.1 0.0 copy-start.5
  115.1 54.8 %all-gather.3.cloned.1.call-done = f32[256,2,512]{2,1,0:T(2,128)} async-done(((f32[16,2,512]{2,1,0:T(2,128)}), f32[256,2,512]{2,1,0:T(2,128)}) %all-gather.3.cloned.1.call-update) | async-done | bytes 1048592 | tf_op jit(solution)/shard_map/all_gather | solution.py:27
  170.0 2.2 reshape.36
  172.2 0.0 copy-start.1
  172.2 0.0 copy-start.3
  172.2 0.3 copy.33
  172.5 0.0 copy-done.5
  172.5 0.5 fusion.63
  173.0 0.0 copy-done
  173.0 0.1 copy-done.1
  173.1 1.1 fusion
  174.1 0.0 copy-done.3
  174.2 0.1 multiply_select_fusion.1
  174.2 0.0 copy-start.2
  174.3 1.7 fusion.8
  176.0 0.7 fusion.42
  176.7 0.3 copy.76
  177.0 0.0 copy-done.2
  177.0 0.8 reshape_reshape.3
  177.8 54.5 %all_to_all.16 = f32[64,4,2,512]{3,2,1,0:T(2,128)S(1)} all-to-all(f32[64,4,2,512]{3,2,1,0:T(2,128)S(1)} %reshape_reshape.3), channel_id=1, replica_groups=mesh['facet'=16,'sub'=8,'vis'=4] {'facet','vis'}, dimensions={0} | all-to-all | bytes 2097152 | tf_op jit(solution)/shard_map/all_to_all | solution.py:20
  232.3 0.4 reduce_sum.38
  232.6 4.5 %fusion.15 = f32[4,512]{1,0:T(4,128)S(1)} fusion(f32[4,1,512]{2,1,0:T(1,128)S(1)} %get-tuple-element.4), kind=kOutput, calls=%fused_computation.29 | convolution fusion | flops 16515072 | bytes 16384 | tf_op jit(solution)/shard_map/dot_general | solution.py:41
  237.1 4.5 %fusion.14 = f32[4,512]{1,0:T(4,128)S(1)} fusion(f32[4,1,512]{2,1,0:T(1,128)S(1)} %get-tuple-element.5), kind=kOutput, calls=%fused_computation.28 | convolution fusion | flops 16515072 | bytes 16384 | tf_op jit(solution)/shard_map/dot_general | solution.py:41
  241.7 4.6 %fusion.2 = f32[4,1,512]{2,0,1:T(4,128)S(1)} fusion(f32[4,512]{1,0:T(4,128)S(1)} %fusion.15, f32[4,1,512]{2,1,0:T(1,128)S(1)} %get-tuple-element.5), kind=kOutput, calls=%fused_computation.10 | convolution fusion | flops 16517120 | bytes 24576 | tf_op jit(solution)/shard_map/dot_general | solution.py:41
  246.2 4.6 %fusion.1 = f32[4,1,512]{2,0,1:T(4,128)S(1)} fusion(f32[4,512]{1,0:T(4,128)S(1)} %fusion.14, f32[4,1,512]{2,1,0:T(1,128)S(1)} %get-tuple-element.4), kind=kOutput, calls=%fused_computation.8 | convolution fusion | flops 16517120 | bytes 24576 | tf_op jit(solution)/shard_map/dot_general | solution.py:41
  250.8 0.1 pad_maximum_fusion.2
  250.9 10.2 %all_gather.14 = f32[16,2,512]{2,1,0:T(2,128)} all-gather(f32[4,2,512]{2,1,0:T(2,128)S(1)} %copy.37), channel_id=1, replica_groups=mesh['facet'=16,'sub'=8,'vis'=4] {'vis'}, dimensions={0}, use_global_device_ids=true | all-gather | bytes 81920 | tf_op jit(solution)/shard_map/all_gather | solution.py:27
  261.1 0.0 all-gather.5.cloned.1.call-update
  261.1 66.0 %all-gather.5.cloned.1.call-done = f32[256,2,512]{2,1,0:T(2,128)} async-done(((f32[16,2,512]{2,1,0:T(2,128)}), f32[256,2,512]{2,1,0:T(2,128)}) %all-gather.5.cloned.1.call-update) | async-done | bytes 1048592 | tf_op jit(solution)/shard_map/all_gather | solution.py:27
  327.1 2.5 fusion.131
  329.6 1.0 fusion.20
  330.6 1.0 convolution_subtract_fusion
  331.7 0.3 broadcast_in_dim.11
  331.9 41.2 %all_to_all.17 = f32[8,128,512]{2,1,0:T(8,128)S(1)} all-to-all(f32[8,128,512]{2,1,0:T(8,128)S(1)} %broadcast_in_dim.11), channel_id=1, replica_groups=mesh['facet'=16,'sub'=8,'vis'=4] {'sub'}, dimensions={0} | all-to-all | bytes 4194304 | tf_op jit(solution)/shard_map/all_to_all | solution.py:33
  373.2 0.9 reduce_sum.39
  (7 shorter events, 0.1 us)
Async XLA Ops:
  7.2 165.8 %copy-start = (f32[16,128,128]{2,1,0:T(8,128)S(1)}, f32[16,128,128]{2,1,0:T(8,128)}, u32[]{:S(2)}) copy-start(f32[16,128,128]{2,1,0:T(8,128)} %param.13) | copy-start | bytes 3145732
  7.2 162.8 %all-gather.3.cloned.1.call-start = ((), (), s32[]{:S(2)}) async-start(), calls=%async_computation.3 | async-start | bytes 1114112 | tf_op jit(solution)/shard_map/all_gather | solution.py:27
  97.0 18.1 %copy-start.4 = (s32[16,128]{1,0:T(8,128)S(1)}, s32[16,128]{1,0:T(8,128)}, u32[]{:S(2)}) copy-start(s32[16,128]{1,0:T(8,128)} %param.15) | copy-start | bytes 24580
  114.2 213.0 %all-gather.5.cloned.1.call-start = ((), (), s32[]{:S(2)}) async-start(), calls=%async_computation.4 | async-start | bytes 1114112 | tf_op jit(solution)/shard_map/all_gather | solution.py:27
  115.1 57.4 %copy-start.5 = (s32[16]{0:T(128)S(1)}, s32[16]{0:T(128)}, u32[]{:S(2)}) copy-start(s32[16]{0:T(128)} %param.11) | copy-start | bytes 196
  172.2 0.8 copy-start.1
  172.2 1.9 copy-start.3
  174.2 2.7 copy-start.2
Sparse Core Ops, SparseCore 0:
  114.3 55.6 all-gather.2
  261.3 65.8 all-gather.4
where the time goes:
time: 381 us
  blocking collectives  189 us (50%)
  waiting for transfers between devices  121 us (32%)
  matrix products  46.4 us (12%)
  between operations  15.7 us (4%)
  local copies, waits for them, and re-layouts  6.73 us (2%)
    all_to_all x2, blocking collectives, summed_on_arrival(): parts = lax.all_to_all(cut_along(x, dim, devices), axis, 0, 0, tiled=True)  125 us
    all_gather x2, waiting for transfers between devices, gathered_by_axis(): nearer = lax.all_gather(x, axes[-1], axis=dim, tiled=True)  121 us
    dot_general x12, matrix products, highest_dot(): jnp.dot(left, right, precision=lax.Precision.HIGHEST, preferred_element_t...  42.5 us
    all_to_all x1, blocking collectives, copy_for_each(): lax.all_to_all(jnp.broadcast_to(x[None], (devices, *x.shape)), axis, 0, 0...  41.2 us
    all_gather x2, blocking collectives, gathered_by_axis(): nearer = lax.all_gather(x, axes[-1], axis=dim, tiled=True)  22.7 us
  transfers between devices with their start and end apart: 2, of which 2 were waited for; matrix products, arithmetic and copies ran while one was open for 0% of the time, Pallas kernels for 0%

commit v1 on v0

v1 whole, which is shorter than its diff:
```python
import jax
import jax.numpy as jnp
import numpy as np
from jax import lax
from jax.sharding import PartitionSpec as P

K = 512
CR = 256
BR = 8
BC = 128
SUBS = 8
RANK = 32
RANKS = 16
HIGH = lax.Precision.HIGH


def prolate(count, band, total, rank):
    j = np.arange(count, dtype=np.float64)
    diag = -np.cos(np.pi * (2 * j - count + 1) / total) * np.cos(np.pi * band / total)
    m = np.arange(1, count, dtype=np.float64)
    off = np.sin(np.pi * m / total) * np.sin(np.pi * (count - m) / total)
    values, vectors = np.linalg.eigh(np.diag(diag) + np.diag(off, 1) + np.diag(off, -1))
    basis = vectors[:, ::-1][:, :rank]
    signs = np.sign(np.sum(basis[count // 2 :], axis=0))
    return basis * signs


def constants(facets, vises, total):
    rows = K // vises
    lanes = K // vises
    bands = K // BC
    sub_lanes = BC // vises
    basis = prolate(K, CR, total, RANK)
    section = prolate(rows, CR, total, RANKS)
    merge = np.stack([section.T @ basis[v * rows : (v + 1) * rows] for v in range(vises)])
    r = np.arange(CR) - (CR - 1) / 2
    p = np.arange(K) - (K - 1) / 2
    kernel = np.exp(-2j * np.pi * np.outer(r, p) / total) @ basis
    centres = np.arange(facets) * K + (K - 1) / 2
    shift = np.exp(-2j * np.pi * np.outer(r, centres) / total)
    expand = shift[:, :, None] * kernel[:, None, :] * total**-0.5
    real, imag = expand.real, expand.imag
    spread = np.stack(
        [np.stack([real, -imag], axis=2), np.stack([imag, real], axis=2)], axis=0
    )
    spread = spread.reshape(2, CR // BR, BR, facets * 2 * RANK).transpose(1, 0, 2, 3)
    spread = spread.reshape(2 * CR, facets * 2 * RANK)
    merges = np.zeros((2, RANK, vises, 2, RANKS))
    for part in range(2):
        merges[part, :, :, part, :] = merge.transpose(2, 0, 1)
    merges = merges.reshape(2 * RANK, vises * 2 * RANKS)
    column = np.arange(K).reshape(bands, vises, sub_lanes).transpose(1, 0, 2).reshape(vises, lanes)
    angle = 2 * np.pi * ((np.arange(K)[None, :, None] * column[:, None, :]) % K) / K
    table = np.concatenate([np.cos(angle), np.sin(angle)], axis=2) * K**-0.5
    return tuple(np.asarray(x, np.float32) for x in (section.T, merges, spread, table))


def dot(spec, left, right):
    return jnp.einsum(spec, left, right, precision=HIGH, preferred_element_type=jnp.float32)


def shards(sky, row_offsets, block_counts, block_ids, kernel_rows, kernel_cols, observed, weights):
    facets = lax.axis_size("facet")
    vises = lax.axis_size("vis")
    subs = lax.axis_size("sub")
    total = facets * K
    rows = sky.shape[0]
    lanes = K // vises
    slots = block_ids.shape[0]
    bands = K // BC
    row_bands = CR // BR
    groups = slots // vises
    sub_lanes = BC // vises
    section, merges, spread, table = constants(facets, vises, total)

    first = (lax.axis_index("facet") * vises + lax.axis_index("vis")) * rows
    pixels = first + jnp.arange(rows, dtype=jnp.int32)

    def phases(offsets):
        product = ((2 * offsets + (CR - 1)) * pixels) % (2 * total)
        angle = product.astype(jnp.float32) * (2.0 * jnp.pi / (2 * total))
        return jnp.cos(angle), jnp.sin(angle)

    cos_p, sin_p = phases(row_offsets[0])
    into = jnp.concatenate([section * cos_p, -section * sin_p], axis=0)
    coef = dot("mp,pk->mk", into, sky)
    both = dot("mk,vkc->vmc", coef, table)
    real = both[:, :RANKS, :lanes] + both[:, RANKS:, lanes:]
    imag = both[:, RANKS:, :lanes] - both[:, :RANKS, lanes:]
    ids_rows = jnp.broadcast_to(
        block_ids.astype(jnp.float32)[None, :, None], (vises, slots, lanes)
    )
    sent = jnp.concatenate([real, imag, ids_rows], axis=1)
    got = lax.all_to_all(sent, "vis", 0, 0, tiled=True)
    ids = got[:, 2 * RANKS :, 0].astype(jnp.int32).reshape(vises * slots)
    facet_coef = dot("kx,xl->kl", merges, got[:, : 2 * RANKS].reshape(vises * 2 * RANKS, lanes))
    sent = jnp.broadcast_to(facet_coef[None], (facets, 2 * RANK, lanes))
    got = lax.all_to_all(sent, "facet", 0, 0, tiled=True)

    grid = dot("gx,xl->gl", spread, got.reshape(facets * 2 * RANK, lanes))
    onehot = (ids[:, None] == jnp.arange(row_bands * bands, dtype=jnp.int32)[None, :]).astype(
        jnp.float32
    )
    blocks = (
        grid.reshape(row_bands, 2 * BR, bands, sub_lanes)
        .transpose(0, 2, 1, 3)
        .reshape(row_bands * bands, 2 * BR * sub_lanes)
    )
    picked = dot("sn,nx->sx", onehot, blocks)
    sent = (
        picked.reshape(vises, groups, vises, 2 * BR, sub_lanes)
        .transpose(0, 1, 3, 2, 4)
        .reshape(vises, groups * 2 * BR, lanes)
    )
    got = lax.all_to_all(sent, "vis", 0, 0, tiled=True)
    chosen = (
        got.reshape(vises, groups, 2 * BR, vises, sub_lanes)
        .transpose(1, 3, 2, 0, 4)
        .reshape(slots, 2, BR, BC)
    )

    along = dot("szrc,sct->szrt", chosen, kernel_cols)
    model = jnp.sum(along * kernel_rows[:, None, :, :], axis=2)
    live = (jnp.arange(slots, dtype=jnp.int32) < block_counts[0])[:, None, None]
    residual = jnp.where(
        live, weights[:, None, :].astype(jnp.float32) * (observed - model), jnp.zeros_like(model)
    )
    back = dot(
        "szrt,sct->szrc", kernel_rows[:, None, :, :] * residual[:, :, None, :], kernel_cols
    )

    sent = (
        back.reshape(groups, vises, 2 * BR, vises, sub_lanes)
        .transpose(3, 0, 2, 1, 4)
        .reshape(vises, groups * 2 * BR, lanes)
    )
    got = lax.all_to_all(sent, "vis", 0, 0, tiled=True)
    parts = (
        got.reshape(vises, groups, 2 * BR, vises, sub_lanes)
        .transpose(0, 1, 3, 2, 4)
        .reshape(vises * slots, 2 * BR * sub_lanes)
    )
    summed = dot("sn,sx->nx", onehot, parts)
    residual_grid = (
        summed.reshape(row_bands, bands, 2 * BR, sub_lanes)
        .transpose(0, 2, 1, 3)
        .reshape(2 * CR, lanes)
    )
    sent = dot("gx,gl->xl", spread, residual_grid).reshape(facets, 2 * RANK, lanes)
    got = lax.all_to_all(sent, "facet", 0, 0, tiled=True)
    facet_coef = jnp.sum(got, axis=0)

    coef = dot("kx,kl->xl", merges, facet_coef).reshape(1, vises, 2 * RANKS, lanes)
    offset_rows = jnp.broadcast_to(
        row_offsets[0].astype(jnp.float32), (subs, vises, 8, lanes)
    )
    sent = jnp.concatenate(
        [jnp.broadcast_to(coef, (subs, vises, 2 * RANKS, lanes)), offset_rows], axis=2
    ).reshape(subs * vises, 2 * RANKS + 8, lanes)
    got = lax.all_to_all(sent, ("sub", "vis"), 0, 0, tiled=True)
    got = got.reshape(subs, vises, 2 * RANKS + 8, lanes)
    offsets = got[:, 0, 2 * RANKS, 0].astype(jnp.int32)
    cos_q, sin_q = phases(offsets[:, None])
    cos_q = section[None] * cos_q[:, None, :]
    sin_q = section[None] * sin_q[:, None, :]
    out = jnp.stack(
        [
            jnp.concatenate([cos_q, -sin_q], axis=1),
            jnp.concatenate([sin_q, cos_q], axis=1),
        ],
        axis=0,
    )
    pixels_cols = dot("zqap,qval->zpvl", out, got[:, :, : 2 * RANKS])
    image = dot("pvl,vkl->pk", pixels_cols[0], table[:, :, :lanes]) - dot(
        "pvl,vkl->pk", pixels_cols[1], table[:, :, lanes:]
    )
    return (image, residual)


def solution(mesh):
    return jax.shard_map(
        shards,
        mesh=mesh,
        in_specs=(
            P(("facet", "vis"), None),
            P("sub"),
            P(("facet", "sub", "vis")),
            P(("facet", "sub", "vis")),
            P(("facet", "sub", "vis"), None, None),
            P(("facet", "sub", "vis"), None, None),
            P(("facet", "sub", "vis"), None, None),
            P(("facet", "sub", "vis"), None),
        ),
        out_specs=(P(("facet", "vis"), None), P(("facet", "sub", "vis"), None, None)),
        check_vma=False,
    )
```

time: 381 us -> 172 us (0.45)
  blocking collectives: 189 us -> 9.44 us
  waiting for transfers between devices: 121 us -> 64.3 us
  starting transfers between devices: 0.3 us -> 46.3 us
  matrix products: 46.4 us -> 15.7 us
  local copies, waits for them, and re-layouts: 6.73 us -> 29.2 us
  between operations: 15.7 us -> 2.41 us
    all_to_all x3 -> x1, blocking collectives: 166 us -> 9.44 us  [shards(): got = lax.all_to_all(sent, 'vis', 0, 0, tiled=True)]
    all_gather x2 -> x0, waiting for transfers between devices: 121 us -> none  [gathered_by_axis(): nearer = lax.all_gather(x, axes[-1], axis=dim, tiled=True)]
    all_to_all x0 -> x5, waiting for transfers between devices: none -> 64.3 us  [the longest x2 43.8 us: shards(): got = lax.all_to_all(sent, 'facet', 0, 0, tiled=True)]
    all_to_all x0 -> x5, starting transfers between devices: none -> 46.3 us  [the longest x2 27.7 us: shards(): got = lax.all_to_all(sent, 'facet', 0, 0, tiled=True)]
    dot_general x16 -> x13, matrix products: 46.4 us -> 15.7 us  [dot(): jnp.einsum(spec, left, right, precision=HIGH, preferred_element_type=jnp....]
    all_gather x2 -> x0, blocking collectives: 22.7 us -> none  [gathered_by_axis(): nearer = lax.all_gather(x, axes[-1], axis=dim, tiled=True)]
    reshape x3 -> x13, local copies, waits for them, and re-layouts: 2.79 us -> 21.7 us  [the longest x3 4.32 us: shards(): got.reshape(vises, groups, 2 * BR, vises, sub_lanes)]
  transfers between devices with their start and end apart: 2 -> 5, of which waited for: 2 -> 5; matrix products, arithmetic and copies ran while one was open for 0% -> 1% of each run, Pallas kernels for 0% -> 0%
where the time goes in v1:
time: 172 us; the launch traced here: 170 us
  waiting for transfers between devices  64.3 us (37%)
  starting transfers between devices  46.3 us (27%)
  local copies, waits for them, and re-layouts  29.2 us (17%)
  matrix products  15.7 us (9%)
  blocking collectives  9.44 us (5%)
  other arithmetic  2.8 us (2%)
  between operations  2.41 us (1%)
    all_to_all x2, waiting for transfers between devices, shards(): got = lax.all_to_all(sent, 'facet', 0, 0, tiled=True)  43.8 us
    all_to_all x2, starting transfers between devices, shards(): got = lax.all_to_all(sent, 'facet', 0, 0, tiled=True)  27.7 us
    dot_general x13, matrix products, dot(): jnp.einsum(spec, left, right, precision=HIGH, preferred_element_type=jnp....  15.7 us
    all_to_all x1, waiting for transfers between devices, shards(): got = lax.all_to_all(sent, ('sub', 'vis'), 0, 0, tiled=True)  12.2 us
    all_to_all x1, starting transfers between devices, shards(): got = lax.all_to_all(sent, ('sub', 'vis'), 0, 0, tiled=True)  11.8 us
    all_to_all x1, blocking collectives, shards(): got = lax.all_to_all(sent, 'vis', 0, 0, tiled=True)  9.44 us
    all_to_all x2, waiting for transfers between devices, shards(): got = lax.all_to_all(sent, 'vis', 0, 0, tiled=True)  8.33 us
    all_to_all x2, starting transfers between devices, shards(): got = lax.all_to_all(sent, 'vis', 0, 0, tiled=True)  6.78 us
  transfers between devices with their start and end apart: 5, of which 5 were waited for; matrix products, arithmetic and copies ran while one was open for 1% of the time, Pallas kernels for 0%

profile of v1, /device:TPU:1, one launch (start us, length us, event | category | flops | bytes accessed | tf_op | source)
XLA Modules:
  0.0 170.2 jit_solution(2108652105104335483)
XLA Ops:
  0.6 0.0 copy-start
  0.6 0.0 copy-start.4
  1.4 0.1 fusion.35
  1.5 0.7 broadcast_multiply_fusion.2
  2.2 0.7 broadcast_multiply_fusion.3
  2.9 1.1 convolution_bitcast_fusion.6
  4.0 0.0 copy-start.1
  4.0 2.4 %convolution_bitcast_fusion.5 = f32[4,32,256]{2,1,0:T(8,128)S(1)} fusion(f32[32,512,1]{1,0,2:T(8,128)S(1)} %convolution_bitcast_fusion.6, f32[4,512,256]{2,1,0:T(8,128)} %constant.72.clone), kind=kOutput, calls=%fused_computation.7 | convolution fusion | flops 100663296 | bytes 2293760 | tf_op jit(solution)/shard_map/mk,vkc->vmc/dot_general | solution.py:59
  6.5 0.1 pad.9.clone
  6.6 0.1 maximum_maximum_fusion
  6.7 9.4 %all_to_all.30 = f32[4,48,128]{2,1,0:T(8,128)S(1)} all-to-all(f32[4,48,128]{2,1,0:T(8,128)S(1)} %maximum_maximum_fusion), channel_id=1, replica_groups=mesh['facet'=16,'sub'=8,'vis'=4] {'vis'}, dimensions={0} | all-to-all | bytes 196608 | tf_op jit(solution)/shard_map/all_to_all | solution.py:94
  16.1 0.2 fusion.37
  16.3 0.9 broadcast_in_dim.17
  17.2 15.0 %all-to-all-start.1 = ((f32[16,64,128]{2,1,0:T(8,128)}), f32[16,64,128]{2,1,0:T(8,128)}, u32[]{:S(2)}, u32[]{:S(2)}) async-start(f32[16,64,128]{2,1,0:T(8,128)} %broadcast_in_dim.17), calls=%async_computation.1 | async-start | bytes 1048576 | tf_op jit(solution)/shard_map/all_to_all | solution.py:98
  32.8 0.1 fusion.12
  32.9 0.1 convert_element_type.61
  33.0 21.3 %all-to-all-done.1 = f32[16,64,128]{2,1,0:T(8,128)} async-done(((f32[16,64,128]{2,1,0:T(8,128)}), f32[16,64,128]{2,1,0:T(8,128)}, u32[]{:S(2)}, u32[]{:S(2)}) %all-to-all-start.1) | async-done | bytes 524320 | tf_op jit(solution)/shard_map/all_to_all | solution.py:98
  54.3 2.0 %fusion.38 = f32[512,128]{1,0:T(8,128)S(1)} fusion(f32[512,1024]{1,0:T(8,128)S(1)} %copy-done.1, f32[1024,128]{1,0:T(8,128)} %bitcast.10), kind=kOutput, calls=%fused_computation.76 | convolution fusion | flops 402653184 | bytes 2883584 | tf_op jit(solution)/shard_map/gx,xl->gl/dot_general | solution.py:59
  56.4 1.4 reshape.218
  57.8 2.3 %copy.50 = f32[32,16,4,32]{3,1,2,0:T(8,128)} copy(f32[32,16,4,32]{3,2,1,0:T(4,128)} %reshape.218) | data formatting | bytes 524288 | tf_op jit(solution)/shard_map/reshape | solution.py:105
  60.1 2.3 %reshape.219 = f32[128,512]{1,0:T(8,128)} reshape(f32[32,4,16,32]{3,2,1,0:T(8,128)} %bitcast.105) | data formatting | bytes 524288 | tf_op jit(solution)/shard_map/reshape | solution.py:107
  62.4 1.1 copy.31
  63.5 0.0 copy-start.3
  63.5 1.4 convolution_bitcast_fusion.2
  64.9 1.9 %reshape.220 = f32[4,64,128]{2,1,0:T(8,128)} reshape(f32[4,4,16,4,32]{4,3,2,1,0:T(4,128)} %convolution_bitcast_fusion.2) | data formatting | bytes 262144 | tf_op jit(solution)/shard_map/reshape | solution.py:113
  66.8 3.5 %all-to-all-start.2 = ((f32[4,64,128]{2,1,0:T(8,128)}), f32[4,64,128]{2,1,0:T(8,128)S(1)}, u32[]{:S(2)}, u32[]{:S(2)}) async-start(f32[4,64,128]{2,1,0:T(8,128)} %reshape.220), calls=%async_computation.2 | async-start | bytes 262144 | tf_op jit(solution)/shard_map/all_to_all | solution.py:115
  70.3 4.8 %all-to-all-done.2 = f32[4,64,128]{2,1,0:T(8,128)S(1)} async-done(((f32[4,64,128]{2,1,0:T(8,128)}), f32[4,64,128]{2,1,0:T(8,128)S(1)}, u32[]{:S(2)}, u32[]{:S(2)}) %all-to-all-start.2) | async-done | bytes 131104 | tf_op jit(solution)/shard_map/all_to_all | solution.py:115
  75.1 1.1 reshape.221
  76.2 2.2 %copy.52 = f32[4,4,16,4,32]{4,0,2,3,1:T(4,128)} copy(f32[4,4,16,4,32]{4,3,2,1,0:T(4,128)} %reshape.221) | data formatting | bytes 262144 | tf_op jit(solution)/shard_map/reshape | solution.py:117
  78.3 1.3 reshape.222
  79.7 0.5 fusion.1
  80.2 0.1 multiply_select_fusion
  80.3 0.0 copy-start.6
  80.3 0.9 fusion.2
  81.2 1.1 reshape.223
  82.3 2.2 %copy.51 = f32[4,4,16,4,32]{4,1,2,0,3:T(4,128)} copy(f32[4,4,16,4,32]{4,3,2,1,0:T(4,128)} %reshape.223) | data formatting | bytes 262144 | tf_op jit(solution)/shard_map/reshape | solution.py:133
  84.5 1.9 %reshape.224 = f32[4,64,128]{2,1,0:T(8,128)} reshape(f32[4,4,16,4,32]{4,3,2,1,0:T(4,128)} %bitcast.109) | data formatting | bytes 262144 | tf_op jit(solution)/shard_map/reshape | solution.py:135
  86.4 3.3 %all-to-all-start.3 = ((f32[4,64,128]{2,1,0:T(8,128)}), f32[4,64,128]{2,1,0:T(8,128)S(1)}, u32[]{:S(2)}, u32[]{:S(2)}) async-start(f32[4,64,128]{2,1,0:T(8,128)} %reshape.224), calls=%async_computation.3 | async-start | bytes 262144 | tf_op jit(solution)/shard_map/all_to_all | solution.py:137
  89.8 0.6 multiply_add_fusion
  90.4 0.7 convert_element_type.59
  91.0 3.5 %all-to-all-done.3 = f32[4,64,128]{2,1,0:T(8,128)S(1)} async-done(((f32[4,64,128]{2,1,0:T(8,128)}), f32[4,64,128]{2,1,0:T(8,128)S(1)}, u32[]{:S(2)}, u32[]{:S(2)}) %all-to-all-start.3) | async-done | bytes 131104 | tf_op jit(solution)/shard_map/all_to_all | solution.py:137
  94.6 1.1 reshape.225
  95.6 1.9 %copy.34 = f32[4,4,4,16,32]{4,3,2,1,0:T(8,128)} copy(f32[4,4,4,16,32]{4,2,3,1,0:T(4,128)} %bitcast.110) | data formatting | bytes 262144 | tf_op jit(solution)/shard_map/transpose | solution.py:140
  97.5 1.2 reshape.226
  98.8 0.1 copy.35
  98.9 0.6 convolution_bitcast_fusion
  99.5 1.7 copy.36
  101.2 1.7 reshape.227
  102.9 0.0 copy-start.5
  102.9 2.6 %fusion.39 = f32[1024,128]{1,0:T(8,128)} fusion(f32[512,1024]{1,0:T(8,128)S(1)} %copy-done.1, f32[512,128]{1,0:T(8,128)S(1)} %reshape.227), kind=kOutput, calls=%fused_computation.77 | convolution fusion | flops 402653184 | bytes 2883584 | tf_op jit(solution)/shard_map/gx,gl->xl/dot_general | solution.py:59
  105.5 12.8 %all-to-all-start.4 = ((f32[16,64,128]{2,1,0:T(8,128)}), f32[16,64,128]{2,1,0:T(8,128)S(1)}, u32[]{:S(2)}, u32[]{:S(2)}) async-start(f32[16,64,128]{2,1,0:T(8,128)} %bitcast.111), calls=%async_computation.4 | async-start | bytes 1048576 | tf_op jit(solution)/shard_map/all_to_all | solution.py:150
  118.3 0.0 copy-start.7
  118.3 22.5 %all-to-all-done.4 = f32[16,64,128]{2,1,0:T(8,128)S(1)} async-done(((f32[16,64,128]{2,1,0:T(8,128)}), f32[16,64,128]{2,1,0:T(8,128)S(1)}, u32[]{:S(2)}, u32[]{:S(2)}) %all-to-all-start.4) | async-done | bytes 524320 | tf_op jit(solution)/shard_map/all_to_all | solution.py:150
  140.8 0.2 fusion.40
  141.1 0.1 broadcast_in_dim.23
  141.1 0.9 concatenate.17
  142.0 11.8 %all-to-all-start.5 = ((f32[32,40,128]{2,1,0:T(8,128)}), f32[32,40,128]{2,1,0:T(8,128)S(1)}, u32[]{:S(2)}, u32[]{:S(2)}) async-start(f32[32,40,128]{2,1,0:T(8,128)} %bitcast.29), calls=%async_computation.5 | async-start | bytes 1310720 | tf_op jit(solution)/shard_map/all_to_all | solution.py:160
  153.8 0.0 copy-start.2
  153.9 12.2 %all-to-all-done.5 = f32[32,40,128]{2,1,0:T(8,128)S(1)} async-done(((f32[32,40,128]{2,1,0:T(8,128)}), f32[32,40,128]{2,1,0:T(8,128)S(1)}, u32[]{:S(2)}, u32[]{:S(2)}) %all-to-all-start.5) | async-done | bytes 655392 | tf_op jit(solution)/shard_map/all_to_all | solution.py:160
  166.0 0.2 fusion.27
  166.3 0.1 fusion.28
  166.5 0.4 convolution_bitcast_fusion.1
  166.9 1.9 %convolution_bitcast_fusion.3 = f32[128,512]{1,0:T(8,128)S(1)} fusion(f32[4,512,128]{2,1,0:T(8,128)} %constant.77.clone, f32[2,128,4,128]{3,1,2,0:T(8,128)S(1)} %convolution_bitcast_fusion.1), kind=kOutput, calls=%fused_computation.3 | convolution fusion | flops 201326592 | bytes 1572864 | tf_op jit(solution)/shard_map/pvl,vkl->pk/dot_general | solution.py:59
  168.8 1.4 fusion
  (27 shorter events, 0.1 us)
Async XLA Ops:
  0.6 79.0 %copy-start = (f32[16,128,128]{2,1,0:T(8,128)S(1)}, f32[16,128,128]{2,1,0:T(8,128)}, u32[]{:S(2)}) copy-start(f32[16,128,128]{2,1,0:T(8,128)} %param.24) | copy-start | bytes 3145732
  0.6 15.5 %copy-start.4 = (f32[64,128]{1,0:T(8,128)S(1)}, f32[64,128]{1,0:T(8,128)}, u32[]{:S(2)}) copy-start(f32[64,128]{1,0:T(8,128)} %constant.73.clone) | copy-start | bytes 98308
  0.7 5.8 %copy-start.12 = (s32[16]{0:T(128)S(1)}, s32[16]{0:T(128)}, u32[]{:S(2)}) copy-start(s32[16]{0:T(128)} %param.22) | copy-start | bytes 196
  4.0 28.1 %copy-start.10 = (s32[16,128]{1,0:T(8,128)S(1)}, s32[16,128]{1,0:T(8,128)}, u32[]{:S(2)}) copy-start(s32[16,128]{1,0:T(8,128)} %param.26) | copy-start | bytes 24580
  4.0 50.3 %copy-start.1 = (f32[512,1024]{1,0:T(8,128)S(1)}, f32[512,1024]{1,0:T(8,128)}, u32[]{:S(2)}) copy-start(f32[512,1024]{1,0:T(8,128)} %constant.74.clone) | copy-start | bytes 6291460
  17.2 37.2 %all-to-all-start.1 = ((f32[16,64,128]{2,1,0:T(8,128)}), f32[16,64,128]{2,1,0:T(8,128)}, u32[]{:S(2)}, u32[]{:S(2)}) async-start(f32[16,64,128]{2,1,0:T(8,128)} %broadcast_in_dim.17), calls=%async_computation.1 | async-start | bytes 1048576 | tf_op jit(solution)/shard_map/all_to_all | solution.py:98
  63.5 16.2 %copy-start.3 = (f32[16,8,128]{2,1,0:T(8,128)S(1)}, f32[16,8,128]{2,1,0:T(8,128)}, u32[]{:S(2)}) copy-start(f32[16,8,128]{2,1,0:T(8,128)} %param.23) | copy-start | bytes 196612
  66.8 13.4 %copy-start.8 = (f32[16,2,128]{2,1,0:T(2,128)S(1)}, f32[16,2,128]{2,1,0:T(2,128)}, u32[]{:S(2)}) copy-start(f32[16,2,128]{2,1,0:T(2,128)} %param.25) | copy-start | bytes 49156
  66.8 8.3 %all-to-all-start.2 = ((f32[4,64,128]{2,1,0:T(8,128)}), f32[4,64,128]{2,1,0:T(8,128)S(1)}, u32[]{:S(2)}, u32[]{:S(2)}) async-start(f32[4,64,128]{2,1,0:T(8,128)} %reshape.220), calls=%async_computation.2 | async-start | bytes 262144 | tf_op jit(solution)/shard_map/all_to_all | solution.py:115
  80.3 15.3 %copy-start.6 = (f32[16,2,128]{2,1,0:T(2,128)}, f32[16,2,128]{2,1,0:T(2,128)S(1)}, u32[]{:S(2)}) copy-start(f32[16,2,128]{2,1,0:T(2,128)S(1)} %multiply_select_fusion) | copy-start | bytes 49156
  86.4 8.1 %all-to-all-start.3 = ((f32[4,64,128]{2,1,0:T(8,128)}), f32[4,64,128]{2,1,0:T(8,128)S(1)}, u32[]{:S(2)}, u32[]{:S(2)}) async-start(f32[4,64,128]{2,1,0:T(8,128)} %reshape.224), calls=%async_computation.3 | async-start | bytes 262144 | tf_op jit(solution)/shard_map/all_to_all | solution.py:137
  95.6 3.3 %copy-start.9 = (s32[32,4]{0,1:T(4,128)S(1)}, s32[32,4]{0,1:T(4,128)}, u32[]{:S(2)}) copy-start(s32[32,4]{0,1:T(4,128)} %multiply_add_fusion) | copy-start | bytes 1540
  95.6 3.3 %copy-start.11 = (s32[64]{0:T(128)S(1)}, s32[64]{0:T(128)}, u32[]{:S(2)}) copy-start(s32[64]{0:T(128)} %convert_element_type.59) | copy-start | bytes 772
  102.9 38.0 %copy-start.5 = (f32[64,128]{1,0:T(8,128)S(1)}, f32[64,128]{1,0:T(8,128)}, u32[]{:S(2)}) copy-start(f32[64,128]{1,0:T(8,128)} %constant.73.clone) | copy-start | bytes 98308
  105.5 35.3 %all-to-all-start.4 = ((f32[16,64,128]{2,1,0:T(8,128)}), f32[16,64,128]{2,1,0:T(8,128)S(1)}, u32[]{:S(2)}, u32[]{:S(2)}) async-start(f32[16,64,128]{2,1,0:T(8,128)} %bitcast.111), calls=%async_computation.4 | async-start | bytes 1048576 | tf_op jit(solution)/shard_map/all_to_all | solution.py:150
  118.3 48.1 %copy-start.7 = (f32[16,128]{1,0:T(8,128)S(1)}, f32[16,128]{1,0:T(8,128)}, u32[]{:S(2)}) copy-start(f32[16,128]{1,0:T(8,128)} %constant.70.clone) | copy-start | bytes 24580
  142.0 24.0 %all-to-all-start.5 = ((f32[32,40,128]{2,1,0:T(8,128)}), f32[32,40,128]{2,1,0:T(8,128)S(1)}, u32[]{:S(2)}, u32[]{:S(2)}) async-start(f32[32,40,128]{2,1,0:T(8,128)} %bitcast.29), calls=%async_computation.5 | async-start | bytes 1310720 | tf_op jit(solution)/shard_map/all_to_all | solution.py:160
  153.8 15.0 %copy-start.2 = (f32[4,512,128]{2,1,0:T(8,128)S(1)}, f32[4,512,128]{2,1,0:T(8,128)}, u32[]{:S(2)}) copy-start(f32[4,512,128]{2,1,0:T(8,128)} %constant.76.clone) | copy-start | bytes 3145732

commit v2 on v1

--- a/solution.py
+++ b/solution.py
@@ -1,7 +1,11 @@
+import functools
+
 import jax
 import jax.numpy as jnp
 import numpy as np
 from jax import lax
+from jax.experimental import pallas as pl
+from jax.experimental.pallas import tpu as pltpu
 from jax.sharding import PartitionSpec as P
 
 K = 512
@@ -52,11 +56,126 @@
     column = np.arange(K).reshape(bands, vises, sub_lanes).transpose(1, 0, 2).reshape(vises, lanes)
     angle = 2 * np.pi * ((np.arange(K)[None, :, None] * column[:, None, :]) % K) / K
     table = np.concatenate([np.cos(angle), np.sin(angle)], axis=2) * K**-0.5
-    return tuple(np.asarray(x, np.float32) for x in (section.T, merges, spread, table))
+    spread_high = spread.astype(jnp.bfloat16)
+    spread_low = (spread - spread_high.astype(np.float64)).astype(jnp.bfloat16)
+    section, merges, table = (np.asarray(x, np.float32) for x in (section.T, merges, table))
+    return section, merges, (spread_high, spread_low), table
 
 
 def dot(spec, left, right):
     return jnp.einsum(spec, left, right, precision=HIGH, preferred_element_type=jnp.float32)
+
+
+def halves(x):
+    high = x.astype(jnp.bfloat16)
+    return high, (x - high.astype(jnp.float32)).astype(jnp.bfloat16)
+
+
+def mxu(left, right, contract):
+    return lax.dot_general(left, right, (contract, ((), ())), preferred_element_type=jnp.float32)
+
+
+def product(left, right, contract):
+    (lh, ll), (rh, rl) = left, right
+    return mxu(lh, rh, contract) + mxu(lh, rl, contract) + mxu(ll, rh, contract)
+
+
+NN = ((1,), (0,))
+NT = ((1,), (1,))
+TN = ((0,), (0,))
+
+
+def slot_rows(ids_ref, member, vises, groups, first):
+    rows = []
+    for v in range(vises):
+        for g in range(groups):
+            at = first + vises * g + member
+            rows.append(jnp.broadcast_to(ids_ref[v, at : at + 1, :], (2 * BR, BC)))
+    return jnp.concatenate(rows, axis=0).astype(jnp.int32)
+
+
+def selection(ids, bands):
+    inner = lax.broadcasted_iota(jnp.int32, ids.shape, 0) % (2 * BR)
+    target = (ids // bands) * (2 * BR) + inner
+    lane = lax.broadcasted_iota(jnp.int32, ids.shape, 1)
+    pieces = [
+        jnp.where(target == lane + part * BC, 1.0, 0.0).astype(jnp.bfloat16)
+        for part in range(2 * CR // BC)
+    ]
+    return jnp.concatenate(pieces, axis=1), ids % bands
+
+
+def everywhere(x, width):
+    step = BC // 2
+    while step >= width:
+        x = x + pltpu.roll(x, step, 1)
+        step //= 2
+    return x
+
+
+def pick_kernel(vises, groups, coef_ref, ids_ref, high_ref, low_ref, out_ref):
+    width = BC // vises
+    grid = product((high_ref[...], low_ref[...]), halves(coef_ref[...]), NN)
+    high, low = halves(grid)
+    piece = lax.broadcasted_iota(jnp.int32, (vises * groups * 2 * BR, BC), 1) // width
+    total = jnp.zeros((vises * groups * 2 * BR, BC), jnp.float32)
+    for member in range(vises):
+        ids = slot_rows(ids_ref, member, vises, groups, 2 * RANKS)
+        hot, band = selection(ids, K // BC)
+        rows = mxu(hot, high, NN) + mxu(hot, low, NN)
+        rows = everywhere(jnp.where(piece == band, rows, 0.0), width)
+        total = jnp.where(piece == member, rows, total)
+    out_ref[...] = total.reshape(out_ref.shape)
+
+
+def place_kernel(vises, groups, part_ref, ids_ref, high_ref, low_ref, out_ref):
+    width = BC // vises
+    parts = part_ref[...].reshape(vises * groups * 2 * BR, BC)
+    piece = lax.broadcasted_iota(jnp.int32, parts.shape, 1) // width
+    turned = jnp.zeros((BC, 2 * CR), jnp.float32)
+    for member in range(vises):
+        ids = slot_rows(ids_ref, member, vises, groups, 2 * RANKS)
+        hot, band = selection(ids, K // BC)
+        rows = everywhere(jnp.where(piece == member, parts, 0.0), width)
+        high, low = halves(jnp.where(piece == band, rows, 0.0))
+        turned = turned + mxu(high, hot, TN) + mxu(low, hot, TN)
+    coef = product(halves(turned), (high_ref[...], low_ref[...]), NN)
+    out_ref[...] = coef.T.reshape(out_ref.shape)
+
+
+def degrid_kernel(vises, groups, got_ref, rows_ref, cols_ref, seen_ref, scale_ref, res_ref, out_ref):
+    width = BC // vises
+    piece = lax.broadcasted_iota(jnp.int32, (2 * BR, BC), 1) // width
+    for g in range(groups):
+        at = pl.ds(g * 2 * BR, 2 * BR)
+        held = [got_ref[v, at, :] for v in range(vises)]
+        backs = []
+        for member in range(vises):
+            slot = vises * g + member
+            block = held[member]
+            for v in range(vises):
+                if v != member:
+                    moved = pltpu.roll(held[v], (width * (v - member)) % BC, 1)
+                    block = jnp.where(piece == v, moved, block)
+            cols = halves(cols_ref[slot])
+            along = product(halves(block), cols, NN).reshape(2, BR, BC)
+            weight_rows = rows_ref[slot]
+            model = jnp.sum(along * weight_rows[None], axis=1)
+            residual = scale_ref[slot : slot + 1, :] * (seen_ref[slot] - model)
+            res_ref[slot] = residual
+            out = (weight_rows[None] * residual[:, None, :]).reshape(2 * BR, BC)
+            backs.append(product(halves(out), cols, NT))
+        for v in range(vises):
+            sent = backs[v]
+            for member in range(vises):
+                if member != v:
+                    moved = pltpu.roll(backs[member], (width * (member - v)) % BC, 1)
+                    sent = jnp.where(piece == member, moved, sent)
+            out_ref[v, at, :] = sent
+
+
+def whole():
+    return pl.BlockSpec(memory_space=pltpu.VMEM)
 
 
 def shards(sky, row_offsets, block_counts, block_ids, kernel_rows, kernel_cols, observed, weights):
@@ -67,14 +186,15 @@
     rows = sky.shape[0]
     lanes = K // vises
     slots = block_ids.shape[0]
-    bands = K // BC
-    row_bands = CR // BR
     groups = slots // vises
-    sub_lanes = BC // vises
     section, merges, spread, table = constants(facets, vises, total)
 
     first = (lax.axis_index("facet") * vises + lax.axis_index("vis")) * rows
     pixels = first + jnp.arange(rows, dtype=jnp.int32)
+
+    live = jnp.arange(slots, dtype=jnp.int32)[:, None] < block_counts[0]
+    scale = jnp.where(live, weights.astype(jnp.float32), 0.0)
+    offset_value = row_offsets[0].astype(jnp.float32)
 
     def phases(offsets):
         product = ((2 * offsets + (CR - 1)) * pixels) % (2 * total)
@@ -91,69 +211,50 @@
         block_ids.astype(jnp.float32)[None, :, None], (vises, slots, lanes)
     )
     sent = jnp.concatenate([real, imag, ids_rows], axis=1)
+    sent, scale, offset_value, pixels = lax.optimization_barrier(
+        (sent, scale, offset_value, pixels)
+    )
     got = lax.all_to_all(sent, "vis", 0, 0, tiled=True)
-    ids = got[:, 2 * RANKS :, 0].astype(jnp.int32).reshape(vises * slots)
+    held = got
     facet_coef = dot("kx,xl->kl", merges, got[:, : 2 * RANKS].reshape(vises * 2 * RANKS, lanes))
     sent = jnp.broadcast_to(facet_coef[None], (facets, 2 * RANK, lanes))
     got = lax.all_to_all(sent, "facet", 0, 0, tiled=True)
 
-    grid = dot("gx,xl->gl", spread, got.reshape(facets * 2 * RANK, lanes))
-    onehot = (ids[:, None] == jnp.arange(row_bands * bands, dtype=jnp.int32)[None, :]).astype(
-        jnp.float32
-    )
-    blocks = (
-        grid.reshape(row_bands, 2 * BR, bands, sub_lanes)
-        .transpose(0, 2, 1, 3)
-        .reshape(row_bands * bands, 2 * BR * sub_lanes)
-    )
-    picked = dot("sn,nx->sx", onehot, blocks)
-    sent = (
-        picked.reshape(vises, groups, vises, 2 * BR, sub_lanes)
-        .transpose(0, 1, 3, 2, 4)
-        .reshape(vises, groups * 2 * BR, lanes)
-    )
+    high, low = (jnp.asarray(x) for x in spread)
+    sent = pl.pallas_call(
+        functools.partial(pick_kernel, vises, groups),
+        out_shape=jax.ShapeDtypeStruct((vises, groups * 2 * BR, lanes), jnp.float32),
+        in_specs=[whole()] * 4,
+        out_specs=whole(),
+        compiler_params=pltpu.CompilerParams(vmem_limit_bytes=16 << 20),
+        name="pick",
+    )(got.reshape(facets * 2 * RANK, lanes), held, high, low)
     got = lax.all_to_all(sent, "vis", 0, 0, tiled=True)
-    chosen = (
-        got.reshape(vises, groups, 2 * BR, vises, sub_lanes)
-        .transpose(1, 3, 2, 0, 4)
-        .reshape(slots, 2, BR, BC)
-    )
-
-    along = dot("szrc,sct->szrt", chosen, kernel_cols)
-    model = jnp.sum(along * kernel_rows[:, None, :, :], axis=2)
-    live = (jnp.arange(slots, dtype=jnp.int32) < block_counts[0])[:, None, None]
-    residual = jnp.where(
-        live, weights[:, None, :].astype(jnp.float32) * (observed - model), jnp.zeros_like(model)
-    )
-    back = dot(
-        "szrt,sct->szrc", kernel_rows[:, None, :, :] * residual[:, :, None, :], kernel_cols
-    )
-
-    sent = (
-        back.reshape(groups, vises, 2 * BR, vises, sub_lanes)
-        .transpose(3, 0, 2, 1, 4)
-        .reshape(vises, groups * 2 * BR, lanes)
-    )
+    residual, sent = pl.pallas_call(
+        functools.partial(degrid_kernel, vises, groups),
+        out_shape=(
+            jax.ShapeDtypeStruct((slots, 2, BC), jnp.float32),
+            jax.ShapeDtypeStruct((vises, groups * 2 * BR, lanes), jnp.float32),
+        ),
+        in_specs=[whole()] * 5,
+        out_specs=(whole(), whole()),
+        compiler_params=pltpu.CompilerParams(vmem_limit_bytes=16 << 20),
+        name="degrid",
+    )(got, kernel_rows, kernel_cols, observed, scale)
     got = lax.all_to_all(sent, "vis", 0, 0, tiled=True)
-    parts = (
-        got.reshape(vises, groups, 2 * BR, vises, sub_lanes)
-        .transpose(0, 1, 3, 2, 4)
-        .reshape(vises * slots, 2 * BR * sub_lanes)
-    )
-    summed = dot("sn,sx->nx", onehot, parts)
-    residual_grid = (
-        summed.reshape(row_bands, bands, 2 * BR, sub_lanes)
-        .transpose(0, 2, 1, 3)
-        .reshape(2 * CR, lanes)
-    )
-    sent = dot("gx,gl->xl", spread, residual_grid).reshape(facets, 2 * RANK, lanes)
+    sent = pl.pallas_call(
+        functools.partial(place_kernel, vises, groups),
+        out_shape=jax.ShapeDtypeStruct((facets, 2 * RANK, lanes), jnp.float32),
+        in_specs=[whole()] * 4,
+        out_specs=whole(),
+        compiler_params=pltpu.CompilerParams(vmem_limit_bytes=16 << 20),
+        name="place",
+    )(got, held, high, low)
     got = lax.all_to_all(sent, "facet", 0, 0, tiled=True)
     facet_coef = jnp.sum(got, axis=0)
 
     coef = dot("kx,kl->xl", merges, facet_coef).reshape(1, vises, 2 * RANKS, lanes)
-    offset_rows = jnp.broadcast_to(
-        row_offsets[0].astype(jnp.float32), (subs, vises, 8, lanes)
-    )
+    offset_rows = jnp.broadcast_to(offset_value, (subs, vises, 8, lanes))
     sent = jnp.concatenate(
         [jnp.broadcast_to(coef, (subs, vises, 2 * RANKS, lanes)), offset_rows], axis=2
     ).reshape(subs * vises, 2 * RANKS + 8, lanes)
@@ -166,14 +267,13 @@
     out = jnp.stack(
         [
             jnp.concatenate([cos_q, -sin_q], axis=1),
-            jnp.concatenate([sin_q, cos_q], axis=1),
+            jnp.concatenate([-sin_q, -cos_q], axis=1),
         ],
         axis=0,
     )
     pixels_cols = dot("zqap,qval->zpvl", out, got[:, :, : 2 * RANKS])
-    image = dot("pvl,vkl->pk", pixels_cols[0], table[:, :, :lanes]) - dot(
-        "pvl,vkl->pk", pixels_cols[1], table[:, :, lanes:]
-    )
+    pixels_cols = jnp.concatenate([pixels_cols[0], pixels_cols[1]], axis=2)
+    image = dot("pvl,vkl->pk", pixels_cols, table)
     return (image, residual)
 
 

time: 172 us -> 138 us (0.80)
  blocking collectives: 9.44 us -> 120 us
  waiting for transfers between devices: 64.3 us -> 0 us
  starting transfers between devices: 46.3 us -> 0 us
  local copies, waits for them, and re-layouts: 29.2 us -> 0.33 us
  matrix products: 15.7 us -> 5.58 us
  Pallas kernels: 0 us -> 7.2 us
    all_to_all x0 -> x3, blocking collectives: none -> 96 us  [the longest x2 72.1 us: shards(): got = lax.all_to_all(sent, 'facet', 0, 0, tiled=True)]
    all_to_all x5 -> x0, waiting for transfers between devices: 64.3 us -> none  [the longest x2 43.8 us: shards(): got = lax.all_to_all(sent, 'facet', 0, 0, tiled=True)]
    all_to_all x5 -> x0, starting transfers between devices: 46.3 us -> none  [the longest x2 27.7 us: shards(): got = lax.all_to_all(sent, 'facet', 0, 0, tiled=True)]
    reshape x13 -> x0, local copies, waits for them, and re-layouts: 21.7 us -> none  [the longest x3 4.32 us: shards(): got.reshape(vises, groups, 2 * BR, vises, sub_lanes)]
    all_to_all x1 -> x3, blocking collectives: 9.44 us -> 23.9 us  [shards(): got = lax.all_to_all(sent, 'vis', 0, 0, tiled=True)]
    dot_general x13 -> x6, matrix products: 15.7 us -> 5.58 us  [dot(): jnp.einsum(spec, left, right, precision=HIGH, preferred_element_type=jnp....]
    pallas_call x0 -> x3, Pallas kernels: none -> 7.2 us  [the longest x1 2.81 us: shards(): pl.pallas_call(functools.partial(pick_kernel, vises, groups), out_shape=j...]
    transpose x2 -> x0, local copies, waits for them, and re-layouts: 3.54 us -> none  [the longest x1 1.89 us: shards(): parts = got.reshape(vises, groups, 2 * BR, vises, sub_lanes).transpose(0,...]
  transfers between devices with their start and end apart: 5 -> 0, of which waited for: 5 -> 0; matrix products, arithmetic and copies ran while one was open for 1% -> 0% of each run, Pallas kernels for 0% -> 0%
where the time goes in v2:
time: 138 us
  blocking collectives  120 us (87%)
  Pallas kernels  7.2 us (5%)
  matrix products  5.58 us (4%)
  other arithmetic  2.71 us (2%)
  between operations  2.19 us (2%)
    all_to_all x2, blocking collectives, shards(): got = lax.all_to_all(sent, 'facet', 0, 0, tiled=True)  72.1 us
    all_to_all x1, blocking collectives, shards(): got = lax.all_to_all(sent, ('sub', 'vis'), 0, 0, tiled=True)  23.9 us
    all_to_all x3, blocking collectives, shards(): got = lax.all_to_all(sent, 'vis', 0, 0, tiled=True)  23.9 us
    dot_general x6, matrix products, dot(): jnp.einsum(spec, left, right, precision=HIGH, preferred_element_type=jnp....  5.58 us
    pallas_call x1, Pallas kernels, shards(): pl.pallas_call(functools.partial(pick_kernel, vises, groups), out_shape=j...  2.81 us

profile of v2, /device:TPU:1, one launch (start us, length us, event | category | flops | bytes accessed | tf_op | source)
XLA Modules:
  0.0 137.8 jit_solution(4159063692009214623)
XLA Ops:
  0.6 0.0 copy-start
  0.6 0.0 copy-start.7
  0.7 0.0 copy-start.9
  2.0 0.7 convert_element_type.41
  2.7 0.1 fusion.23
  2.7 0.7 broadcast_multiply_fusion.1
  3.4 0.7 broadcast_multiply_fusion.2
  4.1 0.0 copy-done
  4.1 0.2 convolution_bitcast_fusion.3
  4.3 0.0 copy-start.1
  4.3 0.0 copy-start.2
  4.4 2.4 %convolution_bitcast_fusion.2 = f32[4,32,256]{2,1,0:T(8,128)S(1)} fusion(f32[32,512,1]{1,0,2:T(8,128)S(1)} %convolution_bitcast_fusion.3, f32[4,512,256]{2,1,0:T(8,128)} %constant.68.clone), kind=kOutput, calls=%fused_computation.2 | convolution fusion | flops 100663296 | bytes 2293760 | tf_op jit(solution)/shard_map/mk,vkc->vmc/dot_general | solution.py:66
  6.8 0.1 pad.11.clone
  6.9 0.0 copy-done.9
  6.9 0.1 convert_select_fusion.scale_ref
  7.0 0.1 maximum_maximum_fusion
  7.0 9.4 %all_to_all.30.ids_ref = f32[4,48,128]{2,1,0:T(8,128)S(1)} all-to-all(f32[4,48,128]{2,1,0:T(8,128)S(1)} %maximum_maximum_fusion), channel_id=1, replica_groups=mesh['facet'=16,'sub'=8,'vis'=4] {'vis'}, dimensions={0} | all-to-all | bytes 196608 | tf_op jit(solution)/shard_map/all_to_all | solution.py:217
  16.5 0.0 copy-done.7
  16.5 0.2 fusion.25
  16.7 0.0 copy-start.3
  16.7 0.0 copy-start.4
  16.7 0.0 copy-start.5
  16.8 37.0 %all_to_all.31 = f32[16,64,128]{2,1,0:T(8,128)S(1)} all-to-all(f32[16,64,128]{2,1,0:T(8,128)S(1)} %broadcast_in_dim.23), channel_id=1, replica_groups=mesh['facet'=16,'sub'=8,'vis'=4] {'facet'}, dimensions={0} | all-to-all | bytes 1048576 | tf_op jit(solution)/shard_map/all_to_all | solution.py:221
  53.7 0.0 copy-done.1
  53.7 0.0 copy-done.2
  53.7 2.8 %pick.1 = f32[4,64,128]{2,1,0:T(8,128)S(1)} custom-call(f32[1024,128]{1,0:T(8,128)S(1)} %bitcast.42, f32[4,48,128]{2,1,0:T(8,128)S(1)} %all_to_all.30.ids_ref, bf16[512,1024]{1,0:T(8,128)(2,1)S(1)} %copy-done.2, bf16[512,1024]{1,0:T(8,128)(2,1)S(1)} %copy-done.1), custom_call_target="tpu_custom_call" | custom-call | tf_op jit(solution)/shard_map/pick/pallas_call | solution.py:224
  56.6 7.2 %all_to_all.32.got_ref = f32[4,64,128]{2,1,0:T(8,128)S(1)} all-to-all(f32[4,64,128]{2,1,0:T(8,128)S(1)} %pick.1), channel_id=1, replica_groups=mesh['facet'=16,'sub'=8,'vis'=4] {'vis'}, dimensions={0} | all-to-all | bytes 262144 | tf_op jit(solution)/shard_map/all_to_all | solution.py:232
  63.8 0.0 copy-done.3
  63.8 0.0 copy-done.4
  63.8 0.0 copy-done.5
  63.8 2.6 %degrid.1 = (f32[16,2,128]{2,1,0:T(2,128)}, f32[4,64,128]{2,1,0:T(8,128)S(1)}) custom-call(f32[4,64,128]{2,1,0:T(8,128)S(1)} %all_to_all.32.got_ref, f32[16,8,128]{2,1,0:T(8,128)S(1)} %copy-done.4, f32[16,128,128]{2,1,0:T(8,128)S(1)} %copy-done.3, f32[16,2,128]{2,1,0:T(2,128)S(1)} %copy-done.5, f32[16,128]{1,0:T(8,128)S(1)} %convert_select_fusion.scale_ref), custom_call_target="tpu_custom_call" | custom-call | tf_op jit(solution)/shard_map/degrid/pallas_call | solution.py:233
  66.4 7.2 %all_to_all.33.part_ref = f32[4,64,128]{2,1,0:T(8,128)S(1)} all-to-all(f32[4,64,128]{2,1,0:T(8,128)S(1)} %get-tuple-element.10), channel_id=1, replica_groups=mesh['facet'=16,'sub'=8,'vis'=4] {'vis'}, dimensions={0} | all-to-all | bytes 262144 | tf_op jit(solution)/shard_map/all_to_all | solution.py:244
  73.6 1.8 %place.1 = f32[16,64,128]{2,1,0:T(8,128)S(1)} custom-call(f32[4,64,128]{2,1,0:T(8,128)S(1)} %all_to_all.33.part_ref, f32[4,48,128]{2,1,0:T(8,128)S(1)} %all_to_all.30.ids_ref, bf16[512,1024]{1,0:T(8,128)(2,1)S(1)} %copy-done.2, bf16[512,1024]{1,0:T(8,128)(2,1)S(1)} %copy-done.1), custom_call_target="tpu_custom_call" | custom-call | tf_op jit(solution)/shard_map/place/pallas_call | solution.py:245
  75.4 35.1 %all_to_all.34 = f32[16,64,128]{2,1,0:T(8,128)S(1)} all-to-all(f32[16,64,128]{2,1,0:T(8,128)S(1)} %place.1), channel_id=1, replica_groups=mesh['facet'=16,'sub'=8,'vis'=4] {'facet'}, dimensions={0} | all-to-all | bytes 1048576 | tf_op jit(solution)/shard_map/all_to_all | solution.py:253
  110.5 0.0 copy-start.8
  110.5 0.3 fusion.26
  110.8 0.1 broadcast_in_dim.25
  110.8 0.1 concatenate.20
  110.9 0.0 copy-start.6
  110.9 23.9 %all_to_all.35 = f32[32,40,128]{2,1,0:T(8,128)S(1)} all-to-all(f32[32,40,128]{2,1,0:T(8,128)S(1)} %bitcast.43), channel_id=1, replica_groups=mesh['facet'=16,'sub'=8,'vis'=4] {'sub','vis'}, dimensions={0} | all-to-all | bytes 1310720 | tf_op jit(solution)/shard_map/all_to_all | solution.py:261
  134.8 0.2 fusion.14
  135.0 0.1 fusion.15
  135.2 0.0 copy-done.8
  135.2 0.6 convolution_bitcast_fusion
  135.9 0.0 copy-done.6
  135.9 1.9 %convolution_bitcast_fusion.1 = f32[128,512]{1,0:T(8,128)} fusion(f32[4,512,256]{2,1,0:T(8,128)S(1)} %copy-done.6, f32[128,4,128]{0,2,1:T(8,128)S(1)} %get-tuple-element.15, f32[128,4,128]{0,2,1:T(8,128)S(1)} %get-tuple-element.14), kind=kOutput, calls=%fused_computation.1 | convolution fusion | flops 402784256 | bytes 2883584 | tf_op jit(solution)/shard_map/pvl,vkl->pk/dot_general | solution.py:66
  (9 shorter events, 0.2 us)
Async XLA Ops:
  0.6 3.5 %copy-start = (f32[128,512]{1,0:T(8,128)S(1)}, f32[128,512]{1,0:T(8,128)}, u32[]{:S(2)}) copy-start(f32[128,512]{1,0:T(8,128)} %param.18) | copy-start | bytes 786436
  0.6 15.8 %copy-start.7 = (f32[64,128]{1,0:T(8,128)S(1)}, f32[64,128]{1,0:T(8,128)}, u32[]{:S(2)}) copy-start(f32[64,128]{1,0:T(8,128)} %constant.69.clone) | copy-start | bytes 98308
  0.7 6.2 %copy-start.9 = (s32[16,128]{1,0:T(8,128)S(1)}, s32[16,128]{1,0:T(8,128)}, u32[]{:S(2)}) copy-start(s32[16,128]{1,0:T(8,128)} %param.25) | copy-start | bytes 24580
  4.3 49.4 %copy-start.1 = (bf16[512,1024]{1,0:T(8,128)(2,1)S(1)}, bf16[512,1024]{1,0:T(8,128)(2,1)}, u32[]{:S(2)}) copy-start(bf16[512,1024]{1,0:T(8,128)(2,1)} %constant.71.clone.low_ref) | copy-start | bytes 3145732
  4.3 49.4 %copy-start.2 = (bf16[512,1024]{1,0:T(8,128)(2,1)S(1)}, bf16[512,1024]{1,0:T(8,128)(2,1)}, u32[]{:S(2)}) copy-start(bf16[512,1024]{1,0:T(8,128)(2,1)} %constant.70.clone.high_ref) | copy-start | bytes 3145732
  16.7 47.1 %copy-start.3 = (f32[16,128,128]{2,1,0:T(8,128)S(1)}, f32[16,128,128]{2,1,0:T(8,128)}, u32[]{:S(2)}) copy-start(f32[16,128,128]{2,1,0:T(8,128)} %cols_ref.1) | copy-start | bytes 3145732
  16.7 47.0 %copy-start.4 = (f32[16,8,128]{2,1,0:T(8,128)S(1)}, f32[16,8,128]{2,1,0:T(8,128)}, u32[]{:S(2)}) copy-start(f32[16,8,128]{2,1,0:T(8,128)} %rows_ref.1) | copy-start | bytes 196612
  16.7 47.0 %copy-start.5 = (f32[16,2,128]{2,1,0:T(2,128)S(1)}, f32[16,2,128]{2,1,0:T(2,128)}, u32[]{:S(2)}) copy-start(f32[16,2,128]{2,1,0:T(2,128)} %seen_ref.1) | copy-start | bytes 49156
  110.5 24.7 %copy-start.8 = (f32[16,128]{1,0:T(8,128)S(1)}, f32[16,128]{1,0:T(8,128)}, u32[]{:S(2)}) copy-start(f32[16,128]{1,0:T(8,128)} %constant.66.clone) | copy-start | bytes 24580
  110.9 25.0 %copy-start.6 = (f32[4,512,256]{2,1,0:T(8,128)S(1)}, f32[4,512,256]{2,1,0:T(8,128)}, u32[]{:S(2)}) copy-start(f32[4,512,256]{2,1,0:T(8,128)} %constant.68.clone) | copy-start | bytes 6291460

commit v3 on v2

v3 whole, which is shorter than its diff:
```python
import functools

import jax
import jax.numpy as jnp
import numpy as np
from jax import lax
from jax.experimental import pallas as pl
from jax.experimental.pallas import tpu as pltpu
from jax.sharding import PartitionSpec as P

K = 512
CR = 256
BR = 8
BC = 128
SUBS = 8
RANK = 28
RANKS = 16
SPARE = RANKS - 1
HIGH = lax.Precision.HIGH


def prolate(count, band, total, rank):
    j = np.arange(count, dtype=np.float64)
    diag = -np.cos(np.pi * (2 * j - count + 1) / total) * np.cos(np.pi * band / total)
    m = np.arange(1, count, dtype=np.float64)
    off = np.sin(np.pi * m / total) * np.sin(np.pi * (count - m) / total)
    values, vectors = np.linalg.eigh(np.diag(diag) + np.diag(off, 1) + np.diag(off, -1))
    basis = vectors[:, ::-1][:, :rank]
    signs = np.sign(np.sum(basis[count // 2 :], axis=0))
    return basis * signs


def constants(facets, vises, total):
    rows = K // vises
    lanes = K // vises
    bands = K // BC
    sub_lanes = BC // vises
    basis = prolate(K, CR, total, RANK)
    section = prolate(rows, CR, total, RANKS)
    section[:, SPARE] = 0.0
    merge = np.stack([section.T @ basis[v * rows : (v + 1) * rows] for v in range(vises)])
    r = np.arange(CR) - (CR - 1) / 2
    p = np.arange(K) - (K - 1) / 2
    kernel = np.exp(-2j * np.pi * np.outer(r, p) / total) @ basis
    centres = np.arange(facets) * K + (K - 1) / 2
    shift = np.exp(-2j * np.pi * np.outer(r, centres) / total)
    expand = shift[:, :, None] * kernel[:, None, :] * total**-0.5
    real, imag = expand.real, expand.imag
    spread = np.stack(
        [np.stack([real, -imag], axis=2), np.stack([imag, real], axis=2)], axis=0
    )
    spread = spread.reshape(2, CR // BR, BR, facets * 2 * RANK).transpose(1, 0, 2, 3)
    spread = spread.reshape(2 * CR, facets * 2 * RANK)
    merges = np.zeros((2, RANK, vises, 2, RANKS))
    for part in range(2):
        merges[part, :, :, part, :] = merge.transpose(2, 0, 1)
    merges = merges.reshape(2 * RANK, vises * 2 * RANKS)
    column = np.arange(K).reshape(bands, vises, sub_lanes).transpose(1, 0, 2).reshape(vises, lanes)
    angle = 2 * np.pi * ((np.arange(K)[None, :, None] * column[:, None, :]) % K) / K
    table = np.concatenate([np.cos(angle), np.sin(angle)], axis=2) * K**-0.5
    shares = bf16_halves(merges.T)
    section, merges = (np.asarray(x, np.float32) for x in (section.T, merges))
    return section, merges, shares, bf16_halves(spread), bf16_halves(table)


def bf16_halves(x):
    high = x.astype(jnp.bfloat16)
    return high, (x - high.astype(np.float64)).astype(jnp.bfloat16)


def dot(spec, left, right):
    return jnp.einsum(spec, left, right, precision=HIGH, preferred_element_type=jnp.float32)


def halves(x):
    high = x.astype(jnp.bfloat16)
    return high, (x - high.astype(jnp.float32)).astype(jnp.bfloat16)


def mxu(left, right, contract):
    return lax.dot_general(left, right, (contract, ((), ())), preferred_element_type=jnp.float32)


NN = ((1,), (0,))
NT = ((1,), (1,))
TN = ((0,), (0,))


def stacked(left, right, contract):
    rows = left.shape[0]
    high, low = halves(left)
    both = mxu(jnp.concatenate([high, low], axis=0), right[0], contract)
    return both[:rows] + both[rows:] + mxu(high, right[1], contract)


def product(left, right, contract):
    (lh, ll), (rh, rl) = left, right
    return mxu(lh, rh, contract) + mxu(lh, rl, contract) + mxu(ll, rh, contract)


def wide(x):
    return jnp.concatenate(halves(x), axis=1)


def angles(offset, first, total):
    pixel = first + lax.broadcasted_iota(jnp.int32, (1, BC), 1)
    turn = ((2 * offset + (CR - 1)) * pixel) % (2 * total)
    angle = turn.astype(jnp.float32) * (jnp.pi / total)
    return jnp.cos(angle), jnp.sin(angle)


def first_pixel(rows):
    return (lax.axis_index("facet") * lax.axis_size("vis") + lax.axis_index("vis")) * rows


def project_kernel(vises, total, offset_ref, count_ref, id_ref, sky_ref, wt_ref, section_ref, high_ref, low_ref, out_ref, scale_ref, offset_row_ref):
    slots = wt_ref.shape[0]
    slot = lax.broadcasted_iota(jnp.int32, wt_ref.shape, 0)
    scale_ref[...] = jnp.where(slot < count_ref[0], wt_ref[...].astype(jnp.float32), 0.0)
    lane = lax.broadcasted_iota(jnp.int32, (1, BC), 1)
    ids = jnp.zeros((1, BC), jnp.int32)
    for s in range(slots):
        ids = jnp.where(lane == s, id_ref[s], ids)
    offset = jnp.full(offset_row_ref.shape, offset_ref[0], jnp.int32)
    offset_row_ref[...] = offset.astype(jnp.float32)
    cos_p, sin_p = angles(offset_ref[0], first_pixel(sky_ref.shape[0]), total)
    section = section_ref[...]
    into = jnp.concatenate([section * cos_p, -section * sin_p], axis=0)
    coef = stacked(into, halves(sky_ref[...]), NN)
    for v in range(vises):
        both = stacked(coef, (high_ref[v], low_ref[v]), NN)
        out_ref[v, :RANKS, :] = both[:RANKS, :BC] + both[RANKS:, BC:]
        out_ref[v, RANKS:, :] = both[RANKS:, :BC] - both[:RANKS, BC:]
        out_ref[v, SPARE : SPARE + 1, :] = ids.astype(jnp.float32)


def ids_columns(held_ref, vises, slots):
    row = lax.broadcasted_iota(jnp.int32, (slots, BC), 0)
    lane = lax.broadcasted_iota(jnp.int32, (slots, BC), 1)
    columns = []
    for v in range(vises):
        ids = jnp.broadcast_to(held_ref[v, SPARE : SPARE + 1, :], (slots, BC))
        column = jnp.sum(jnp.where(row == lane, ids, 0.0), axis=1, keepdims=True)
        columns.append(jnp.broadcast_to(column, (slots, BC)).astype(jnp.int32))
    return columns


def slot_rows(columns, member, vises, groups):
    rows = []
    for v in range(vises):
        for g in range(groups):
            at = vises * g + member
            rows.append(jnp.broadcast_to(columns[v][at : at + 1], (2 * BR, BC)))
    return jnp.concatenate(rows, axis=0)


def selection(ids, bands):
    inner = lax.broadcasted_iota(jnp.int32, ids.shape, 0) % (2 * BR)
    target = (ids // bands) * (2 * BR) + inner
    lane = lax.broadcasted_iota(jnp.int32, ids.shape, 1)
    pieces = [
        jnp.where(target == lane + part * BC, 1.0, 0.0).astype(jnp.bfloat16)
        for part in range(2 * CR // BC)
    ]
    return jnp.concatenate(pieces, axis=1), ids % bands


def everywhere(x, width):
    step = BC // 2
    while step >= width:
        x = x + pltpu.roll(x, step, 1)
        step //= 2
    return x


def pick_kernel(vises, groups, coef_ref, held_ref, high_ref, low_ref, out_ref):
    width = BC // vises
    coef = wide(coef_ref[...])
    grid = mxu(high_ref[...], coef, NN)
    grid = grid[:, :BC] + grid[:, BC:] + mxu(low_ref[...], coef[:, :BC], NN)
    grid = wide(grid)
    columns = ids_columns(held_ref, vises, vises * groups)
    piece = lax.broadcasted_iota(jnp.int32, (vises * groups * 2 * BR, BC), 1) // width
    total = jnp.zeros((vises * groups * 2 * BR, BC), jnp.float32)
    for member in range(vises):
        hot, band = selection(slot_rows(columns, member, vises, groups), K // BC)
        rows = mxu(hot, grid, NN)
        rows = rows[:, :BC] + rows[:, BC:]
        rows = everywhere(jnp.where(piece == band, rows, 0.0), width)
        total = jnp.where(piece == member, rows, total)
    out_ref[...] = total.reshape(out_ref.shape)


def place_kernel(vises, groups, part_ref, held_ref, high_ref, low_ref, out_ref):
    width = BC // vises
    parts = part_ref[...].reshape(vises * groups * 2 * BR, BC)
    columns = ids_columns(held_ref, vises, vises * groups)
    piece = lax.broadcasted_iota(jnp.int32, parts.shape, 1) // width
    turned = jnp.zeros((2 * BC, 2 * CR), jnp.float32)
    for member in range(vises):
        hot, band = selection(slot_rows(columns, member, vises, groups), K // BC)
        rows = everywhere(jnp.where(piece == member, parts, 0.0), width)
        turned = turned + mxu(wide(jnp.where(piece == band, rows, 0.0)), hot, TN)
    turned = turned[:BC] + turned[BC:]
    coef = stacked(turned, (high_ref[...], low_ref[...]), NN)
    out_ref[...] = coef.T.reshape(out_ref.shape)


def degrid_kernel(vises, groups, got_ref, rows_ref, cols_ref, seen_ref, scale_ref, res_ref, out_ref):
    width = BC // vises
    tall = 2 * BR
    piece = lax.broadcasted_iota(jnp.int32, (tall, BC), 1) // width
    for g in range(groups):
        at = pl.ds(g * tall, tall)
        held = [got_ref[v, at, :] for v in range(vises)]
        backs = []
        for member in range(vises):
            slot = vises * g + member
            block = held[member]
            for v in range(vises):
                if v != member:
                    moved = pltpu.roll(held[v], (width * (v - member)) % BC, 1)
                    block = jnp.where(piece == v, moved, block)
            high, low = halves(cols_ref[slot])
            both = mxu(
                jnp.concatenate(halves(block), axis=0), jnp.concatenate([high, low], axis=1), NN
            )
            along = both[:tall, :BC] + both[:tall, BC:] + both[tall:, :BC]
            weight_rows = rows_ref[slot]
            model = jnp.sum(along.reshape(2, BR, BC) * weight_rows[None], axis=1)
            residual = scale_ref[slot : slot + 1, :] * (seen_ref[slot] - model)
            res_ref[slot] = residual
            out = (weight_rows[None] * residual[:, None, :]).reshape(tall, BC)
            both = mxu(
                jnp.concatenate(halves(out), axis=0), jnp.concatenate([high, low], axis=0), NT
            )
            backs.append(both[:tall, :BC] + both[:tall, BC:] + both[tall:, :BC])
        for v in range(vises):
            sent = backs[v]
            for member in range(vises):
                if member != v:
                    moved = pltpu.roll(backs[member], (width * (member - v)) % BC, 1)
                    sent = jnp.where(piece == member, moved, sent)
            out_ref[v, at, :] = sent


def share_kernel(vises, subs, got_ref, offset_row_ref, high_ref, low_ref, out_ref):
    facet = got_ref[0]
    for f in range(1, got_ref.shape[0]):
        facet = facet + got_ref[f]
    coef = product((high_ref[...], low_ref[...]), halves(facet), NN)
    row = lax.broadcasted_iota(jnp.int32, coef.shape, 0) % (2 * RANKS)
    coef = jnp.where(row == SPARE, offset_row_ref[:1, :], coef)
    coef = coef.reshape(vises, 2 * RANKS, BC)
    for q in range(subs):
        out_ref[q * vises : (q + 1) * vises] = coef


def image_kernel(vises, subs, total, got_ref, section_ref, high_ref, low_ref, out_ref):
    rows = out_ref.shape[0]
    section = section_ref[...]
    first = first_pixel(rows)
    out = []
    coef = []
    for q in range(subs):
        offset = got_ref[q * vises, SPARE : SPARE + 1, :].astype(jnp.int32)
        cos_p, sin_p = angles(offset, first, total)
        cos_p, sin_p = section * cos_p, section * sin_p
        out.append(
            jnp.concatenate(
                [
                    jnp.concatenate([cos_p, -sin_p], axis=1),
                    jnp.concatenate([-sin_p, -cos_p], axis=1),
                ],
                axis=0,
            )
        )
        coef.append(jnp.concatenate([got_ref[q * vises + v] for v in range(vises)], axis=1))
    out_high, out_low = halves(jnp.concatenate(out, axis=0))
    high, low = halves(jnp.concatenate(coef, axis=0))
    grid = mxu(out_high, high, TN) + mxu(out_high, low, TN) + mxu(out_low, high, TN)
    image = jnp.zeros(out_ref.shape, jnp.float32)
    for v in range(vises):
        at = slice(v * BC, (v + 1) * BC)
        part = jnp.concatenate([grid[:rows, at], grid[rows:, at]], axis=1)
        image = image + stacked(part, (high_ref[v], low_ref[v]), NT)
    out_ref[...] = image


def whole():
    return pl.BlockSpec(memory_space=pltpu.VMEM)


def shards(sky, row_offsets, block_counts, block_ids, kernel_rows, kernel_cols, observed, weights):
    facets = lax.axis_size("facet")
    vises = lax.axis_size("vis")
    subs = lax.axis_size("sub")
    total = facets * K
    rows = sky.shape[0]
    lanes = K // vises
    slots = block_ids.shape[0]
    groups = slots // vises
    section, merges, shares, spread, table = constants(facets, vises, total)
    shares = [jnp.asarray(x) for x in shares]
    spread = [jnp.asarray(x) for x in spread]
    table = [jnp.asarray(x) for x in table]

    def call(kernel, name, args, outs, scalars=0):
        smem = pl.BlockSpec(memory_space=pltpu.SMEM)
        specs = tuple(whole() for _ in outs)
        return pl.pallas_call(
            kernel,
            out_shape=tuple(jax.ShapeDtypeStruct(x, jnp.float32) for x in outs),
            in_specs=[smem] * scalars + [whole()] * (len(args) - scalars),
            out_specs=specs,
            compiler_params=pltpu.CompilerParams(vmem_limit_bytes=16 << 20),
            name=name,
        )(*args)

    sent, scale, offset_row = call(
        functools.partial(project_kernel, vises, total),
        "project",
        (row_offsets, block_counts, block_ids, sky, weights, section, *table),
        ((vises, 2 * RANKS, lanes), (slots, BC), (8, lanes)),
        scalars=3,
    )
    held = lax.all_to_all(sent, "vis", 0, 0, tiled=True)
    facet_coef = dot("kx,xl->kl", merges, held.reshape(vises * 2 * RANKS, lanes))
    sent = jnp.broadcast_to(facet_coef[None], (facets, 2 * RANK, lanes))
    got = lax.all_to_all(sent, "facet", 0, 0, tiled=True)

    exchange = (vises, groups * 2 * BR, lanes)
    (sent,) = call(
        functools.partial(pick_kernel, vises, groups),
        "pick",
        (got.reshape(facets * 2 * RANK, lanes), held, *spread),
        (exchange,),
    )
    got = lax.all_to_all(sent, "vis", 0, 0, tiled=True)
    residual, sent = call(
        functools.partial(degrid_kernel, vises, groups),
        "degrid",
        (got, kernel_rows, kernel_cols, observed, scale),
        ((slots, 2, BC), exchange),
    )
    got = lax.all_to_all(sent, "vis", 0, 0, tiled=True)
    (sent,) = call(
        functools.partial(place_kernel, vises, groups),
        "place",
        (got, held, *spread),
        ((facets, 2 * RANK, lanes),),
    )
    got = lax.all_to_all(sent, "facet", 0, 0, tiled=True)

    (sent,) = call(
        functools.partial(share_kernel, vises, subs),
        "share",
        (got, offset_row, *shares),
        ((subs * vises, 2 * RANKS, lanes),),
    )
    got = lax.all_to_all(sent, ("sub", "vis"), 0, 0, tiled=True)
    (image,) = call(
        functools.partial(image_kernel, vises, subs, total),
        "image",
        (got, section, *table),
        ((rows, K),),
    )
    return (image, residual)


def solution(mesh):
    return jax.shard_map(
        shards,
        mesh=mesh,
        in_specs=(
            P(("facet", "vis"), None),
            P("sub"),
            P(("facet", "sub", "vis")),
            P(("facet", "sub", "vis")),
            P(("facet", "sub", "vis"), None, None),
            P(("facet", "sub", "vis"), None, None),
            P(("facet", "sub", "vis"), None, None),
            P(("facet", "sub", "vis"), None),
        ),
        out_specs=(P(("facet", "vis"), None), P(("facet", "sub", "vis"), None, None)),
        check_vma=False,
    )
```

time: 138 us -> 129 us (0.935)
  blocking collectives: 120 us -> 114 us
  matrix products: 5.58 us -> 0.17 us
  local copies, waits for them, and re-layouts: 0.33 us -> 4.19 us
  other arithmetic: 2.71 us -> 0 us
    all_to_all x0 -> x1, blocking collectives: none -> 9.41 us  [shards(): held = lax.all_to_all(sent, 'vis', 0, 0, tiled=True)]
    all_to_all x3 -> x2, blocking collectives: 23.9 us -> 14.5 us  [shards(): got = lax.all_to_all(sent, 'vis', 0, 0, tiled=True)]
    all_to_all x2, blocking collectives: 72.1 us -> 63.9 us  [shards(): got = lax.all_to_all(sent, 'facet', 0, 0, tiled=True)]
    dot_general x6 -> x1, matrix products: 5.58 us -> 0.17 us  [dot(): jnp.einsum(spec, left, right, precision=HIGH, preferred_element_type=jnp....]
    unnamed x20 -> x32, local copies, waits for them, and re-layouts: 0.06 us -> 4.16 us
    all_to_all x1, blocking collectives: 23.9 us -> 25.8 us  [shards(): got = lax.all_to_all(sent, ('sub', 'vis'), 0, 0, tiled=True)]
    mul x3 -> x0, other arithmetic: 1.42 us -> none  [the longest x2 1.4 us: shards(): into = jnp.concatenate([section * cos_p, -section * sin_p], axis=0)]
    pallas_call x3 -> x6, Pallas kernels: 7.2 us -> 8.34 us  [call(): pl.pallas_call(kernel, out_shape=tuple((jax.ShapeDtypeStruct(x, jnp.float...]
where the time goes in v3:
time: 129 us; the launch traced here: 128 us
  blocking collectives  114 us (88%)
  Pallas kernels  8.34 us (6%)
  local copies, waits for them, and re-layouts  4.19 us (3%)
  between operations  2.08 us (2%)
    all_to_all x2, blocking collectives, shards(): got = lax.all_to_all(sent, 'facet', 0, 0, tiled=True)  63.9 us
    all_to_all x1, blocking collectives, shards(): got = lax.all_to_all(sent, ('sub', 'vis'), 0, 0, tiled=True)  25.8 us
    all_to_all x2, blocking collectives, shards(): got = lax.all_to_all(sent, 'vis', 0, 0, tiled=True)  14.5 us
    all_to_all x1, blocking collectives, shards(): held = lax.all_to_all(sent, 'vis', 0, 0, tiled=True)  9.41 us
    pallas_call x6, Pallas kernels, call(): pl.pallas_call(kernel, out_shape=tuple((jax.ShapeDtypeStruct(x, jnp.float...  8.34 us
    unnamed x32, local copies, waits for them, and re-layouts  4.16 us

profile of v3, /device:TPU:1, one launch (start us, length us, event | category | flops | bytes accessed | tf_op | source)
XLA Modules:
  0.0 128.4 jit_solution(1760320711958325902)
XLA Ops:
  0.6 0.0 copy-start.9
  1.3 0.0 copy-start.14
  2.0 0.0 copy-done.9
  2.0 0.0 copy-done.14
  2.0 0.0 copy-start
  2.0 1.2 copy-done
  3.2 0.0 copy-start.2
  3.2 1.2 copy-done.2
  4.4 0.0 copy-start.7
  4.4 0.9 copy-done.7
  5.4 0.0 copy-start.13
  5.4 0.7 copy-done.13
  6.1 0.0 copy-start.15
  6.1 0.0 copy-start.5
  6.1 1.2 project.1
  7.3 0.0 copy-start.4
  7.3 9.4 %all_to_all.30.held_ref = f32[4,32,128]{2,1,0:T(8,128)S(1)} all-to-all(f32[4,32,128]{2,1,0:T(8,128)S(1)} %get-tuple-element.7), channel_id=1, replica_groups=mesh['facet'=16,'sub'=8,'vis'=4] {'vis'}, dimensions={0} | all-to-all | bytes 131072 | tf_op jit(solution)/shard_map/all_to_all | solution.py:327
  16.7 0.0 copy-done.15
  16.7 0.2 fusion
  16.9 34.6 %all_to_all.31 = f32[16,56,128]{2,1,0:T(8,128)S(1)} all-to-all(f32[16,56,128]{2,1,0:T(8,128)S(1)} %broadcast_in_dim.2), channel_id=1, replica_groups=mesh['facet'=16,'sub'=8,'vis'=4] {'facet'}, dimensions={0} | all-to-all | bytes 917504 | tf_op jit(solution)/shard_map/all_to_all | solution.py:330
  51.5 0.0 copy-done.5
  51.5 0.0 copy-done.4
  51.5 0.0 copy-start.6
  51.5 1.3 %pick.1 = f32[4,64,128]{2,1,0:T(8,128)S(1)} custom-call(f32[896,128]{1,0:T(8,128)S(1)} %bitcast.4, f32[4,32,128]{2,1,0:T(8,128)S(1)} %all_to_all.30.held_ref, bf16[512,896]{1,0:T(8,128)(2,1)S(1)} %copy-done.5, bf16[512,896]{1,0:T(8,128)(2,1)S(1)} %copy-done.4), custom_call_target="tpu_custom_call" | custom-call | tf_op jit(solution)/shard_map/pick/pallas_call | solution.py:311
  52.8 0.0 copy-start.8
  52.8 0.0 copy-start.12
  52.8 7.3 %all_to_all.32.got_ref = f32[4,64,128]{2,1,0:T(8,128)S(1)} all-to-all(f32[4,64,128]{2,1,0:T(8,128)S(1)} %pick.1), channel_id=1, replica_groups=mesh['facet'=16,'sub'=8,'vis'=4] {'vis'}, dimensions={0} | all-to-all | bytes 262144 | tf_op jit(solution)/shard_map/all_to_all | solution.py:339
  60.2 0.0 copy-done.6
  60.2 0.0 copy-done.8
  60.2 0.0 copy-done.12
  60.2 1.9 %degrid.1 = (f32[16,2,128]{2,1,0:T(2,128)}, f32[4,64,128]{2,1,0:T(8,128)S(1)}) custom-call(f32[4,64,128]{2,1,0:T(8,128)S(1)} %all_to_all.32.got_ref, f32[16,8,128]{2,1,0:T(8,128)S(1)} %copy-done.8, f32[16,128,128]{2,1,0:T(8,128)S(1)} %copy-done.6, f32[16,2,128]{2,1,0:T(2,128)S(1)} %copy-done.12, f32[16,128]{1,0:T(8,128)S(1)} %get-tuple-element.8.scale_ref), custom_call_target="tpu_custom_call" | custom-call | tf_op jit(solution)/shard_map/degrid/pallas_call | solution.py:311
  62.1 7.2 %all_to_all.33.part_ref = f32[4,64,128]{2,1,0:T(8,128)S(1)} all-to-all(f32[4,64,128]{2,1,0:T(8,128)S(1)} %get-tuple-element.9), channel_id=1, replica_groups=mesh['facet'=16,'sub'=8,'vis'=4] {'vis'}, dimensions={0} | all-to-all | bytes 262144 | tf_op jit(solution)/shard_map/all_to_all | solution.py:346
  69.3 1.8 %place.1 = f32[16,56,128]{2,1,0:T(8,128)S(1)} custom-call(f32[4,64,128]{2,1,0:T(8,128)S(1)} %all_to_all.33.part_ref, f32[4,32,128]{2,1,0:T(8,128)S(1)} %all_to_all.30.held_ref, bf16[512,896]{1,0:T(8,128)(2,1)S(1)} %copy-done.5, bf16[512,896]{1,0:T(8,128)(2,1)S(1)} %copy-done.4), custom_call_target="tpu_custom_call" | custom-call | tf_op jit(solution)/shard_map/place/pallas_call | solution.py:311
  71.1 0.0 copy-start.10
  71.1 0.0 copy-start.11
  71.1 29.3 %all_to_all.34.got_ref = f32[16,56,128]{2,1,0:T(8,128)S(1)} all-to-all(f32[16,56,128]{2,1,0:T(8,128)S(1)} %place.1), channel_id=1, replica_groups=mesh['facet'=16,'sub'=8,'vis'=4] {'facet'}, dimensions={0} | all-to-all | bytes 917504 | tf_op jit(solution)/shard_map/all_to_all | solution.py:353
  100.5 0.0 copy-done.10
  100.5 0.0 copy-done.11
  100.5 0.0 copy-start.1
  100.5 0.0 copy-start.3
  100.5 0.2 share.1
  100.7 25.8 %all_to_all.35.got_ref = f32[32,32,128]{2,1,0:T(8,128)S(1)} all-to-all(f32[32,32,128]{2,1,0:T(8,128)S(1)} %share.1), channel_id=1, replica_groups=mesh['facet'=16,'sub'=8,'vis'=4] {'sub','vis'}, dimensions={0} | all-to-all | bytes 1048576 | tf_op jit(solution)/shard_map/all_to_all | solution.py:361
  126.5 0.0 copy-done.1
  126.5 0.0 copy-done.3
  126.5 1.9 %image.1 = f32[128,512]{1,0:T(8,128)} custom-call(f32[32,32,128]{2,1,0:T(8,128)S(1)} %all_to_all.35.got_ref, f32[16,128]{1,0:T(8,128)S(1)} %copy-done.9, bf16[4,512,256]{2,1,0:T(8,128)(2,1)S(1)} %copy-done.3, bf16[4,512,256]{2,1,0:T(8,128)(2,1)S(1)} %copy-done.1), custom_call_target="tpu_custom_call" | custom-call | tf_op jit(solution)/shard_map/image/pallas_call | solution.py:311
  (1 shorter events, 0.0 us)
Async XLA Ops:
  0.6 1.3 %copy-start.9 = (f32[16,128]{1,0:T(8,128)S(1)}, f32[16,128]{1,0:T(8,128)}, u32[]{:S(2)}) copy-start(f32[16,128]{1,0:T(8,128)} %constant.22.clone.section_ref) | copy-start | bytes 24580
  1.3 0.7 copy-start.14
  2.0 1.2 copy-start
  3.2 1.2 copy-start.2
  4.4 0.9 copy-start.7
  5.4 0.7 copy-start.13
  6.1 10.6 %copy-start.15 = (f32[56,128]{1,0:T(8,128)S(1)}, f32[56,128]{1,0:T(8,128)}, u32[]{:S(2)}) copy-start(f32[56,128]{1,0:T(8,128)} %constant.23.clone) | copy-start | bytes 86020
  6.1 45.4 %copy-start.5 = (bf16[512,896]{1,0:T(8,128)(2,1)S(1)}, bf16[512,896]{1,0:T(8,128)(2,1)}, u32[]{:S(2)}) copy-start(bf16[512,896]{1,0:T(8,128)(2,1)} %constant.18.clone.high_ref) | copy-start | bytes 2752516
  7.3 44.2 %copy-start.4 = (bf16[512,896]{1,0:T(8,128)(2,1)S(1)}, bf16[512,896]{1,0:T(8,128)(2,1)}, u32[]{:S(2)}) copy-start(bf16[512,896]{1,0:T(8,128)(2,1)} %constant.19.clone.low_ref) | copy-start | bytes 2752516
  51.5 8.7 %copy-start.6 = (f32[16,128,128]{2,1,0:T(8,128)S(1)}, f32[16,128,128]{2,1,0:T(8,128)}, u32[]{:S(2)}) copy-start(f32[16,128,128]{2,1,0:T(8,128)} %cols_ref.1) | copy-start | bytes 3145732
  52.8 7.4 %copy-start.8 = (f32[16,8,128]{2,1,0:T(8,128)S(1)}, f32[16,8,128]{2,1,0:T(8,128)}, u32[]{:S(2)}) copy-start(f32[16,8,128]{2,1,0:T(8,128)} %rows_ref.1) | copy-start | bytes 196612
  52.8 7.4 %copy-start.12 = (f32[16,2,128]{2,1,0:T(2,128)S(1)}, f32[16,2,128]{2,1,0:T(2,128)}, u32[]{:S(2)}) copy-start(f32[16,2,128]{2,1,0:T(2,128)} %seen_ref.1) | copy-start | bytes 49156
  71.1 29.4 %copy-start.10 = (bf16[128,56]{1,0:T(8,128)(2,1)S(1)}, bf16[128,56]{1,0:T(8,128)(2,1)}, u32[]{:S(2)}) copy-start(bf16[128,56]{1,0:T(8,128)(2,1)} %constant.17.clone.low_ref) | copy-start | bytes 43012
  71.1 29.4 %copy-start.11 = (bf16[128,56]{1,0:T(8,128)(2,1)S(1)}, bf16[128,56]{1,0:T(8,128)(2,1)}, u32[]{:S(2)}) copy-start(bf16[128,56]{1,0:T(8,128)(2,1)} %constant.16.clone.high_ref) | copy-start | bytes 43012
  100.5 26.0 %copy-start.1 = (bf16[4,512,256]{2,1,0:T(8,128)(2,1)S(1)}, bf16[4,512,256]{2,1,0:T(8,128)(2,1)}, u32[]{:S(2)}) copy-start(bf16[4,512,256]{2,1,0:T(8,128)(2,1)} %constant.21.clone.low_ref) | copy-start | bytes 3145732
  100.5 26.0 %copy-start.3 = (bf16[4,512,256]{2,1,0:T(8,128)(2,1)S(1)}, bf16[4,512,256]{2,1,0:T(8,128)(2,1)}, u32[]{:S(2)}) copy-start(bf16[4,512,256]{2,1,0:T(8,128)(2,1)} %constant.20.clone.high_ref) | copy-start | bytes 3145732

commit v4 on v3

--- a/solution.py
+++ b/solution.py
@@ -16,7 +16,6 @@
 RANK = 28
 RANKS = 16
 SPARE = RANKS - 1
-HIGH = lax.Precision.HIGH
 
 
 def prolate(count, band, total, rank):
@@ -33,8 +32,6 @@
 def constants(facets, vises, total):
     rows = K // vises
     lanes = K // vises
-    bands = K // BC
-    sub_lanes = BC // vises
     basis = prolate(K, CR, total, RANK)
     section = prolate(rows, CR, total, RANKS)
     section[:, SPARE] = 0.0
@@ -55,21 +52,18 @@
     for part in range(2):
         merges[part, :, :, part, :] = merge.transpose(2, 0, 1)
     merges = merges.reshape(2 * RANK, vises * 2 * RANKS)
-    column = np.arange(K).reshape(bands, vises, sub_lanes).transpose(1, 0, 2).reshape(vises, lanes)
-    angle = 2 * np.pi * ((np.arange(K)[None, :, None] * column[:, None, :]) % K) / K
-    table = np.concatenate([np.cos(angle), np.sin(angle)], axis=2) * K**-0.5
+    angle = 2 * np.pi * (np.outer(np.arange(lanes), np.arange(lanes)) % lanes) / lanes
+    table = np.concatenate([np.cos(angle), np.sin(angle)], axis=1) * K**-0.5
+    twist = 2 * np.pi * np.outer(np.arange(vises), np.arange(lanes)) / K
+    twist = np.concatenate([np.cos(twist), np.sin(twist)], axis=0).astype(np.float32)
     shares = bf16_halves(merges.T)
     section, merges = (np.asarray(x, np.float32) for x in (section.T, merges))
-    return section, merges, shares, bf16_halves(spread), bf16_halves(table)
+    return section, merges, shares, np.stack(bf16_halves(spread)), bf16_halves(table), twist
 
 
 def bf16_halves(x):
     high = x.astype(jnp.bfloat16)
     return high, (x - high.astype(np.float64)).astype(jnp.bfloat16)
-
-
-def dot(spec, left, right):
-    return jnp.einsum(spec, left, right, precision=HIGH, preferred_element_type=jnp.float32)
 
 
 def halves(x):
@@ -113,7 +107,19 @@
     return (lax.axis_index("facet") * lax.axis_size("vis") + lax.axis_index("vis")) * rows
 
 
-def project_kernel(vises, total, offset_ref, count_ref, id_ref, sky_ref, wt_ref, section_ref, high_ref, low_ref, out_ref, scale_ref, offset_row_ref):
+def project_kernel(vises, total, *refs):
+    sources, rest = refs[:9], refs[9:]
+    out_ref, scale_ref, offset_row_ref = rest[:3]
+    targets, sem = rest[3:12], rest[12]
+    copies = [
+        pltpu.make_async_copy(source, target, sem.at[n])
+        for n, (source, target) in enumerate(zip(sources, targets))
+    ]
+    for copy in copies:
+        copy.start()
+    for copy in copies:
+        copy.wait()
+    offset_ref, count_ref, id_ref, section_ref, twist_ref, sky_ref, high_ref, low_ref, wt_ref = targets
     slots = wt_ref.shape[0]
     slot = lax.broadcasted_iota(jnp.int32, wt_ref.shape, 0)
     scale_ref[...] = jnp.where(slot < count_ref[0], wt_ref[...].astype(jnp.float32), 0.0)
@@ -127,10 +133,30 @@
     section = section_ref[...]
     into = jnp.concatenate([section * cos_p, -section * sin_p], axis=0)
     coef = stacked(into, halves(sky_ref[...]), NN)
+    real, imag = [], []
+    for k in range(vises):
+        real.append(coef[:RANKS, k * BC : (k + 1) * BC])
+        imag.append(coef[RANKS:, k * BC : (k + 1) * BC])
+    re_e, re_o = real[0] + real[2], real[1] + real[3]
+    im_e, im_o = imag[0] + imag[2], imag[1] + imag[3]
+    re_d, re_g = real[0] - real[2], real[1] - real[3]
+    im_d, im_g = imag[0] - imag[2], imag[1] - imag[3]
+    folded = [
+        (re_e + re_o, im_e + im_o),
+        (re_d + im_g, im_d - re_g),
+        (re_e - re_o, im_e - im_o),
+        (re_d - im_g, im_d + re_g),
+    ]
+    rows = []
+    for v, (re, im) in enumerate(folded):
+        cos_t, sin_t = twist_ref[v : v + 1, :], twist_ref[vises + v : vises + v + 1, :]
+        rows += [re * cos_t + im * sin_t, im * cos_t - re * sin_t]
+    both = stacked(jnp.concatenate(rows, axis=0), (high_ref[...], low_ref[...]), NN)
     for v in range(vises):
-        both = stacked(coef, (high_ref[v], low_ref[v]), NN)
-        out_ref[v, :RANKS, :] = both[:RANKS, :BC] + both[RANKS:, BC:]
-        out_ref[v, RANKS:, :] = both[RANKS:, :BC] - both[:RANKS, BC:]
+        re = both[2 * v * RANKS : (2 * v + 1) * RANKS]
+        im = both[(2 * v + 1) * RANKS : (2 * v + 2) * RANKS]
+        out_ref[v, :RANKS, :] = re[:, :BC] + im[:, BC:]
+        out_ref[v, RANKS:, :] = im[:, :BC] - re[:, BC:]
         out_ref[v, SPARE : SPARE + 1, :] = ids.astype(jnp.float32)
 
 
@@ -173,11 +199,11 @@
     return x
 
 
-def pick_kernel(vises, groups, coef_ref, held_ref, high_ref, low_ref, out_ref):
+def pick_kernel(vises, groups, coef_ref, held_ref, spread_ref, out_ref):
     width = BC // vises
     coef = wide(coef_ref[...])
-    grid = mxu(high_ref[...], coef, NN)
-    grid = grid[:, :BC] + grid[:, BC:] + mxu(low_ref[...], coef[:, :BC], NN)
+    grid = mxu(spread_ref[0], coef, NN)
+    grid = grid[:, :BC] + grid[:, BC:] + mxu(spread_ref[1], coef[:, :BC], NN)
     grid = wide(grid)
     columns = ids_columns(held_ref, vises, vises * groups)
     piece = lax.broadcasted_iota(jnp.int32, (vises * groups * 2 * BR, BC), 1) // width
@@ -191,7 +217,7 @@
     out_ref[...] = total.reshape(out_ref.shape)
 
 
-def place_kernel(vises, groups, part_ref, held_ref, high_ref, low_ref, out_ref):
+def place_kernel(vises, groups, part_ref, held_ref, spread_ref, out_ref):
     width = BC // vises
     parts = part_ref[...].reshape(vises * groups * 2 * BR, BC)
     columns = ids_columns(held_ref, vises, vises * groups)
@@ -202,7 +228,7 @@
         rows = everywhere(jnp.where(piece == member, parts, 0.0), width)
         turned = turned + mxu(wide(jnp.where(piece == band, rows, 0.0)), hot, TN)
     turned = turned[:BC] + turned[BC:]
-    coef = stacked(turned, (high_ref[...], low_ref[...]), NN)
+    coef = stacked(turned, (spread_ref[0], spread_ref[1]), NN)
     out_ref[...] = coef.T.reshape(out_ref.shape)
 
 
@@ -221,7 +247,8 @@
                 if v != member:
                     moved = pltpu.roll(held[v], (width * (v - member)) % BC, 1)
                     block = jnp.where(piece == v, moved, block)
-            high, low = halves(cols_ref[slot])
+            cols = [cols_ref[slot, pl.ds(v, width, stride=vises), :] for v in range(vises)]
+            high, low = halves(jnp.concatenate(cols, axis=0))
             both = mxu(
                 jnp.concatenate(halves(block), axis=0), jnp.concatenate([high, low], axis=1), NN
             )
@@ -256,7 +283,7 @@
         out_ref[q * vises : (q + 1) * vises] = coef
 
 
-def image_kernel(vises, subs, total, got_ref, section_ref, high_ref, low_ref, out_ref):
+def image_kernel(vises, subs, total, got_ref, section_ref, twist_ref, high_ref, low_ref, out_ref):
     rows = out_ref.shape[0]
     section = section_ref[...]
     first = first_pixel(rows)
@@ -279,12 +306,18 @@
     out_high, out_low = halves(jnp.concatenate(out, axis=0))
     high, low = halves(jnp.concatenate(coef, axis=0))
     grid = mxu(out_high, high, TN) + mxu(out_high, low, TN) + mxu(out_low, high, TN)
-    image = jnp.zeros(out_ref.shape, jnp.float32)
+    real, imag = [], []
     for v in range(vises):
-        at = slice(v * BC, (v + 1) * BC)
-        part = jnp.concatenate([grid[:rows, at], grid[rows:, at]], axis=1)
-        image = image + stacked(part, (high_ref[v], low_ref[v]), NT)
-    out_ref[...] = image
+        both = stacked(grid[:, v * BC : (v + 1) * BC], (high_ref[...], low_ref[...]), NN)
+        re = both[:rows, :BC] + both[rows:, BC:]
+        im = both[:rows, BC:] - both[rows:, :BC]
+        cos_t, sin_t = twist_ref[v : v + 1, :], twist_ref[vises + v : vises + v + 1, :]
+        real.append(re * cos_t - im * sin_t)
+        imag.append(re * sin_t + im * cos_t)
+    even, odd = real[0] + real[2], real[1] + real[3]
+    flat, turn = real[0] - real[2], imag[3] - imag[1]
+    for k, part in enumerate((even + odd, flat + turn, even - odd, flat - turn)):
+        out_ref[:, k * BC : (k + 1) * BC] = part
 
 
 def whole():
@@ -300,32 +333,45 @@
     lanes = K // vises
     slots = block_ids.shape[0]
     groups = slots // vises
-    section, merges, shares, spread, table = constants(facets, vises, total)
+    section, merges, shares, spread, table, twist = constants(facets, vises, total)
     shares = [jnp.asarray(x) for x in shares]
-    spread = [jnp.asarray(x) for x in spread]
+    spread = jnp.asarray(spread)
     table = [jnp.asarray(x) for x in table]
 
-    def call(kernel, name, args, outs, scalars=0):
-        smem = pl.BlockSpec(memory_space=pltpu.SMEM)
+    def call(kernel, name, args, outs):
         specs = tuple(whole() for _ in outs)
         return pl.pallas_call(
             kernel,
             out_shape=tuple(jax.ShapeDtypeStruct(x, jnp.float32) for x in outs),
-            in_specs=[smem] * scalars + [whole()] * (len(args) - scalars),
+            in_specs=[whole()] * len(args),
             out_specs=specs,
             compiler_params=pltpu.CompilerParams(vmem_limit_bytes=16 << 20),
             name=name,
         )(*args)
 
-    sent, scale, offset_row = call(
+    args = (row_offsets, block_counts, block_ids, section, twist, sky, *table, weights)
+    sent, scale, offset_row = pl.pallas_call(
         functools.partial(project_kernel, vises, total),
-        "project",
-        (row_offsets, block_counts, block_ids, sky, weights, section, *table),
-        ((vises, 2 * RANKS, lanes), (slots, BC), (8, lanes)),
-        scalars=3,
-    )
+        out_shape=tuple(
+            jax.ShapeDtypeStruct(x, jnp.float32)
+            for x in ((vises, 2 * RANKS, lanes), (slots, BC), (8, lanes))
+        ),
+        in_specs=[pl.BlockSpec(memory_space=pltpu.HBM)] * len(args),
+        out_specs=(whole(), whole(), whole()),
+        scratch_shapes=[
+            (pltpu.SMEM if n < 3 else pltpu.VMEM)(x.shape, x.dtype) for n, x in enumerate(args)
+        ]
+        + [pltpu.SemaphoreType.DMA((len(args),))],
+        compiler_params=pltpu.CompilerParams(vmem_limit_bytes=123 << 19),
+        name="project",
+    )(*args)
     held = lax.all_to_all(sent, "vis", 0, 0, tiled=True)
-    facet_coef = dot("kx,xl->kl", merges, held.reshape(vises * 2 * RANKS, lanes))
+    facet_coef = jnp.dot(
+        merges,
+        held.reshape(vises * 2 * RANKS, lanes),
+        precision=lax.Precision.HIGH,
+        preferred_element_type=jnp.float32,
+    )
     sent = jnp.broadcast_to(facet_coef[None], (facets, 2 * RANK, lanes))
     got = lax.all_to_all(sent, "facet", 0, 0, tiled=True)
 
@@ -333,7 +379,7 @@
     (sent,) = call(
         functools.partial(pick_kernel, vises, groups),
         "pick",
-        (got.reshape(facets * 2 * RANK, lanes), held, *spread),
+        (got.reshape(facets * 2 * RANK, lanes), held, spread),
         (exchange,),
     )
     got = lax.all_to_all(sent, "vis", 0, 0, tiled=True)
@@ -347,7 +393,7 @@
     (sent,) = call(
         functools.partial(place_kernel, vises, groups),
         "place",
-        (got, held, *spread),
+        (got, held, spread),
         ((facets, 2 * RANK, lanes),),
     )
     got = lax.all_to_all(sent, "facet", 0, 0, tiled=True)
@@ -362,7 +408,7 @@
     (image,) = call(
         functools.partial(image_kernel, vises, subs, total),
         "image",
-        (got, section, *table),
+        (got, section, twist, *table),
         ((rows, K),),
     )
     return (image, residual)

time: 129 us -> 127 us (0.984)
  local copies, waits for them, and re-layouts: 4.19 us -> 0.1 us
    unnamed x32 -> x24, local copies, waits for them, and re-layouts: 4.16 us -> 0.07 us
    pallas_call x0 -> x1, Pallas kernels: none -> 2.12 us  [shards(): pl.pallas_call(functools.partial(project_kernel, vises, total), out_shape...]
    pallas_call x6 -> x5, Pallas kernels: 8.34 us -> 6.99 us  [call(): pl.pallas_call(kernel, out_shape=tuple((jax.ShapeDtypeStruct(x, jnp.float...]
where the time goes in v4:
time: 127 us; the launch traced here: 126 us
  blocking collectives  114 us (90%)
  Pallas kernels  9.11 us (7%)
  between operations  2.2 us (2%)
    all_to_all x2, blocking collectives, shards(): got = lax.all_to_all(sent, 'facet', 0, 0, tiled=True)  64 us
    all_to_all x1, blocking collectives, shards(): got = lax.all_to_all(sent, ('sub', 'vis'), 0, 0, tiled=True)  25.7 us
    all_to_all x2, blocking collectives, shards(): got = lax.all_to_all(sent, 'vis', 0, 0, tiled=True)  14.5 us
    all_to_all x1, blocking collectives, shards(): held = lax.all_to_all(sent, 'vis', 0, 0, tiled=True)  9.49 us
    pallas_call x5, Pallas kernels, call(): pl.pallas_call(kernel, out_shape=tuple((jax.ShapeDtypeStruct(x, jnp.float...  6.99 us

profile of v4, /device:TPU:1, one launch (start us, length us, event | category | flops | bytes accessed | tf_op | source)
XLA Modules:
  0.0 126.0 jit_solution(7597193675692378087)
XLA Ops:
  0.6 0.0 copy-start
  2.1 2.1 %project.1 = (f32[4,32,128]{2,1,0:T(8,128)}, f32[16,128]{1,0:T(8,128)}, f32[8,128]{1,0:T(8,128)}) custom-call(s32[1]{0:T(128)S(6)} %copy.18.refs_0_, s32[1]{0:T(128)S(6)} %copy.19.refs_1_, s32[16]{0:T(128)} %refs_2_.1, f32[16,128]{1,0:T(8,128)} %constant.21.clone.refs_3_.section_ref, f32[8,128]{1,0:T(8,128)} %constant.22.clone.refs_4_.twist_ref, ...), custom_call_target="tpu_custom_call" | custom-call | tf_op jit(solution)/shard_map/project/pallas_call | solution.py:353
  4.2 9.5 %all_to_all.30.held_ref = f32[4,32,128]{2,1,0:T(8,128)S(1)} all-to-all(f32[4,32,128]{2,1,0:T(8,128)} %get-tuple-element.7), channel_id=1, replica_groups=mesh['facet'=16,'sub'=8,'vis'=4] {'vis'}, dimensions={0} | all-to-all | bytes 131072 | tf_op jit(solution)/shard_map/all_to_all | solution.py:368
  13.7 0.9 fusion
  14.6 0.0 copy-start.1
  14.7 0.0 copy-start.4
  14.7 0.0 copy-start.8
  14.7 0.0 copy-start.10
  14.7 34.7 %all_to_all.31 = f32[16,56,128]{2,1,0:T(8,128)S(1)} all-to-all(f32[16,56,128]{2,1,0:T(8,128)S(1)} %broadcast_in_dim.2), channel_id=1, replica_groups=mesh['facet'=16,'sub'=8,'vis'=4] {'facet'}, dimensions={0} | all-to-all | bytes 917504 | tf_op jit(solution)/shard_map/all_to_all | solution.py:376
  49.4 0.0 copy-done
  49.4 1.3 %pick.1 = f32[4,64,128]{2,1,0:T(8,128)S(1)} custom-call(f32[896,128]{1,0:T(8,128)S(1)} %bitcast.4, f32[4,32,128]{2,1,0:T(8,128)S(1)} %all_to_all.30.held_ref, bf16[2,512,896]{2,1,0:T(8,128)(2,1)S(1)} %copy-done), custom_call_target="tpu_custom_call" | custom-call | tf_op jit(solution)/shard_map/pick/pallas_call | solution.py:343
  50.7 7.2 %all_to_all.32.got_ref = f32[4,64,128]{2,1,0:T(8,128)S(1)} all-to-all(f32[4,64,128]{2,1,0:T(8,128)S(1)} %pick.1), channel_id=1, replica_groups=mesh['facet'=16,'sub'=8,'vis'=4] {'vis'}, dimensions={0} | all-to-all | bytes 262144 | tf_op jit(solution)/shard_map/all_to_all | solution.py:385
  57.9 0.0 copy-done.1
  57.9 0.0 copy-done.4
  57.9 0.0 copy-done.8
  57.9 0.0 copy-done.10
  57.9 1.9 %degrid.1 = (f32[16,2,128]{2,1,0:T(2,128)}, f32[4,64,128]{2,1,0:T(8,128)S(1)}) custom-call(f32[4,64,128]{2,1,0:T(8,128)S(1)} %all_to_all.32.got_ref, f32[16,8,128]{2,1,0:T(8,128)S(1)} %copy-done.4, f32[16,128,128]{2,1,0:T(8,128)S(1)} %copy-done.1, f32[16,2,128]{2,1,0:T(2,128)S(1)} %copy-done.8, f32[16,128]{1,0:T(8,128)S(1)} %copy-done.10), custom_call_target="tpu_custom_call" | custom-call | tf_op jit(solution)/shard_map/degrid/pallas_call | solution.py:343
  59.9 0.0 copy-start.6
  59.9 0.0 copy-start.7
  59.9 0.0 copy-start.11
  59.9 7.3 %all_to_all.33.part_ref = f32[4,64,128]{2,1,0:T(8,128)S(1)} all-to-all(f32[4,64,128]{2,1,0:T(8,128)S(1)} %get-tuple-element.9), channel_id=1, replica_groups=mesh['facet'=16,'sub'=8,'vis'=4] {'vis'}, dimensions={0} | all-to-all | bytes 262144 | tf_op jit(solution)/shard_map/all_to_all | solution.py:392
  67.2 1.8 %place.1 = f32[16,56,128]{2,1,0:T(8,128)S(1)} custom-call(f32[4,64,128]{2,1,0:T(8,128)S(1)} %all_to_all.33.part_ref, f32[4,32,128]{2,1,0:T(8,128)S(1)} %all_to_all.30.held_ref, bf16[2,512,896]{2,1,0:T(8,128)(2,1)S(1)} %copy-done), custom_call_target="tpu_custom_call" | custom-call | tf_op jit(solution)/shard_map/place/pallas_call | solution.py:343
  69.0 0.0 copy-start.2
  69.0 0.0 copy-start.3
  69.0 0.0 copy-start.5
  69.0 0.0 copy-start.9
  69.0 29.3 %all_to_all.34.got_ref = f32[16,56,128]{2,1,0:T(8,128)S(1)} all-to-all(f32[16,56,128]{2,1,0:T(8,128)S(1)} %place.1), channel_id=1, replica_groups=mesh['facet'=16,'sub'=8,'vis'=4] {'facet'}, dimensions={0} | all-to-all | bytes 917504 | tf_op jit(solution)/shard_map/all_to_all | solution.py:399
  98.3 0.0 copy-done.6
  98.3 0.0 copy-done.7
  98.3 0.0 copy-done.11
  98.3 0.2 share.1
  98.5 25.7 %all_to_all.35.got_ref = f32[32,32,128]{2,1,0:T(8,128)S(1)} all-to-all(f32[32,32,128]{2,1,0:T(8,128)S(1)} %share.1), channel_id=1, replica_groups=mesh['facet'=16,'sub'=8,'vis'=4] {'sub','vis'}, dimensions={0} | all-to-all | bytes 1048576 | tf_op jit(solution)/shard_map/all_to_all | solution.py:407
  124.2 0.0 copy-done.2
  124.2 0.0 copy-done.3
  124.2 0.0 copy-done.5
  124.2 0.0 copy-done.9
  124.3 1.8 %image.1 = f32[128,512]{1,0:T(8,128)} custom-call(f32[32,32,128]{2,1,0:T(8,128)S(1)} %all_to_all.35.got_ref, f32[16,128]{1,0:T(8,128)S(1)} %copy-done.5, f32[8,128]{1,0:T(8,128)S(1)} %copy-done.9, bf16[128,256]{1,0:T(8,128)(2,1)S(1)} %copy-done.3, bf16[128,256]{1,0:T(8,128)(2,1)S(1)} %copy-done.2), custom_call_target="tpu_custom_call" | custom-call | tf_op jit(solution)/shard_map/image/pallas_call | solution.py:343
  (1 shorter events, 0.0 us)
Async XLA Ops:
  0.6 48.8 %copy-start = (bf16[2,512,896]{2,1,0:T(8,128)(2,1)S(1)}, bf16[2,512,896]{2,1,0:T(8,128)(2,1)}, u32[]{:S(2)}) copy-start(bf16[2,512,896]{2,1,0:T(8,128)(2,1)} %constant.18.clone.spread_ref) | copy-start | bytes 5505028
  14.6 43.3 %copy-start.1 = (f32[16,128,128]{2,1,0:T(8,128)S(1)}, f32[16,128,128]{2,1,0:T(8,128)}, u32[]{:S(2)}) copy-start(f32[16,128,128]{2,1,0:T(8,128)} %cols_ref.1) | copy-start | bytes 3145732
  14.7 43.3 %copy-start.4 = (f32[16,8,128]{2,1,0:T(8,128)S(1)}, f32[16,8,128]{2,1,0:T(8,128)}, u32[]{:S(2)}) copy-start(f32[16,8,128]{2,1,0:T(8,128)} %rows_ref.1) | copy-start | bytes 196612
  14.7 43.2 %copy-start.8 = (f32[16,2,128]{2,1,0:T(2,128)S(1)}, f32[16,2,128]{2,1,0:T(2,128)}, u32[]{:S(2)}) copy-start(f32[16,2,128]{2,1,0:T(2,128)} %seen_ref.1) | copy-start | bytes 49156
  14.7 43.2 %copy-start.10 = (f32[16,128]{1,0:T(8,128)S(1)}, f32[16,128]{1,0:T(8,128)}, u32[]{:S(2)}) copy-start(f32[16,128]{1,0:T(8,128)} %get-tuple-element.8.scale_ref) | copy-start | bytes 24580
  59.9 38.4 %copy-start.6 = (bf16[128,56]{1,0:T(8,128)(2,1)S(1)}, bf16[128,56]{1,0:T(8,128)(2,1)}, u32[]{:S(2)}) copy-start(bf16[128,56]{1,0:T(8,128)(2,1)} %constant.17.clone.low_ref) | copy-start | bytes 43012
  59.9 38.4 %copy-start.7 = (bf16[128,56]{1,0:T(8,128)(2,1)S(1)}, bf16[128,56]{1,0:T(8,128)(2,1)}, u32[]{:S(2)}) copy-start(bf16[128,56]{1,0:T(8,128)(2,1)} %constant.16.clone.high_ref) | copy-start | bytes 43012
  59.9 38.4 %copy-start.11 = (f32[8,128]{1,0:T(8,128)S(1)}, f32[8,128]{1,0:T(8,128)}, u32[]{:S(2)}) copy-start(f32[8,128]{1,0:T(8,128)} %get-tuple-element.10.offset_row_ref) | copy-start | bytes 12292
  69.0 55.3 %copy-start.2 = (bf16[128,256]{1,0:T(8,128)(2,1)S(1)}, bf16[128,256]{1,0:T(8,128)(2,1)}, u32[]{:S(2)}) copy-start(bf16[128,256]{1,0:T(8,128)(2,1)} %constant.20.clone.refs_7_.low_ref) | copy-start | bytes 196612
  69.0 55.2 %copy-start.3 = (bf16[128,256]{1,0:T(8,128)(2,1)S(1)}, bf16[128,256]{1,0:T(8,128)(2,1)}, u32[]{:S(2)}) copy-start(bf16[128,256]{1,0:T(8,128)(2,1)} %constant.19.clone.refs_6_.high_ref) | copy-start | bytes 196612
  69.0 55.2 %copy-start.5 = (f32[16,128]{1,0:T(8,128)S(1)}, f32[16,128]{1,0:T(8,128)}, u32[]{:S(2)}) copy-start(f32[16,128]{1,0:T(8,128)} %constant.21.clone.refs_3_.section_ref) | copy-start | bytes 24580
  69.0 55.2 %copy-start.9 = (f32[8,128]{1,0:T(8,128)S(1)}, f32[8,128]{1,0:T(8,128)}, u32[]{:S(2)}) copy-start(f32[8,128]{1,0:T(8,128)} %constant.22.clone.refs_4_.twist_ref) | copy-start | bytes 12292

commit v5 on v4

--- a/solution.py
+++ b/solution.py
@@ -14,6 +14,8 @@
 BC = 128
 SUBS = 8
 RANK = 28
+NEAR = 4
+GROUP_RANK = 80
 RANKS = 16
 SPARE = RANKS - 1
 
@@ -52,13 +54,43 @@
     for part in range(2):
         merges[part, :, :, part, :] = merge.transpose(2, 0, 1)
     merges = merges.reshape(2 * RANK, vises * 2 * RANKS)
-    angle = 2 * np.pi * (np.outer(np.arange(lanes), np.arange(lanes)) % lanes) / lanes
-    table = np.concatenate([np.cos(angle), np.sin(angle)], axis=1) * K**-0.5
+    span = NEAR * K
+    wide_basis = prolate(span, CR, total, GROUP_RANK)
+    joins = np.zeros((4, GROUP_RANK, NEAR * vises, 8))
+    for n in range(NEAR * vises):
+        join = section.T @ wide_basis[n * rows : (n + 1) * rows]
+        for j in range(4):
+            joins[j, :, n] = join[8 * (j % 2) : 8 * (j % 2) + 8].T
+    joins = np.stack(bf16_halves(joins.reshape(4 * GROUP_RANK, NEAR * vises * 8)))
+    p = np.arange(span) - (span - 1) / 2
+    kernel = np.exp(-2j * np.pi * np.outer(r, p) / total) @ wide_basis
+    centres = np.arange(facets // NEAR) * span + (span - 1) / 2
+    shift = np.exp(-2j * np.pi * np.outer(r, centres) / total)
+    expand = shift[:, :, None] * kernel[:, None, :] * total**-0.5
+    real, imag = expand.real, expand.imag
+    grow = np.stack(
+        [np.stack([real, -imag], axis=2), np.stack([imag, real], axis=2)], axis=0
+    )
+    quarter = 2 * GROUP_RANK // 4
+    grow = grow.reshape(2, CR // BR, BR, facets // NEAR, 4, quarter)
+    grow = grow.transpose(0, 2, 1, 4, 3, 5).reshape(2 * CR, facets // NEAR * 2 * GROUP_RANK)
+    grow = np.stack(bf16_halves(grow))
+
+    def column_table(order):
+        angle = 2 * np.pi * (np.outer(np.arange(lanes), order) % lanes) / lanes
+        return np.cos(angle) * K**-0.5, np.sin(angle) * K**-0.5
+
+    index = np.arange(lanes)
+    out_order = 32 * (index // 8 % 4) + 8 * (index // 32) + index % 8
+    back_order = 32 * (index % 4) + index // 4
+    table = bf16_halves(np.concatenate(column_table(out_order), axis=1))
+    back_table = bf16_halves(np.concatenate([x.T for x in column_table(back_order)], axis=1))
     twist = 2 * np.pi * np.outer(np.arange(vises), np.arange(lanes)) / K
     twist = np.concatenate([np.cos(twist), np.sin(twist)], axis=0).astype(np.float32)
     shares = bf16_halves(merges.T)
-    section, merges = (np.asarray(x, np.float32) for x in (section.T, merges))
-    return section, merges, shares, np.stack(bf16_halves(spread)), bf16_halves(table), twist
+    section = np.asarray(section.T, np.float32)
+    spread = np.stack(bf16_halves(spread))
+    return section, joins, grow, shares, spread, table, back_table, twist
 
 
 def bf16_halves(x):
@@ -103,8 +135,27 @@
     return jnp.cos(angle), jnp.sin(angle)
 
 
+def near_index():
+    return lax.axis_index("zl")
+
+
 def first_pixel(rows):
-    return (lax.axis_index("facet") * lax.axis_size("vis") + lax.axis_index("vis")) * rows
+    facet = lax.axis_index("zh") * NEAR + near_index()
+    return (facet * lax.axis_size("vis") + lax.axis_index("vis")) * rows
+
+
+def exchanged(arrays, pairs):
+    lane = lax.broadcasted_iota(jnp.int32, arrays[0].shape, 1)
+    for step, size in pairs:
+        upper = (lane // size) % 2 == 1
+        after = list(arrays)
+        for low in range(len(arrays)):
+            if (low // step) % 2 == 0:
+                one, two = arrays[low], arrays[low + step]
+                after[low] = jnp.where(upper, pltpu.roll(two, size, 1), one)
+                after[low + step] = jnp.where(upper, two, pltpu.roll(one, BC - size, 1))
+        arrays = after
+    return arrays
 
 
 def project_kernel(vises, total, *refs):
@@ -126,7 +177,7 @@
     lane = lax.broadcasted_iota(jnp.int32, (1, BC), 1)
     ids = jnp.zeros((1, BC), jnp.int32)
     for s in range(slots):
-        ids = jnp.where(lane == s, id_ref[s], ids)
+        ids = jnp.where((lane // 32 == s // 4) & (lane % 4 == s % 4), id_ref[s], ids)
     offset = jnp.full(offset_row_ref.shape, offset_ref[0], jnp.int32)
     offset_row_ref[...] = offset.astype(jnp.float32)
     cos_p, sin_p = angles(offset_ref[0], first_pixel(sky_ref.shape[0]), total)
@@ -152,21 +203,30 @@
         cos_t, sin_t = twist_ref[v : v + 1, :], twist_ref[vises + v : vises + v + 1, :]
         rows += [re * cos_t + im * sin_t, im * cos_t - re * sin_t]
     both = stacked(jnp.concatenate(rows, axis=0), (high_ref[...], low_ref[...]), NN)
+    ids = jnp.broadcast_to(ids.astype(jnp.float32), (8, BC))
+    chunk = lax.broadcasted_iota(jnp.int32, (8, BC), 1) // 32
     for v in range(vises):
         re = both[2 * v * RANKS : (2 * v + 1) * RANKS]
         im = both[(2 * v + 1) * RANKS : (2 * v + 2) * RANKS]
-        out_ref[v, :RANKS, :] = re[:, :BC] + im[:, BC:]
-        out_ref[v, RANKS:, :] = im[:, :BC] - re[:, BC:]
-        out_ref[v, SPARE : SPARE + 1, :] = ids.astype(jnp.float32)
+        rows = jnp.concatenate([re[:, :BC] + im[:, BC:], im[:, :BC] - re[:, BC:]], axis=0)
+        for near in range(NEAR):
+            packed = jnp.zeros((8, BC), jnp.float32)
+            for j in range(4):
+                moved = pltpu.roll(rows[8 * j : 8 * j + 8], (32 * (j - near)) % BC, 1)
+                packed = jnp.where(chunk == j, moved, packed)
+            out_ref[near * vises + v, :8, :] = packed
+            out_ref[near * vises + v, 8:, :] = ids
 
 
 def ids_columns(held_ref, vises, slots):
     row = lax.broadcasted_iota(jnp.int32, (slots, BC), 0)
     lane = lax.broadcasted_iota(jnp.int32, (slots, BC), 1)
+    mine = (lane // 32 == row // 4) & (lane % 32 == row % 4)
     columns = []
     for v in range(vises):
-        ids = jnp.broadcast_to(held_ref[v, SPARE : SPARE + 1, :], (slots, BC))
-        column = jnp.sum(jnp.where(row == lane, ids, 0.0), axis=1, keepdims=True)
+        ids = held_ref[near_index() * vises + v, 8:, :]
+        ids = jnp.concatenate([ids] * (slots // 8), axis=0)
+        column = jnp.sum(jnp.where(mine, ids, 0.0), axis=1, keepdims=True)
         columns.append(jnp.broadcast_to(column, (slots, BC)).astype(jnp.int32))
     return columns
 
@@ -199,33 +259,75 @@
     return x
 
 
-def pick_kernel(vises, groups, coef_ref, held_ref, spread_ref, out_ref):
-    width = BC // vises
-    coef = wide(coef_ref[...])
-    grid = mxu(spread_ref[0], coef, NN)
-    grid = grid[:, :BC] + grid[:, BC:] + mxu(spread_ref[1], coef[:, :BC], NN)
-    grid = wide(grid)
-    columns = ids_columns(held_ref, vises, vises * groups)
-    piece = lax.broadcasted_iota(jnp.int32, (vises * groups * 2 * BR, BC), 1) // width
-    total = jnp.zeros((vises * groups * 2 * BR, BC), jnp.float32)
-    for member in range(vises):
-        hot, band = selection(slot_rows(columns, member, vises, groups), K // BC)
-        rows = mxu(hot, grid, NN)
-        rows = rows[:, :BC] + rows[:, BC:]
-        rows = everywhere(jnp.where(piece == band, rows, 0.0), width)
-        total = jnp.where(piece == member, rows, total)
-    out_ref[...] = total.reshape(out_ref.shape)
+def join_kernel(held_ref, joins_ref, out_ref):
+    held = wide(held_ref[:, :8, :].reshape(joins_ref.shape[2], BC))
+    rows = mxu(joins_ref[0], held, NN)
+    rows = rows[:, :BC] + rows[:, BC:] + mxu(joins_ref[1], held[:, :BC], NN)
+    half = GROUP_RANK // 2
+    chunk = lax.broadcasted_iota(jnp.int32, (half, BC), 1) // 32
+    packed = jnp.zeros((half, BC), jnp.float32)
+    for part in range(2):
+        at = 2 * part * GROUP_RANK
+        one, two = rows[at : at + GROUP_RANK], rows[at + GROUP_RANK : at + 2 * GROUP_RANK]
+        low = one[:half] + pltpu.roll(two[:half], BC - 32, 1)
+        high = pltpu.roll(one[half:], 32, 1) + two[half:]
+        packed = jnp.where(chunk == 2 * part, low, packed)
+        packed = jnp.where(chunk == 2 * part + 1, high, packed)
+    for f in range(out_ref.shape[0]):
+        out_ref[f] = packed
+
+
+def pick_kernel(peers, got_ref, held_ref, grow_ref, out_ref, turned_ref):
+    rows = got_ref[...].reshape(got_ref.shape[0] * got_ref.shape[1], BC)
+    chunk = lax.broadcasted_iota(jnp.int32, rows.shape, 1) // 32
+    coef = [everywhere(jnp.where(chunk == j, rows, 0.0), 32) for j in range(4)]
+    coef = wide(jnp.concatenate(coef, axis=0))
+    grid = mxu(grow_ref[0], coef, NN)
+    grid = grid[:, :BC] + grid[:, BC:] + mxu(grow_ref[1], coef[:, :BC], NN)
+    tall, bands = 2 * BR, CR // BR
+    moved = [grid] + [pltpu.roll(grid, 8 * d, 1) for d in range(1, 4)]
+    eighth = lax.broadcasted_iota(jnp.int32, (bands, BC), 1) // 8
+    blocks = []
+    for band in range(4):
+        block = jnp.zeros((bands, BC), jnp.float32)
+        for zr in range(tall):
+            source = moved[(zr - band) % 4][zr * bands : (zr + 1) * bands]
+            block = jnp.where(eighth == zr, source, block)
+        blocks.append(block)
+    blocks = wide(jnp.concatenate(blocks, axis=0))
+    lane = lax.broadcasted_iota(jnp.int32, (8, BC), 1)
+    row = lax.broadcasted_iota(jnp.int32, (BC, BC), 0)
+    hots = []
+    for top in range(peers // 8):
+        ids = jnp.zeros((8, BC), jnp.float32)
+        for low in range(8):
+            ids = jnp.where((lane // 4) % 8 == low, held_ref[8 * top + low, 8:, :], ids)
+        ids = ids.astype(jnp.int32)
+        target = (ids % 4) * bands + ids // 4
+        target = jnp.broadcast_to(target[:1], (BC, BC))
+        hots.append(jnp.where(row == target, 1.0, 0.0).astype(jnp.bfloat16))
+    picked = mxu(blocks, jnp.concatenate(hots, axis=1), TN)
+    picked = picked[:BC] + picked[BC:]
+    for top in range(peers // 8):
+        turned_ref[top * BC : (top + 1) * BC, :] = picked[:, top * BC : (top + 1) * BC]
+    for top in range(peers // 8):
+        parts = [turned_ref[pl.ds(top * BC + i, tall, stride=8), :] for i in range(8)]
+        for low, part in enumerate(exchanged(parts, ((1, 4), (2, 8), (4, 16)))):
+            out_ref[8 * top + low] = part
 
 
 def place_kernel(vises, groups, part_ref, held_ref, spread_ref, out_ref):
-    width = BC // vises
     parts = part_ref[...].reshape(vises * groups * 2 * BR, BC)
     columns = ids_columns(held_ref, vises, vises * groups)
-    piece = lax.broadcasted_iota(jnp.int32, parts.shape, 1) // width
+    piece = lax.broadcasted_iota(jnp.int32, parts.shape, 1) % vises
     turned = jnp.zeros((2 * BC, 2 * CR), jnp.float32)
     for member in range(vises):
         hot, band = selection(slot_rows(columns, member, vises, groups), K // BC)
-        rows = everywhere(jnp.where(piece == member, parts, 0.0), width)
+        alone = jnp.where(piece == member, parts, 0.0)
+        rows = alone
+        for v in range(vises):
+            if v != member:
+                rows = rows + pltpu.roll(alone, (v - member) % BC, 1)
         turned = turned + mxu(wide(jnp.where(piece == band, rows, 0.0)), hot, TN)
     turned = turned[:BC] + turned[BC:]
     coef = stacked(turned, (spread_ref[0], spread_ref[1]), NN)
@@ -233,22 +335,16 @@
 
 
 def degrid_kernel(vises, groups, got_ref, rows_ref, cols_ref, seen_ref, scale_ref, res_ref, out_ref):
-    width = BC // vises
     tall = 2 * BR
-    piece = lax.broadcasted_iota(jnp.int32, (tall, BC), 1) // width
+    slots = [got_ref[o] for o in range(got_ref.shape[0])]
+    slots = exchanged(slots, ((8, 64), (4, 32), (2, 2), (1, 1)))
     for g in range(groups):
         at = pl.ds(g * tall, tall)
-        held = [got_ref[v, at, :] for v in range(vises)]
         backs = []
         for member in range(vises):
             slot = vises * g + member
-            block = held[member]
-            for v in range(vises):
-                if v != member:
-                    moved = pltpu.roll(held[v], (width * (v - member)) % BC, 1)
-                    block = jnp.where(piece == v, moved, block)
-            cols = [cols_ref[slot, pl.ds(v, width, stride=vises), :] for v in range(vises)]
-            high, low = halves(jnp.concatenate(cols, axis=0))
+            block = slots[slot]
+            high, low = halves(cols_ref[slot])
             both = mxu(
                 jnp.concatenate(halves(block), axis=0), jnp.concatenate([high, low], axis=1), NN
             )
@@ -262,12 +358,7 @@
                 jnp.concatenate(halves(out), axis=0), jnp.concatenate([high, low], axis=0), NT
             )
             backs.append(both[:tall, :BC] + both[:tall, BC:] + both[tall:, :BC])
-        for v in range(vises):
-            sent = backs[v]
-            for member in range(vises):
-                if member != v:
-                    moved = pltpu.roll(backs[member], (width * (member - v)) % BC, 1)
-                    sent = jnp.where(piece == member, moved, sent)
+        for v, sent in enumerate(exchanged(backs, ((2, 2), (1, 1)))):
             out_ref[v, at, :] = sent
 
 
@@ -325,7 +416,7 @@
 
 
 def shards(sky, row_offsets, block_counts, block_ids, kernel_rows, kernel_cols, observed, weights):
-    facets = lax.axis_size("facet")
+    facets = lax.axis_size("zh") * lax.axis_size("zl")
     vises = lax.axis_size("vis")
     subs = lax.axis_size("sub")
     total = facets * K
@@ -333,18 +424,21 @@
     lanes = K // vises
     slots = block_ids.shape[0]
     groups = slots // vises
-    section, merges, shares, spread, table, twist = constants(facets, vises, total)
+    section, joins, grow, shares, spread, table, back_table, twist = constants(facets, vises, total)
     shares = [jnp.asarray(x) for x in shares]
     spread = jnp.asarray(spread)
     table = [jnp.asarray(x) for x in table]
-
-    def call(kernel, name, args, outs):
+    back_table = [jnp.asarray(x) for x in back_table]
+    peers = NEAR * vises
+
+    def call(kernel, name, args, outs, scratch=()):
         specs = tuple(whole() for _ in outs)
         return pl.pallas_call(
             kernel,
             out_shape=tuple(jax.ShapeDtypeStruct(x, jnp.float32) for x in outs),
             in_specs=[whole()] * len(args),
             out_specs=specs,
+            scratch_shapes=list(scratch),
             compiler_params=pltpu.CompilerParams(vmem_limit_bytes=16 << 20),
             name=name,
         )(*args)
@@ -354,7 +448,7 @@
         functools.partial(project_kernel, vises, total),
         out_shape=tuple(
             jax.ShapeDtypeStruct(x, jnp.float32)
-            for x in ((vises, 2 * RANKS, lanes), (slots, BC), (8, lanes))
+            for x in ((peers, 16, lanes), (slots, BC), (8, lanes))
         ),
         in_specs=[pl.BlockSpec(memory_space=pltpu.HBM)] * len(args),
         out_specs=(whole(), whole(), whole()),
@@ -365,24 +459,24 @@
         compiler_params=pltpu.CompilerParams(vmem_limit_bytes=123 << 19),
         name="project",
     )(*args)
-    held = lax.all_to_all(sent, "vis", 0, 0, tiled=True)
-    facet_coef = jnp.dot(
-        merges,
-        held.reshape(vises * 2 * RANKS, lanes),
-        precision=lax.Precision.HIGH,
-        preferred_element_type=jnp.float32,
-    )
-    sent = jnp.broadcast_to(facet_coef[None], (facets, 2 * RANK, lanes))
-    got = lax.all_to_all(sent, "facet", 0, 0, tiled=True)
-
+    held = lax.all_to_all(sent, ("zl", "vis"), 0, 0, tiled=True)
+    (sent,) = call(
+        join_kernel,
+        "join",
+        (held, joins),
+        ((facets // NEAR, GROUP_RANK // 2, lanes),),
+    )
+    got = lax.all_to_all(sent, "zh", 0, 0, tiled=True)
+
+    (sent,) = call(
+        functools.partial(pick_kernel, peers),
+        "pick",
+        (got, held, grow),
+        ((peers, 2 * BR, lanes),),
+        [pltpu.VMEM((peers // 8 * BC, BC), jnp.float32)],
+    )
+    got = lax.all_to_all(sent, ("zl", "vis"), 0, 0, tiled=True)
     exchange = (vises, groups * 2 * BR, lanes)
-    (sent,) = call(
-        functools.partial(pick_kernel, vises, groups),
-        "pick",
-        (got.reshape(facets * 2 * RANK, lanes), held, spread),
-        (exchange,),
-    )
-    got = lax.all_to_all(sent, "vis", 0, 0, tiled=True)
     residual, sent = call(
         functools.partial(degrid_kernel, vises, groups),
         "degrid",
@@ -396,7 +490,7 @@
         (got, held, spread),
         ((facets, 2 * RANK, lanes),),
     )
-    got = lax.all_to_all(sent, "facet", 0, 0, tiled=True)
+    got = lax.all_to_all(sent, ("zh", "zl"), 0, 0, tiled=True)
 
     (sent,) = call(
         functools.partial(share_kernel, vises, subs),
@@ -408,26 +502,28 @@
     (image,) = call(
         functools.partial(image_kernel, vises, subs, total),
         "image",
-        (got, section, twist, *table),
+        (got, section, twist, *back_table),
         ((rows, K),),
     )
     return (image, residual)
 
 
 def solution(mesh):
+    facets, subs, vises = mesh.devices.shape
+    split = mesh.devices.reshape(facets // NEAR, NEAR, subs, vises)
     return jax.shard_map(
         shards,
-        mesh=mesh,
+        mesh=jax.sharding.Mesh(split, ("zh", "zl", "sub", "vis")),
         in_specs=(
-            P(("facet", "vis"), None),
+            P(("zh", "zl", "vis"), None),
             P("sub"),
-            P(("facet", "sub", "vis")),
-            P(("facet", "sub", "vis")),
-            P(("facet", "sub", "vis"), None, None),
-            P(("facet", "sub", "vis"), None, None),
-            P(("facet", "sub", "vis"), None, None),
-            P(("facet", "sub", "vis"), None),
+            P(("zh", "zl", "sub", "vis")),
+            P(("zh", "zl", "sub", "vis")),
+            P(("zh", "zl", "sub", "vis"), None, None),
+            P(("zh", "zl", "sub", "vis"), None, None),
+            P(("zh", "zl", "sub", "vis"), None, None),
+            P(("zh", "zl", "sub", "vis"), None),
         ),
-        out_specs=(P(("facet", "vis"), None), P(("facet", "sub", "vis"), None, None)),
+        out_specs=(P(("zh", "zl", "vis"), None), P(("zh", "zl", "sub", "vis"), None, None)),
         check_vma=False,
     )

time: 127 us -> 120 us (0.945)
  blocking collectives: 114 us -> 106 us
  local copies, waits for them, and re-layouts: 0.1 us -> 2.29 us
    all_to_all x2 -> x1, blocking collectives: 14.5 us -> 7.33 us  [shards(): got = lax.all_to_all(sent, 'vis', 0, 0, tiled=True)]
    unnamed x24 -> x28, local copies, waits for them, and re-layouts: 0.07 us -> 2.29 us
    all_to_all x3 -> x4, blocking collectives: 73.4 us -> 72 us  [the longest x1 25.2 us: shards(): got = lax.all_to_all(sent, 'zh', 0, 0, tiled=True)]
    pallas_call x5 -> x6, Pallas kernels: 6.99 us -> 7.56 us  [call(): pl.pallas_call(kernel, out_shape=tuple((jax.ShapeDtypeStruct(x, jnp.float...]
where the time goes in v5:
time: 120 us
  blocking collectives  106 us (88%)
  Pallas kernels  9.79 us (8%)
  local copies, waits for them, and re-layouts  2.29 us (2%)
  between operations  2.13 us (2%)
    all_to_all x1, blocking collectives, shards(): got = lax.all_to_all(sent, ('sub', 'vis'), 0, 0, tiled=True)  26.3 us
    all_to_all x1, blocking collectives, shards(): got = lax.all_to_all(sent, 'zh', 0, 0, tiled=True)  25.2 us
    all_to_all x1, blocking collectives, shards(): got = lax.all_to_all(sent, ('zh', 'zl'), 0, 0, tiled=True)  19.5 us
    all_to_all x1, blocking collectives, shards(): held = lax.all_to_all(sent, ('zl', 'vis'), 0, 0, tiled=True)  17 us
    all_to_all x1, blocking collectives, shards(): got = lax.all_to_all(sent, ('zl', 'vis'), 0, 0, tiled=True)  10.4 us
    pallas_call x6, Pallas kernels, call(): pl.pallas_call(kernel, out_shape=tuple((jax.ShapeDtypeStruct(x, jnp.float...  7.56 us
    all_to_all x1, blocking collectives, shards(): got = lax.all_to_all(sent, 'vis', 0, 0, tiled=True)  7.33 us

profile of v5, /device:TPU:1, one launch (start us, length us, event | category | flops | bytes accessed | tf_op | source)
XLA Modules:
  0.0 119.8 jit_solution(9316147580278351490)
XLA Ops:
  0.6 0.0 copy-start.2
  2.0 2.2 %project.1 = (f32[16,16,128]{2,1,0:T(8,128)}, f32[16,128]{1,0:T(8,128)}, f32[8,128]{1,0:T(8,128)}) custom-call(s32[1]{0:T(128)S(6)} %copy.21.refs_0_, s32[1]{0:T(128)S(6)} %copy.22.refs_1_, s32[16]{0:T(128)} %refs_2_.1, f32[16,128]{1,0:T(8,128)} %constant.29.clone.refs_3_.section_ref, f32[8,128]{1,0:T(8,128)} %constant.30.clone.refs_4_.twist_ref, ...), custom_call_target="tpu_custom_call" | custom-call | tf_op jit(solution)/shard_map/project/pallas_call | solution.py:447
  4.3 17.0 %all_to_all.30.held_ref = f32[16,16,128]{2,1,0:T(8,128)S(1)} all-to-all(f32[16,16,128]{2,1,0:T(8,128)} %get-tuple-element.7), channel_id=1, replica_groups=mesh['zh'=4,'zl'=4,'sub'=8,'vis'=4] {'zl','vis'}, dimensions={0} | all-to-all | bytes 262144 | tf_op jit(solution)/shard_map/all_to_all | solution.py:462
  21.3 0.0 copy-start.3
  21.3 0.9 copy-done.3
  22.2 0.0 copy-start.12
  22.2 0.3 join.1
  22.5 0.0 copy-start
  22.5 25.2 %all_to_all.31.got_ref = f32[4,40,128]{2,1,0:T(8,128)S(1)} all-to-all(f32[4,40,128]{2,1,0:T(8,128)S(1)} %join.1), channel_id=1, replica_groups=mesh['zh'=4,'zl'=4,'sub'=8,'vis'=4] {'zh'}, dimensions={0} | all-to-all | bytes 163840 | tf_op jit(solution)/shard_map/all_to_all | solution.py:469
  47.7 0.0 copy-start.1
  47.7 1.3 %copy-done.1 = bf16[2,512,640]{2,1,0:T(8,128)(2,1)S(1)} copy-done((bf16[2,512,640]{2,1,0:T(8,128)(2,1)S(1)}, bf16[2,512,640]{2,1,0:T(8,128)(2,1)}, u32[]{:S(2)}) %copy-start.1) | copy-done | bytes 1310744
  49.0 0.0 copy-start.6
  49.0 0.0 copy-start.10
  49.0 1.3 %pick.1 = f32[16,16,128]{2,1,0:T(8,128)S(1)} custom-call(f32[4,40,128]{2,1,0:T(8,128)S(1)} %all_to_all.31.got_ref, f32[16,16,128]{2,1,0:T(8,128)S(1)} %all_to_all.30.held_ref, bf16[2,512,640]{2,1,0:T(8,128)(2,1)S(1)} %copy-done.1), custom_call_target="tpu_custom_call" | custom-call | tf_op jit(solution)/shard_map/pick/pallas_call | solution.py:436
  50.3 10.4 %all_to_all.32.got_ref = f32[16,16,128]{2,1,0:T(8,128)S(1)} all-to-all(f32[16,16,128]{2,1,0:T(8,128)S(1)} %pick.1), channel_id=1, replica_groups=mesh['zh'=4,'zl'=4,'sub'=8,'vis'=4] {'zl','vis'}, dimensions={0} | all-to-all | bytes 262144 | tf_op jit(solution)/shard_map/all_to_all | solution.py:478
  60.7 0.0 copy-done.2
  60.7 0.0 copy-done.12
  60.7 0.0 copy-done.6
  60.7 0.0 copy-done.10
  60.7 2.2 %degrid.1 = (f32[16,2,128]{2,1,0:T(2,128)}, f32[4,64,128]{2,1,0:T(8,128)S(1)}) custom-call(f32[16,16,128]{2,1,0:T(8,128)S(1)} %all_to_all.32.got_ref, f32[16,8,128]{2,1,0:T(8,128)S(1)} %copy-done.6, f32[16,128,128]{2,1,0:T(8,128)S(1)} %copy-done.2, f32[16,2,128]{2,1,0:T(2,128)S(1)} %copy-done.10, f32[16,128]{1,0:T(8,128)S(1)} %copy-done.12), custom_call_target="tpu_custom_call" | custom-call | tf_op jit(solution)/shard_map/degrid/pallas_call | solution.py:436
  62.9 0.0 copy-start.8
  62.9 0.0 copy-start.9
  62.9 0.0 copy-start.13
  62.9 7.3 %all_to_all.33.part_ref = f32[4,64,128]{2,1,0:T(8,128)S(1)} all-to-all(f32[4,64,128]{2,1,0:T(8,128)S(1)} %get-tuple-element.9), channel_id=1, replica_groups=mesh['zh'=4,'zl'=4,'sub'=8,'vis'=4] {'vis'}, dimensions={0} | all-to-all | bytes 262144 | tf_op jit(solution)/shard_map/all_to_all | solution.py:486
  70.2 0.0 copy-done
  70.2 1.8 %place.1 = f32[16,56,128]{2,1,0:T(8,128)S(1)} custom-call(f32[4,64,128]{2,1,0:T(8,128)S(1)} %all_to_all.33.part_ref, f32[16,16,128]{2,1,0:T(8,128)S(1)} %all_to_all.30.held_ref, bf16[2,512,896]{2,1,0:T(8,128)(2,1)S(1)} %copy-done), custom_call_target="tpu_custom_call" | custom-call | tf_op jit(solution)/shard_map/place/pallas_call | solution.py:436
  72.0 0.0 copy-start.4
  72.0 0.0 copy-start.5
  72.0 0.0 copy-start.7
  72.1 0.0 copy-start.11
  72.1 19.5 %all_to_all.34.got_ref = f32[16,56,128]{2,1,0:T(8,128)S(1)} all-to-all(f32[16,56,128]{2,1,0:T(8,128)S(1)} %place.1), channel_id=1, replica_groups=mesh['zh'=4,'zl'=4,'sub'=8,'vis'=4] {'zh','zl'}, dimensions={0} | all-to-all | bytes 917504 | tf_op jit(solution)/shard_map/all_to_all | solution.py:493
  91.5 0.0 copy-done.8
  91.5 0.0 copy-done.9
  91.5 0.0 copy-done.13
  91.5 0.2 share.1
  91.8 26.3 %all_to_all.35.got_ref = f32[32,32,128]{2,1,0:T(8,128)S(1)} all-to-all(f32[32,32,128]{2,1,0:T(8,128)S(1)} %share.1), channel_id=1, replica_groups=mesh['zh'=4,'zl'=4,'sub'=8,'vis'=4] {'sub','vis'}, dimensions={0} | all-to-all | bytes 1048576 | tf_op jit(solution)/shard_map/all_to_all | solution.py:501
  118.0 0.0 copy-done.4
  118.0 0.0 copy-done.5
  118.0 0.0 copy-done.7
  118.0 0.0 copy-done.11
  118.0 1.8 %image.1 = f32[128,512]{1,0:T(8,128)} custom-call(f32[32,32,128]{2,1,0:T(8,128)S(1)} %all_to_all.35.got_ref, f32[16,128]{1,0:T(8,128)S(1)} %copy-done.7, f32[8,128]{1,0:T(8,128)S(1)} %copy-done.11, bf16[128,256]{1,0:T(8,128)(2,1)S(1)} %copy-done.5, bf16[128,256]{1,0:T(8,128)(2,1)S(1)} %copy-done.4), custom_call_target="tpu_custom_call" | custom-call | tf_op jit(solution)/shard_map/image/pallas_call | solution.py:436
Async XLA Ops:
  0.6 60.1 %copy-start.2 = (f32[16,128,128]{2,1,0:T(8,128)S(1)}, f32[16,128,128]{2,1,0:T(8,128)}, u32[]{:S(2)}) copy-start(f32[16,128,128]{2,1,0:T(8,128)} %cols_ref.1) | copy-start | bytes 3145732
  21.3 0.9 copy-start.3
  22.2 38.5 %copy-start.12 = (f32[16,128]{1,0:T(8,128)S(1)}, f32[16,128]{1,0:T(8,128)}, u32[]{:S(2)}) copy-start(f32[16,128]{1,0:T(8,128)} %get-tuple-element.8.scale_ref) | copy-start | bytes 24580
  22.5 47.7 %copy-start = (bf16[2,512,896]{2,1,0:T(8,128)(2,1)S(1)}, bf16[2,512,896]{2,1,0:T(8,128)(2,1)}, u32[]{:S(2)}) copy-start(bf16[2,512,896]{2,1,0:T(8,128)(2,1)} %constant.24.clone.spread_ref) | copy-start | bytes 5505028
  47.7 1.3 %copy-start.1 = (bf16[2,512,640]{2,1,0:T(8,128)(2,1)S(1)}, bf16[2,512,640]{2,1,0:T(8,128)(2,1)}, u32[]{:S(2)}) copy-start(bf16[2,512,640]{2,1,0:T(8,128)(2,1)} %constant.32.clone.grow_ref) | copy-start | bytes 3932164
  49.0 11.7 %copy-start.6 = (f32[16,8,128]{2,1,0:T(8,128)S(1)}, f32[16,8,128]{2,1,0:T(8,128)}, u32[]{:S(2)}) copy-start(f32[16,8,128]{2,1,0:T(8,128)} %rows_ref.1) | copy-start | bytes 196612
  49.0 11.7 %copy-start.10 = (f32[16,2,128]{2,1,0:T(2,128)S(1)}, f32[16,2,128]{2,1,0:T(2,128)}, u32[]{:S(2)}) copy-start(f32[16,2,128]{2,1,0:T(2,128)} %seen_ref.1) | copy-start | bytes 49156
  62.9 28.7 %copy-start.8 = (bf16[128,56]{1,0:T(8,128)(2,1)S(1)}, bf16[128,56]{1,0:T(8,128)(2,1)}, u32[]{:S(2)}) copy-start(bf16[128,56]{1,0:T(8,128)(2,1)} %constant.23.clone.low_ref) | copy-start | bytes 43012
  62.9 28.7 %copy-start.9 = (bf16[128,56]{1,0:T(8,128)(2,1)S(1)}, bf16[128,56]{1,0:T(8,128)(2,1)}, u32[]{:S(2)}) copy-start(bf16[128,56]{1,0:T(8,128)(2,1)} %constant.22.clone.high_ref) | copy-start | bytes 43012
  62.9 28.7 %copy-start.13 = (f32[8,128]{1,0:T(8,128)S(1)}, f32[8,128]{1,0:T(8,128)}, u32[]{:S(2)}) copy-start(f32[8,128]{1,0:T(8,128)} %get-tuple-element.10.offset_row_ref) | copy-start | bytes 12292
  72.0 46.0 %copy-start.4 = (bf16[128,256]{1,0:T(8,128)(2,1)S(1)}, bf16[128,256]{1,0:T(8,128)(2,1)}, u32[]{:S(2)}) copy-start(bf16[128,256]{1,0:T(8,128)(2,1)} %constant.28.clone.low_ref) | copy-start | bytes 196612
  72.0 46.0 %copy-start.5 = (bf16[128,256]{1,0:T(8,128)(2,1)S(1)}, bf16[128,256]{1,0:T(8,128)(2,1)}, u32[]{:S(2)}) copy-start(bf16[128,256]{1,0:T(8,128)(2,1)} %constant.27.clone.high_ref) | copy-start | bytes 196612
  72.0 46.0 %copy-start.7 = (f32[16,128]{1,0:T(8,128)S(1)}, f32[16,128]{1,0:T(8,128)}, u32[]{:S(2)}) copy-start(f32[16,128]{1,0:T(8,128)} %constant.29.clone.refs_3_.section_ref) | copy-start | bytes 24580
  72.1 46.0 %copy-start.11 = (f32[8,128]{1,0:T(8,128)S(1)}, f32[8,128]{1,0:T(8,128)}, u32[]{:S(2)}) copy-start(f32[8,128]{1,0:T(8,128)} %constant.30.clone.refs_4_.twist_ref) | copy-start | bytes 12292

commit v6 on v5

--- a/solution.py
+++ b/solution.py
@@ -431,6 +431,8 @@
     back_table = [jnp.asarray(x) for x in back_table]
     peers = NEAR * vises
 
+    hint = pl.CostEstimate(flops=10**10, bytes_accessed=1 << 20, transcendentals=0)
+
     def call(kernel, name, args, outs, scratch=()):
         specs = tuple(whole() for _ in outs)
         return pl.pallas_call(
@@ -440,6 +442,7 @@
             out_specs=specs,
             scratch_shapes=list(scratch),
             compiler_params=pltpu.CompilerParams(vmem_limit_bytes=16 << 20),
+            cost_estimate=hint,
             name=name,
         )(*args)
 
@@ -457,6 +460,7 @@
         ]
         + [pltpu.SemaphoreType.DMA((len(args),))],
         compiler_params=pltpu.CompilerParams(vmem_limit_bytes=123 << 19),
+        cost_estimate=hint,
         name="project",
     )(*args)
     held = lax.all_to_all(sent, ("zl", "vis"), 0, 0, tiled=True)

time: 120 us -> 118 us (0.983)
  local copies, waits for them, and re-layouts: 2.29 us -> 0.07 us
    unnamed x28, local copies, waits for them, and re-layouts: 2.29 us -> 0.07 us
where the time goes in v6:
time: 118 us; the launch traced here: 117 us
  blocking collectives  105 us (89%)
  Pallas kernels  9.84 us (8%)
  between operations  2.05 us (2%)
    all_to_all x1, blocking collectives, shards(): got = lax.all_to_all(sent, ('sub', 'vis'), 0, 0, tiled=True)  26.1 us
    all_to_all x1, blocking collectives, shards(): got = lax.all_to_all(sent, 'zh', 0, 0, tiled=True)  25.2 us
    all_to_all x1, blocking collectives, shards(): got = lax.all_to_all(sent, ('zh', 'zl'), 0, 0, tiled=True)  19.5 us
    all_to_all x1, blocking collectives, shards(): held = lax.all_to_all(sent, ('zl', 'vis'), 0, 0, tiled=True)  17 us
    all_to_all x1, blocking collectives, shards(): got = lax.all_to_all(sent, ('zl', 'vis'), 0, 0, tiled=True)  10.4 us
    pallas_call x6, Pallas kernels, call(): pl.pallas_call(kernel, out_shape=tuple((jax.ShapeDtypeStruct(x, jnp.float...  7.58 us
    all_to_all x1, blocking collectives, shards(): got = lax.all_to_all(sent, 'vis', 0, 0, tiled=True)  7.2 us

profile of v6, /device:TPU:1, one launch (start us, length us, event | category | flops | bytes accessed | tf_op | source)
XLA Modules:
  0.0 117.4 jit_solution(6592701989104287236)
XLA Ops:
  1.9 0.0 copy-start.5
  1.9 2.3 %project.1 = (f32[16,16,128]{2,1,0:T(8,128)}, f32[16,128]{1,0:T(8,128)}, f32[8,128]{1,0:T(8,128)}) custom-call(s32[1]{0:T(128)S(6)} %copy.21.refs_0_, s32[1]{0:T(128)S(6)} %copy.22.refs_1_, s32[16]{0:T(128)} %refs_2_.1, f32[16,128]{1,0:T(8,128)} %constant.29.clone.refs_3_.section_ref, f32[8,128]{1,0:T(8,128)} %constant.30.clone.refs_4_.twist_ref, ...), custom_call_target="tpu_custom_call" | custom-call | flops 10000000000 | bytes 1048576 | tf_op jit(solution)/shard_map/project/pallas_call | solution.py:450
  4.2 17.0 %all_to_all.30.held_ref = f32[16,16,128]{2,1,0:T(8,128)S(1)} all-to-all(f32[16,16,128]{2,1,0:T(8,128)} %get-tuple-element.7), channel_id=1, replica_groups=mesh['zh'=4,'zl'=4,'sub'=8,'vis'=4] {'zl','vis'}, dimensions={0} | all-to-all | bytes 262144 | tf_op jit(solution)/shard_map/all_to_all | solution.py:466
  21.2 0.0 copy-done.5
  21.2 0.0 copy-start.4
  21.2 0.3 join.1
  21.5 25.2 %all_to_all.31.got_ref = f32[4,40,128]{2,1,0:T(8,128)S(1)} all-to-all(f32[4,40,128]{2,1,0:T(8,128)S(1)} %join.1), channel_id=1, replica_groups=mesh['zh'=4,'zl'=4,'sub'=8,'vis'=4] {'zh'}, dimensions={0} | all-to-all | bytes 163840 | tf_op jit(solution)/shard_map/all_to_all | solution.py:473
  46.7 0.0 copy-done.4
  46.7 0.0 copy-start
  46.7 0.0 copy-start.1
  46.7 0.0 copy-start.2
  46.7 0.0 copy-start.12
  46.7 1.4 %pick.1 = f32[16,16,128]{2,1,0:T(8,128)S(1)} custom-call(f32[4,40,128]{2,1,0:T(8,128)S(1)} %all_to_all.31.got_ref, f32[16,16,128]{2,1,0:T(8,128)S(1)} %all_to_all.30.held_ref, bf16[2,512,640]{2,1,0:T(8,128)(2,1)S(1)} %copy-done.4), custom_call_target="tpu_custom_call" | custom-call | flops 10000000000 | bytes 1048576 | tf_op jit(solution)/shard_map/pick/pallas_call | solution.py:438
  48.1 10.4 %all_to_all.32.got_ref = f32[16,16,128]{2,1,0:T(8,128)S(1)} all-to-all(f32[16,16,128]{2,1,0:T(8,128)S(1)} %pick.1), channel_id=1, replica_groups=mesh['zh'=4,'zl'=4,'sub'=8,'vis'=4] {'zl','vis'}, dimensions={0} | all-to-all | bytes 262144 | tf_op jit(solution)/shard_map/all_to_all | solution.py:482
  58.4 0.0 copy-done
  58.4 0.0 copy-done.1
  58.4 0.0 copy-done.2
  58.4 0.0 copy-done.12
  58.5 0.0 copy-start.3
  58.5 2.2 %degrid.1 = (f32[16,2,128]{2,1,0:T(2,128)}, f32[4,64,128]{2,1,0:T(8,128)S(1)}) custom-call(f32[16,16,128]{2,1,0:T(8,128)S(1)} %all_to_all.32.got_ref, f32[16,8,128]{2,1,0:T(8,128)S(1)} %copy-done.1, f32[16,128,128]{2,1,0:T(8,128)S(1)} %copy-done, f32[16,2,128]{2,1,0:T(2,128)S(1)} %copy-done.2, f32[16,128]{1,0:T(8,128)S(1)} %copy-done.12), custom_call_target="tpu_custom_call" | custom-call | flops 10000000000 | bytes 1048576 | tf_op jit(solution)/shard_map/degrid/pallas_call | solution.py:438
  60.6 7.2 %all_to_all.33.part_ref = f32[4,64,128]{2,1,0:T(8,128)S(1)} all-to-all(f32[4,64,128]{2,1,0:T(8,128)S(1)} %get-tuple-element.9), channel_id=1, replica_groups=mesh['zh'=4,'zl'=4,'sub'=8,'vis'=4] {'vis'}, dimensions={0} | all-to-all | bytes 262144 | tf_op jit(solution)/shard_map/all_to_all | solution.py:490
  67.8 0.0 copy-done.3
  67.8 0.0 copy-start.8
  67.8 0.0 copy-start.9
  67.8 0.0 copy-start.13
  67.8 1.8 %place.1 = f32[16,56,128]{2,1,0:T(8,128)S(1)} custom-call(f32[4,64,128]{2,1,0:T(8,128)S(1)} %all_to_all.33.part_ref, f32[16,16,128]{2,1,0:T(8,128)S(1)} %all_to_all.30.held_ref, bf16[2,512,896]{2,1,0:T(8,128)(2,1)S(1)} %copy-done.3), custom_call_target="tpu_custom_call" | custom-call | flops 10000000000 | bytes 1048576 | tf_op jit(solution)/shard_map/place/pallas_call | solution.py:438
  69.6 19.5 %all_to_all.34.got_ref = f32[16,56,128]{2,1,0:T(8,128)S(1)} all-to-all(f32[16,56,128]{2,1,0:T(8,128)S(1)} %place.1), channel_id=1, replica_groups=mesh['zh'=4,'zl'=4,'sub'=8,'vis'=4] {'zh','zl'}, dimensions={0} | all-to-all | bytes 917504 | tf_op jit(solution)/shard_map/all_to_all | solution.py:497
  89.1 0.0 copy-done.8
  89.1 0.0 copy-done.9
  89.2 0.0 copy-done.13
  89.2 0.0 copy-start.6
  89.2 0.0 copy-start.7
  89.2 0.0 copy-start.10
  89.2 0.0 copy-start.11
  89.2 0.2 share.1
  89.4 26.1 %all_to_all.35.got_ref = f32[32,32,128]{2,1,0:T(8,128)S(1)} all-to-all(f32[32,32,128]{2,1,0:T(8,128)S(1)} %share.1), channel_id=1, replica_groups=mesh['zh'=4,'zl'=4,'sub'=8,'vis'=4] {'sub','vis'}, dimensions={0} | all-to-all | bytes 1048576 | tf_op jit(solution)/shard_map/all_to_all | solution.py:505
  115.6 0.0 copy-done.6
  115.6 0.0 copy-done.7
  115.6 0.0 copy-done.10
  115.6 0.0 copy-done.11
  115.6 1.8 %image.1 = f32[128,512]{1,0:T(8,128)} custom-call(f32[32,32,128]{2,1,0:T(8,128)S(1)} %all_to_all.35.got_ref, f32[16,128]{1,0:T(8,128)S(1)} %copy-done.10, f32[8,128]{1,0:T(8,128)S(1)} %copy-done.11, bf16[128,256]{1,0:T(8,128)(2,1)S(1)} %copy-done.7, bf16[128,256]{1,0:T(8,128)(2,1)S(1)} %copy-done.6), custom_call_target="tpu_custom_call" | custom-call | flops 10000000000 | bytes 1048576 | tf_op jit(solution)/shard_map/image/pallas_call | solution.py:438
Async XLA Ops:
  1.9 19.3 %copy-start.5 = (bf16[2,320,128]{2,1,0:T(8,128)(2,1)S(1)}, bf16[2,320,128]{2,1,0:T(8,128)(2,1)}, u32[]{:S(2)}) copy-start(bf16[2,320,128]{2,1,0:T(8,128)(2,1)} %constant.31.clone.joins_ref) | copy-start | bytes 491524
  21.2 25.5 %copy-start.4 = (bf16[2,512,640]{2,1,0:T(8,128)(2,1)S(1)}, bf16[2,512,640]{2,1,0:T(8,128)(2,1)}, u32[]{:S(2)}) copy-start(bf16[2,512,640]{2,1,0:T(8,128)(2,1)} %constant.32.clone.grow_ref) | copy-start | bytes 3932164
  46.7 11.8 %copy-start = (f32[16,128,128]{2,1,0:T(8,128)S(1)}, f32[16,128,128]{2,1,0:T(8,128)}, u32[]{:S(2)}) copy-start(f32[16,128,128]{2,1,0:T(8,128)} %cols_ref.1) | copy-start | bytes 3145732
  46.7 11.8 %copy-start.1 = (f32[16,8,128]{2,1,0:T(8,128)S(1)}, f32[16,8,128]{2,1,0:T(8,128)}, u32[]{:S(2)}) copy-start(f32[16,8,128]{2,1,0:T(8,128)} %rows_ref.1) | copy-start | bytes 196612
  46.7 11.8 %copy-start.2 = (f32[16,2,128]{2,1,0:T(2,128)S(1)}, f32[16,2,128]{2,1,0:T(2,128)}, u32[]{:S(2)}) copy-start(f32[16,2,128]{2,1,0:T(2,128)} %seen_ref.1) | copy-start | bytes 49156
  46.7 11.7 %copy-start.12 = (f32[16,128]{1,0:T(8,128)S(1)}, f32[16,128]{1,0:T(8,128)}, u32[]{:S(2)}) copy-start(f32[16,128]{1,0:T(8,128)} %get-tuple-element.8.scale_ref) | copy-start | bytes 24580
  58.5 9.4 %copy-start.3 = (bf16[2,512,896]{2,1,0:T(8,128)(2,1)S(1)}, bf16[2,512,896]{2,1,0:T(8,128)(2,1)}, u32[]{:S(2)}) copy-start(bf16[2,512,896]{2,1,0:T(8,128)(2,1)} %constant.24.clone.spread_ref) | copy-start | bytes 5505028
  67.8 21.3 %copy-start.8 = (bf16[128,56]{1,0:T(8,128)(2,1)S(1)}, bf16[128,56]{1,0:T(8,128)(2,1)}, u32[]{:S(2)}) copy-start(bf16[128,56]{1,0:T(8,128)(2,1)} %constant.23.clone.low_ref) | copy-start | bytes 43012
  67.8 21.3 %copy-start.9 = (bf16[128,56]{1,0:T(8,128)(2,1)S(1)}, bf16[128,56]{1,0:T(8,128)(2,1)}, u32[]{:S(2)}) copy-start(bf16[128,56]{1,0:T(8,128)(2,1)} %constant.22.clone.high_ref) | copy-start | bytes 43012
  67.8 21.3 %copy-start.13 = (f32[8,128]{1,0:T(8,128)S(1)}, f32[8,128]{1,0:T(8,128)}, u32[]{:S(2)}) copy-start(f32[8,128]{1,0:T(8,128)} %get-tuple-element.10.offset_row_ref) | copy-start | bytes 12292
  89.2 26.4 %copy-start.6 = (bf16[128,256]{1,0:T(8,128)(2,1)S(1)}, bf16[128,256]{1,0:T(8,128)(2,1)}, u32[]{:S(2)}) copy-start(bf16[128,256]{1,0:T(8,128)(2,1)} %constant.28.clone.low_ref) | copy-start | bytes 196612
  89.2 26.4 %copy-start.7 = (bf16[128,256]{1,0:T(8,128)(2,1)S(1)}, bf16[128,256]{1,0:T(8,128)(2,1)}, u32[]{:S(2)}) copy-start(bf16[128,256]{1,0:T(8,128)(2,1)} %constant.27.clone.high_ref) | copy-start | bytes 196612
  89.2 26.4 %copy-start.10 = (f32[16,128]{1,0:T(8,128)S(1)}, f32[16,128]{1,0:T(8,128)}, u32[]{:S(2)}) copy-start(f32[16,128]{1,0:T(8,128)} %constant.29.clone.refs_3_.section_ref) | copy-start | bytes 24580
  89.2 26.4 %copy-start.11 = (f32[8,128]{1,0:T(8,128)S(1)}, f32[8,128]{1,0:T(8,128)}, u32[]{:S(2)}) copy-start(f32[8,128]{1,0:T(8,128)} %constant.30.clone.refs_4_.twist_ref) | copy-start | bytes 12292

commit v7 on v6

--- a/solution.py
+++ b/solution.py
@@ -129,7 +129,7 @@
 
 
 def angles(offset, first, total):
-    pixel = first + lax.broadcasted_iota(jnp.int32, (1, BC), 1)
+    pixel = first + lax.broadcasted_iota(jnp.int32, offset.shape, 1)
     turn = ((2 * offset + (CR - 1)) * pixel) % (2 * total)
     angle = turn.astype(jnp.float32) * (jnp.pi / total)
     return jnp.cos(angle), jnp.sin(angle)
@@ -168,21 +168,22 @@
     ]
     for copy in copies:
         copy.start()
-    for copy in copies:
+    offset_ref, count_ref, id_ref, section_ref, twist_ref, sky_ref, high_ref, low_ref, wt_ref = targets
+    for copy in copies[:5]:
         copy.wait()
-    offset_ref, count_ref, id_ref, section_ref, twist_ref, sky_ref, high_ref, low_ref, wt_ref = targets
-    slots = wt_ref.shape[0]
+    offset = jnp.full(offset_row_ref.shape, offset_ref[0], jnp.int32)
+    offset_row_ref[...] = offset.astype(jnp.float32)
+    cos_p, sin_p = angles(offset[:1], first_pixel(sky_ref.shape[0]), total)
+    section = section_ref[...]
+    into = jnp.concatenate([section * cos_p, -section * sin_p], axis=0)
+    lane = lax.broadcasted_iota(jnp.int32, (1, BC), 1)
+    ids = jnp.zeros((1, BC), jnp.int32)
+    for s in range(id_ref.shape[0]):
+        ids = jnp.where((lane // 32 == s // 4) & (lane % 4 == s % 4), id_ref[s], ids)
+    for copy in copies[5:]:
+        copy.wait()
     slot = lax.broadcasted_iota(jnp.int32, wt_ref.shape, 0)
     scale_ref[...] = jnp.where(slot < count_ref[0], wt_ref[...].astype(jnp.float32), 0.0)
-    lane = lax.broadcasted_iota(jnp.int32, (1, BC), 1)
-    ids = jnp.zeros((1, BC), jnp.int32)
-    for s in range(slots):
-        ids = jnp.where((lane // 32 == s // 4) & (lane % 4 == s % 4), id_ref[s], ids)
-    offset = jnp.full(offset_row_ref.shape, offset_ref[0], jnp.int32)
-    offset_row_ref[...] = offset.astype(jnp.float32)
-    cos_p, sin_p = angles(offset_ref[0], first_pixel(sky_ref.shape[0]), total)
-    section = section_ref[...]
-    into = jnp.concatenate([section * cos_p, -section * sin_p], axis=0)
     coef = stacked(into, halves(sky_ref[...]), NN)
     real, imag = [], []
     for k in range(vises):
@@ -377,13 +378,13 @@
 def image_kernel(vises, subs, total, got_ref, section_ref, twist_ref, high_ref, low_ref, out_ref):
     rows = out_ref.shape[0]
     section = section_ref[...]
-    first = first_pixel(rows)
+    offsets = [got_ref[q * vises, SPARE : SPARE + 1, :] for q in range(subs)]
+    offsets = jnp.concatenate(offsets, axis=0).astype(jnp.int32)
+    cos_all, sin_all = angles(offsets, first_pixel(rows), total)
     out = []
     coef = []
     for q in range(subs):
-        offset = got_ref[q * vises, SPARE : SPARE + 1, :].astype(jnp.int32)
-        cos_p, sin_p = angles(offset, first, total)
-        cos_p, sin_p = section * cos_p, section * sin_p
+        cos_p, sin_p = section * cos_all[q : q + 1], section * sin_all[q : q + 1]
         out.append(
             jnp.concatenate(
                 [
@@ -394,9 +395,10 @@
             )
         )
         coef.append(jnp.concatenate([got_ref[q * vises + v] for v in range(vises)], axis=1))
-    out_high, out_low = halves(jnp.concatenate(out, axis=0))
+    out = wide(jnp.concatenate(out, axis=0))
     high, low = halves(jnp.concatenate(coef, axis=0))
-    grid = mxu(out_high, high, TN) + mxu(out_high, low, TN) + mxu(out_low, high, TN)
+    grid = mxu(out, high, TN)
+    grid = grid[: 2 * rows] + grid[2 * rows :] + mxu(out[:, : 2 * rows], low, TN)
     real, imag = [], []
     for v in range(vises):
         both = stacked(grid[:, v * BC : (v + 1) * BC], (high_ref[...], low_ref[...]), NN)

time: 118 us -> 118 us (level)
  no operation moved by 1% of the time
where the time goes in v7:
time: 118 us; the launch traced here: 117 us
  blocking collectives  105 us (89%)
  Pallas kernels  9.69 us (8%)
  between operations  2.05 us (2%)
    all_to_all x1, blocking collectives, shards(): got = lax.all_to_all(sent, ('sub', 'vis'), 0, 0, tiled=True)  26.1 us
    all_to_all x1, blocking collectives, shards(): got = lax.all_to_all(sent, 'zh', 0, 0, tiled=True)  25.2 us
    all_to_all x1, blocking collectives, shards(): got = lax.all_to_all(sent, ('zh', 'zl'), 0, 0, tiled=True)  19.5 us
    all_to_all x1, blocking collectives, shards(): held = lax.all_to_all(sent, ('zl', 'vis'), 0, 0, tiled=True)  17 us
    all_to_all x1, blocking collectives, shards(): got = lax.all_to_all(sent, ('zl', 'vis'), 0, 0, tiled=True)  10.4 us
    pallas_call x6, Pallas kernels, call(): pl.pallas_call(kernel, out_shape=tuple((jax.ShapeDtypeStruct(x, jnp.float...  7.47 us
    all_to_all x1, blocking collectives, shards(): got = lax.all_to_all(sent, 'vis', 0, 0, tiled=True)  7.2 us

profile of v7, /device:TPU:1, one launch (start us, length us, event | category | flops | bytes accessed | tf_op | source)
XLA Modules:
  0.0 117.1 jit_solution(12635472524739578036)
XLA Ops:
  1.9 0.0 copy-start.5
  1.9 2.2 %project.1 = (f32[16,16,128]{2,1,0:T(8,128)}, f32[16,128]{1,0:T(8,128)}, f32[8,128]{1,0:T(8,128)}) custom-call(s32[1]{0:T(128)S(6)} %copy.21.refs_0_, s32[1]{0:T(128)S(6)} %copy.22.refs_1_, s32[16]{0:T(128)} %refs_2_.1, f32[16,128]{1,0:T(8,128)} %constant.29.clone.refs_3_.section_ref, f32[8,128]{1,0:T(8,128)} %constant.30.clone.refs_4_.twist_ref, ...), custom_call_target="tpu_custom_call" | custom-call | flops 10000000000 | bytes 1048576 | tf_op jit(solution)/shard_map/project/pallas_call | solution.py:452
  4.2 17.0 %all_to_all.30.held_ref = f32[16,16,128]{2,1,0:T(8,128)S(1)} all-to-all(f32[16,16,128]{2,1,0:T(8,128)} %get-tuple-element.7), channel_id=1, replica_groups=mesh['zh'=4,'zl'=4,'sub'=8,'vis'=4] {'zl','vis'}, dimensions={0} | all-to-all | bytes 262144 | tf_op jit(solution)/shard_map/all_to_all | solution.py:468
  21.2 0.0 copy-done.5
  21.2 0.0 copy-start.4
  21.2 0.3 join.1
  21.5 25.2 %all_to_all.31.got_ref = f32[4,40,128]{2,1,0:T(8,128)S(1)} all-to-all(f32[4,40,128]{2,1,0:T(8,128)S(1)} %join.1), channel_id=1, replica_groups=mesh['zh'=4,'zl'=4,'sub'=8,'vis'=4] {'zh'}, dimensions={0} | all-to-all | bytes 163840 | tf_op jit(solution)/shard_map/all_to_all | solution.py:475
  46.6 0.0 copy-done.4
  46.6 0.0 copy-start
  46.6 0.0 copy-start.1
  46.6 0.0 copy-start.2
  46.6 0.0 copy-start.12
  46.7 1.4 %pick.1 = f32[16,16,128]{2,1,0:T(8,128)S(1)} custom-call(f32[4,40,128]{2,1,0:T(8,128)S(1)} %all_to_all.31.got_ref, f32[16,16,128]{2,1,0:T(8,128)S(1)} %all_to_all.30.held_ref, bf16[2,512,640]{2,1,0:T(8,128)(2,1)S(1)} %copy-done.4), custom_call_target="tpu_custom_call" | custom-call | flops 10000000000 | bytes 1048576 | tf_op jit(solution)/shard_map/pick/pallas_call | solution.py:440
  48.0 10.4 %all_to_all.32.got_ref = f32[16,16,128]{2,1,0:T(8,128)S(1)} all-to-all(f32[16,16,128]{2,1,0:T(8,128)S(1)} %pick.1), channel_id=1, replica_groups=mesh['zh'=4,'zl'=4,'sub'=8,'vis'=4] {'zl','vis'}, dimensions={0} | all-to-all | bytes 262144 | tf_op jit(solution)/shard_map/all_to_all | solution.py:484
  58.4 0.0 copy-done
  58.4 0.0 copy-done.1
  58.4 0.0 copy-done.2
  58.4 0.0 copy-done.12
  58.4 0.0 copy-start.3
  58.4 2.2 %degrid.1 = (f32[16,2,128]{2,1,0:T(2,128)}, f32[4,64,128]{2,1,0:T(8,128)S(1)}) custom-call(f32[16,16,128]{2,1,0:T(8,128)S(1)} %all_to_all.32.got_ref, f32[16,8,128]{2,1,0:T(8,128)S(1)} %copy-done.1, f32[16,128,128]{2,1,0:T(8,128)S(1)} %copy-done, f32[16,2,128]{2,1,0:T(2,128)S(1)} %copy-done.2, f32[16,128]{1,0:T(8,128)S(1)} %copy-done.12), custom_call_target="tpu_custom_call" | custom-call | flops 10000000000 | bytes 1048576 | tf_op jit(solution)/shard_map/degrid/pallas_call | solution.py:440
  60.6 7.2 %all_to_all.33.part_ref = f32[4,64,128]{2,1,0:T(8,128)S(1)} all-to-all(f32[4,64,128]{2,1,0:T(8,128)S(1)} %get-tuple-element.9), channel_id=1, replica_groups=mesh['zh'=4,'zl'=4,'sub'=8,'vis'=4] {'vis'}, dimensions={0} | all-to-all | bytes 262144 | tf_op jit(solution)/shard_map/all_to_all | solution.py:492
  67.8 0.0 copy-done.3
  67.8 0.0 copy-start.8
  67.8 0.0 copy-start.9
  67.8 0.0 copy-start.13
  67.8 1.8 %place.1 = f32[16,56,128]{2,1,0:T(8,128)S(1)} custom-call(f32[4,64,128]{2,1,0:T(8,128)S(1)} %all_to_all.33.part_ref, f32[16,16,128]{2,1,0:T(8,128)S(1)} %all_to_all.30.held_ref, bf16[2,512,896]{2,1,0:T(8,128)(2,1)S(1)} %copy-done.3), custom_call_target="tpu_custom_call" | custom-call | flops 10000000000 | bytes 1048576 | tf_op jit(solution)/shard_map/place/pallas_call | solution.py:440
  69.6 19.5 %all_to_all.34.got_ref = f32[16,56,128]{2,1,0:T(8,128)S(1)} all-to-all(f32[16,56,128]{2,1,0:T(8,128)S(1)} %place.1), channel_id=1, replica_groups=mesh['zh'=4,'zl'=4,'sub'=8,'vis'=4] {'zh','zl'}, dimensions={0} | all-to-all | bytes 917504 | tf_op jit(solution)/shard_map/all_to_all | solution.py:499
  89.1 0.0 copy-done.8
  89.1 0.0 copy-done.9
  89.1 0.0 copy-done.13
  89.1 0.0 copy-start.6
  89.1 0.0 copy-start.7
  89.1 0.0 copy-start.10
  89.1 0.0 copy-start.11
  89.2 0.2 share.1
  89.4 26.1 %all_to_all.35.got_ref = f32[32,32,128]{2,1,0:T(8,128)S(1)} all-to-all(f32[32,32,128]{2,1,0:T(8,128)S(1)} %share.1), channel_id=1, replica_groups=mesh['zh'=4,'zl'=4,'sub'=8,'vis'=4] {'sub','vis'}, dimensions={0} | all-to-all | bytes 1048576 | tf_op jit(solution)/shard_map/all_to_all | solution.py:507
  115.4 0.0 copy-done.6
  115.4 0.0 copy-done.7
  115.4 0.0 copy-done.10
  115.4 0.0 copy-done.11
  115.5 1.7 %image.1 = f32[128,512]{1,0:T(8,128)} custom-call(f32[32,32,128]{2,1,0:T(8,128)S(1)} %all_to_all.35.got_ref, f32[16,128]{1,0:T(8,128)S(1)} %copy-done.10, f32[8,128]{1,0:T(8,128)S(1)} %copy-done.11, bf16[128,256]{1,0:T(8,128)(2,1)S(1)} %copy-done.7, bf16[128,256]{1,0:T(8,128)(2,1)S(1)} %copy-done.6), custom_call_target="tpu_custom_call" | custom-call | flops 10000000000 | bytes 1048576 | tf_op jit(solution)/shard_map/image/pallas_call | solution.py:440
Async XLA Ops:
  1.9 19.3 %copy-start.5 = (bf16[2,320,128]{2,1,0:T(8,128)(2,1)S(1)}, bf16[2,320,128]{2,1,0:T(8,128)(2,1)}, u32[]{:S(2)}) copy-start(bf16[2,320,128]{2,1,0:T(8,128)(2,1)} %constant.31.clone.joins_ref) | copy-start | bytes 491524
  21.2 25.5 %copy-start.4 = (bf16[2,512,640]{2,1,0:T(8,128)(2,1)S(1)}, bf16[2,512,640]{2,1,0:T(8,128)(2,1)}, u32[]{:S(2)}) copy-start(bf16[2,512,640]{2,1,0:T(8,128)(2,1)} %constant.32.clone.grow_ref) | copy-start | bytes 3932164
  46.6 11.8 %copy-start = (f32[16,128,128]{2,1,0:T(8,128)S(1)}, f32[16,128,128]{2,1,0:T(8,128)}, u32[]{:S(2)}) copy-start(f32[16,128,128]{2,1,0:T(8,128)} %cols_ref.1) | copy-start | bytes 3145732
  46.6 11.8 %copy-start.1 = (f32[16,8,128]{2,1,0:T(8,128)S(1)}, f32[16,8,128]{2,1,0:T(8,128)}, u32[]{:S(2)}) copy-start(f32[16,8,128]{2,1,0:T(8,128)} %rows_ref.1) | copy-start | bytes 196612
  46.6 11.8 %copy-start.2 = (f32[16,2,128]{2,1,0:T(2,128)S(1)}, f32[16,2,128]{2,1,0:T(2,128)}, u32[]{:S(2)}) copy-start(f32[16,2,128]{2,1,0:T(2,128)} %seen_ref.1) | copy-start | bytes 49156
  46.6 11.7 %copy-start.12 = (f32[16,128]{1,0:T(8,128)S(1)}, f32[16,128]{1,0:T(8,128)}, u32[]{:S(2)}) copy-start(f32[16,128]{1,0:T(8,128)} %get-tuple-element.8.scale_ref) | copy-start | bytes 24580
  58.4 9.4 %copy-start.3 = (bf16[2,512,896]{2,1,0:T(8,128)(2,1)S(1)}, bf16[2,512,896]{2,1,0:T(8,128)(2,1)}, u32[]{:S(2)}) copy-start(bf16[2,512,896]{2,1,0:T(8,128)(2,1)} %constant.24.clone.spread_ref) | copy-start | bytes 5505028
  67.8 21.3 %copy-start.8 = (bf16[128,56]{1,0:T(8,128)(2,1)S(1)}, bf16[128,56]{1,0:T(8,128)(2,1)}, u32[]{:S(2)}) copy-start(bf16[128,56]{1,0:T(8,128)(2,1)} %constant.23.clone.low_ref) | copy-start | bytes 43012
  67.8 21.3 %copy-start.9 = (bf16[128,56]{1,0:T(8,128)(2,1)S(1)}, bf16[128,56]{1,0:T(8,128)(2,1)}, u32[]{:S(2)}) copy-start(bf16[128,56]{1,0:T(8,128)(2,1)} %constant.22.clone.high_ref) | copy-start | bytes 43012
  67.8 21.3 %copy-start.13 = (f32[8,128]{1,0:T(8,128)S(1)}, f32[8,128]{1,0:T(8,128)}, u32[]{:S(2)}) copy-start(f32[8,128]{1,0:T(8,128)} %get-tuple-element.10.offset_row_ref) | copy-start | bytes 12292
  89.1 26.3 %copy-start.6 = (bf16[128,256]{1,0:T(8,128)(2,1)S(1)}, bf16[128,256]{1,0:T(8,128)(2,1)}, u32[]{:S(2)}) copy-start(bf16[128,256]{1,0:T(8,128)(2,1)} %constant.28.clone.low_ref) | copy-start | bytes 196612
  89.1 26.3 %copy-start.7 = (bf16[128,256]{1,0:T(8,128)(2,1)S(1)}, bf16[128,256]{1,0:T(8,128)(2,1)}, u32[]{:S(2)}) copy-start(bf16[128,256]{1,0:T(8,128)(2,1)} %constant.27.clone.high_ref) | copy-start | bytes 196612
  89.1 26.3 %copy-start.10 = (f32[16,128]{1,0:T(8,128)S(1)}, f32[16,128]{1,0:T(8,128)}, u32[]{:S(2)}) copy-start(f32[16,128]{1,0:T(8,128)} %constant.29.clone.refs_3_.section_ref) | copy-start | bytes 24580
  89.1 26.3 %copy-start.11 = (f32[8,128]{1,0:T(8,128)S(1)}, f32[8,128]{1,0:T(8,128)}, u32[]{:S(2)}) copy-start(f32[8,128]{1,0:T(8,128)} %constant.30.clone.refs_4_.twist_ref) | copy-start | bytes 12292

commit v8 on v7

--- a/solution.py
+++ b/solution.py
@@ -321,7 +321,7 @@
     parts = part_ref[...].reshape(vises * groups * 2 * BR, BC)
     columns = ids_columns(held_ref, vises, vises * groups)
     piece = lax.broadcasted_iota(jnp.int32, parts.shape, 1) % vises
-    turned = jnp.zeros((2 * BC, 2 * CR), jnp.float32)
+    left, right = [], []
     for member in range(vises):
         hot, band = selection(slot_rows(columns, member, vises, groups), K // BC)
         alone = jnp.where(piece == member, parts, 0.0)
@@ -329,7 +329,9 @@
         for v in range(vises):
             if v != member:
                 rows = rows + pltpu.roll(alone, (v - member) % BC, 1)
-        turned = turned + mxu(wide(jnp.where(piece == band, rows, 0.0)), hot, TN)
+        left.append(wide(jnp.where(piece == band, rows, 0.0)))
+        right.append(hot)
+    turned = mxu(jnp.concatenate(left, axis=0), jnp.concatenate(right, axis=0), TN)
     turned = turned[:BC] + turned[BC:]
     coef = stacked(turned, (spread_ref[0], spread_ref[1]), NN)
     out_ref[...] = coef.T.reshape(out_ref.shape)

time: 118 us -> 118 us (level)
  no operation moved by 1% of the time
where the time goes in v8:
time: 118 us; the launch traced here: 117 us
  blocking collectives  105 us (89%)
  Pallas kernels  9.67 us (8%)
  between operations  2.05 us (2%)
    all_to_all x1, blocking collectives, shards(): got = lax.all_to_all(sent, ('sub', 'vis'), 0, 0, tiled=True)  26.1 us
    all_to_all x1, blocking collectives, shards(): got = lax.all_to_all(sent, 'zh', 0, 0, tiled=True)  25.2 us
    all_to_all x1, blocking collectives, shards(): got = lax.all_to_all(sent, ('zh', 'zl'), 0, 0, tiled=True)  19.5 us
    all_to_all x1, blocking collectives, shards(): held = lax.all_to_all(sent, ('zl', 'vis'), 0, 0, tiled=True)  17 us
    all_to_all x1, blocking collectives, shards(): got = lax.all_to_all(sent, ('zl', 'vis'), 0, 0, tiled=True)  10.4 us
    pallas_call x6, Pallas kernels, call(): pl.pallas_call(kernel, out_shape=tuple((jax.ShapeDtypeStruct(x, jnp.float...  7.46 us
    all_to_all x1, blocking collectives, shards(): got = lax.all_to_all(sent, 'vis', 0, 0, tiled=True)  7.2 us

profile of v8, /device:TPU:1, one launch (start us, length us, event | category | flops | bytes accessed | tf_op | source)
XLA Modules:
  0.0 117.1 jit_solution(16510992051172422735)
XLA Ops:
  1.9 0.0 copy-start.5
  1.9 2.2 %project.1 = (f32[16,16,128]{2,1,0:T(8,128)}, f32[16,128]{1,0:T(8,128)}, f32[8,128]{1,0:T(8,128)}) custom-call(s32[1]{0:T(128)S(6)} %copy.21.refs_0_, s32[1]{0:T(128)S(6)} %copy.22.refs_1_, s32[16]{0:T(128)} %refs_2_.1, f32[16,128]{1,0:T(8,128)} %constant.29.clone.refs_3_.section_ref, f32[8,128]{1,0:T(8,128)} %constant.30.clone.refs_4_.twist_ref, ...), custom_call_target="tpu_custom_call" | custom-call | flops 10000000000 | bytes 1048576 | tf_op jit(solution)/shard_map/project/pallas_call | solution.py:454
  4.2 17.0 %all_to_all.30.held_ref = f32[16,16,128]{2,1,0:T(8,128)S(1)} all-to-all(f32[16,16,128]{2,1,0:T(8,128)} %get-tuple-element.7), channel_id=1, replica_groups=mesh['zh'=4,'zl'=4,'sub'=8,'vis'=4] {'zl','vis'}, dimensions={0} | all-to-all | bytes 262144 | tf_op jit(solution)/shard_map/all_to_all | solution.py:470
  21.2 0.0 copy-done.5
  21.2 0.0 copy-start.4
  21.2 0.3 join.1
  21.5 25.2 %all_to_all.31.got_ref = f32[4,40,128]{2,1,0:T(8,128)S(1)} all-to-all(f32[4,40,128]{2,1,0:T(8,128)S(1)} %join.1), channel_id=1, replica_groups=mesh['zh'=4,'zl'=4,'sub'=8,'vis'=4] {'zh'}, dimensions={0} | all-to-all | bytes 163840 | tf_op jit(solution)/shard_map/all_to_all | solution.py:477
  46.6 0.0 copy-done.4
  46.6 0.0 copy-start
  46.6 0.0 copy-start.1
  46.6 0.0 copy-start.2
  46.6 0.0 copy-start.12
  46.7 1.4 %pick.1 = f32[16,16,128]{2,1,0:T(8,128)S(1)} custom-call(f32[4,40,128]{2,1,0:T(8,128)S(1)} %all_to_all.31.got_ref, f32[16,16,128]{2,1,0:T(8,128)S(1)} %all_to_all.30.held_ref, bf16[2,512,640]{2,1,0:T(8,128)(2,1)S(1)} %copy-done.4), custom_call_target="tpu_custom_call" | custom-call | flops 10000000000 | bytes 1048576 | tf_op jit(solution)/shard_map/pick/pallas_call | solution.py:442
  48.0 10.4 %all_to_all.32.got_ref = f32[16,16,128]{2,1,0:T(8,128)S(1)} all-to-all(f32[16,16,128]{2,1,0:T(8,128)S(1)} %pick.1), channel_id=1, replica_groups=mesh['zh'=4,'zl'=4,'sub'=8,'vis'=4] {'zl','vis'}, dimensions={0} | all-to-all | bytes 262144 | tf_op jit(solution)/shard_map/all_to_all | solution.py:486
  58.4 0.0 copy-done
  58.4 0.0 copy-done.1
  58.4 0.0 copy-done.2
  58.4 0.0 copy-done.12
  58.4 0.0 copy-start.3
  58.4 2.2 %degrid.1 = (f32[16,2,128]{2,1,0:T(2,128)}, f32[4,64,128]{2,1,0:T(8,128)S(1)}) custom-call(f32[16,16,128]{2,1,0:T(8,128)S(1)} %all_to_all.32.got_ref, f32[16,8,128]{2,1,0:T(8,128)S(1)} %copy-done.1, f32[16,128,128]{2,1,0:T(8,128)S(1)} %copy-done, f32[16,2,128]{2,1,0:T(2,128)S(1)} %copy-done.2, f32[16,128]{1,0:T(8,128)S(1)} %copy-done.12), custom_call_target="tpu_custom_call" | custom-call | flops 10000000000 | bytes 1048576 | tf_op jit(solution)/shard_map/degrid/pallas_call | solution.py:442
  60.6 7.2 %all_to_all.33.part_ref = f32[4,64,128]{2,1,0:T(8,128)S(1)} all-to-all(f32[4,64,128]{2,1,0:T(8,128)S(1)} %get-tuple-element.9), channel_id=1, replica_groups=mesh['zh'=4,'zl'=4,'sub'=8,'vis'=4] {'vis'}, dimensions={0} | all-to-all | bytes 262144 | tf_op jit(solution)/shard_map/all_to_all | solution.py:494
  67.8 0.0 copy-done.3
  67.8 0.0 copy-start.8
  67.8 0.0 copy-start.9
  67.8 0.0 copy-start.13
  67.8 1.8 %place.1 = f32[16,56,128]{2,1,0:T(8,128)S(1)} custom-call(f32[4,64,128]{2,1,0:T(8,128)S(1)} %all_to_all.33.part_ref, f32[16,16,128]{2,1,0:T(8,128)S(1)} %all_to_all.30.held_ref, bf16[2,512,896]{2,1,0:T(8,128)(2,1)S(1)} %copy-done.3), custom_call_target="tpu_custom_call" | custom-call | flops 10000000000 | bytes 1048576 | tf_op jit(solution)/shard_map/place/pallas_call | solution.py:442
  69.6 19.5 %all_to_all.34.got_ref = f32[16,56,128]{2,1,0:T(8,128)S(1)} all-to-all(f32[16,56,128]{2,1,0:T(8,128)S(1)} %place.1), channel_id=1, replica_groups=mesh['zh'=4,'zl'=4,'sub'=8,'vis'=4] {'zh','zl'}, dimensions={0} | all-to-all | bytes 917504 | tf_op jit(solution)/shard_map/all_to_all | solution.py:501
  89.1 0.0 copy-done.8
  89.1 0.0 copy-done.9
  89.1 0.0 copy-done.13
  89.1 0.0 copy-start.6
  89.1 0.0 copy-start.7
  89.1 0.0 copy-start.10
  89.1 0.0 copy-start.11
  89.1 0.2 share.1
  89.3 26.1 %all_to_all.35.got_ref = f32[32,32,128]{2,1,0:T(8,128)S(1)} all-to-all(f32[32,32,128]{2,1,0:T(8,128)S(1)} %share.1), channel_id=1, replica_groups=mesh['zh'=4,'zl'=4,'sub'=8,'vis'=4] {'sub','vis'}, dimensions={0} | all-to-all | bytes 1048576 | tf_op jit(solution)/shard_map/all_to_all | solution.py:509
  115.4 0.0 copy-done.6
  115.4 0.0 copy-done.7
  115.4 0.0 copy-done.10
  115.4 0.0 copy-done.11
  115.5 1.7 %image.1 = f32[128,512]{1,0:T(8,128)} custom-call(f32[32,32,128]{2,1,0:T(8,128)S(1)} %all_to_all.35.got_ref, f32[16,128]{1,0:T(8,128)S(1)} %copy-done.10, f32[8,128]{1,0:T(8,128)S(1)} %copy-done.11, bf16[128,256]{1,0:T(8,128)(2,1)S(1)} %copy-done.7, bf16[128,256]{1,0:T(8,128)(2,1)S(1)} %copy-done.6), custom_call_target="tpu_custom_call" | custom-call | flops 10000000000 | bytes 1048576 | tf_op jit(solution)/shard_map/image/pallas_call | solution.py:442
Async XLA Ops:
  1.9 19.3 %copy-start.5 = (bf16[2,320,128]{2,1,0:T(8,128)(2,1)S(1)}, bf16[2,320,128]{2,1,0:T(8,128)(2,1)}, u32[]{:S(2)}) copy-start(bf16[2,320,128]{2,1,0:T(8,128)(2,1)} %constant.31.clone.joins_ref) | copy-start | bytes 491524
  21.2 25.5 %copy-start.4 = (bf16[2,512,640]{2,1,0:T(8,128)(2,1)S(1)}, bf16[2,512,640]{2,1,0:T(8,128)(2,1)}, u32[]{:S(2)}) copy-start(bf16[2,512,640]{2,1,0:T(8,128)(2,1)} %constant.32.clone.grow_ref) | copy-start | bytes 3932164
  46.6 11.8 %copy-start = (f32[16,128,128]{2,1,0:T(8,128)S(1)}, f32[16,128,128]{2,1,0:T(8,128)}, u32[]{:S(2)}) copy-start(f32[16,128,128]{2,1,0:T(8,128)} %cols_ref.1) | copy-start | bytes 3145732
  46.6 11.8 %copy-start.1 = (f32[16,8,128]{2,1,0:T(8,128)S(1)}, f32[16,8,128]{2,1,0:T(8,128)}, u32[]{:S(2)}) copy-start(f32[16,8,128]{2,1,0:T(8,128)} %rows_ref.1) | copy-start | bytes 196612
  46.6 11.8 %copy-start.2 = (f32[16,2,128]{2,1,0:T(2,128)S(1)}, f32[16,2,128]{2,1,0:T(2,128)}, u32[]{:S(2)}) copy-start(f32[16,2,128]{2,1,0:T(2,128)} %seen_ref.1) | copy-start | bytes 49156
  46.6 11.7 %copy-start.12 = (f32[16,128]{1,0:T(8,128)S(1)}, f32[16,128]{1,0:T(8,128)}, u32[]{:S(2)}) copy-start(f32[16,128]{1,0:T(8,128)} %get-tuple-element.8.scale_ref) | copy-start | bytes 24580
  58.4 9.4 %copy-start.3 = (bf16[2,512,896]{2,1,0:T(8,128)(2,1)S(1)}, bf16[2,512,896]{2,1,0:T(8,128)(2,1)}, u32[]{:S(2)}) copy-start(bf16[2,512,896]{2,1,0:T(8,128)(2,1)} %constant.24.clone.spread_ref) | copy-start | bytes 5505028
  67.8 21.3 %copy-start.8 = (bf16[128,56]{1,0:T(8,128)(2,1)S(1)}, bf16[128,56]{1,0:T(8,128)(2,1)}, u32[]{:S(2)}) copy-start(bf16[128,56]{1,0:T(8,128)(2,1)} %constant.23.clone.low_ref) | copy-start | bytes 43012
  67.8 21.3 %copy-start.9 = (bf16[128,56]{1,0:T(8,128)(2,1)S(1)}, bf16[128,56]{1,0:T(8,128)(2,1)}, u32[]{:S(2)}) copy-start(bf16[128,56]{1,0:T(8,128)(2,1)} %constant.22.clone.high_ref) | copy-start | bytes 43012
  67.8 21.3 %copy-start.13 = (f32[8,128]{1,0:T(8,128)S(1)}, f32[8,128]{1,0:T(8,128)}, u32[]{:S(2)}) copy-start(f32[8,128]{1,0:T(8,128)} %get-tuple-element.10.offset_row_ref) | copy-start | bytes 12292
  89.1 26.3 %copy-start.6 = (bf16[128,256]{1,0:T(8,128)(2,1)S(1)}, bf16[128,256]{1,0:T(8,128)(2,1)}, u32[]{:S(2)}) copy-start(bf16[128,256]{1,0:T(8,128)(2,1)} %constant.28.clone.low_ref) | copy-start | bytes 196612
  89.1 26.3 %copy-start.7 = (bf16[128,256]{1,0:T(8,128)(2,1)S(1)}, bf16[128,256]{1,0:T(8,128)(2,1)}, u32[]{:S(2)}) copy-start(bf16[128,256]{1,0:T(8,128)(2,1)} %constant.27.clone.high_ref) | copy-start | bytes 196612
  89.1 26.3 %copy-start.10 = (f32[16,128]{1,0:T(8,128)S(1)}, f32[16,128]{1,0:T(8,128)}, u32[]{:S(2)}) copy-start(f32[16,128]{1,0:T(8,128)} %constant.29.clone.refs_3_.section_ref) | copy-start | bytes 24580
  89.1 26.3 %copy-start.11 = (f32[8,128]{1,0:T(8,128)S(1)}, f32[8,128]{1,0:T(8,128)}, u32[]{:S(2)}) copy-start(f32[8,128]{1,0:T(8,128)} %constant.30.clone.refs_4_.twist_ref) | copy-start | bytes 12292
